TPU v7x, 512 devices: a whole 4x4x16 slice. The times are simulated.
512 devices in a mesh: seq: 16 (over z), head: 4 (over y), req: 8 (over x, core).
Axes of the slice: x: 4, y: 4, z: 16, core: 2. Of those that a mesh axis runs over, the one named last changes fastest.
Arguments:
- pre_qkv: bfloat16 [32768, 3, 4096], P('seq', None, ('head', 'req')), may hold values from -200 to 200
- cache_kv: bfloat16 [32, 2, 1024, 4096], P('req', None, 'seq', 'head'), may hold values from -6 to 6
- dec_new: bfloat16 [128, 3, 2, 4096], P('req', None, None, 'head'), may hold values from -200 to 200
- out_weight: bfloat16 [4096, 4096], P('head', 'seq'), may hold values from -0.09375 to 0.09375
- owner_slot: int32 [32], replicated, may hold values from 0 to 127, as said below
- prompt_lengths: int32 [32], replicated, may hold values from 1 to 1024
Outputs:
- prefill_out: bfloat16 [32768, 4096], P('seq', ('head', 'req'))
- decode_out: bfloat16 [128, 2, 4096], P('req', None, ('seq', 'head'))
Inputs may be any that keep to these rules, and one draw needn't show every extreme that they name: `owner_slot`: distinct slots; slot s belongs to decode group s // 16. Of the requests of one aligned block of 4, at most 2 are owned by one group, and the last group, 7, owns exactly 2 from every block.
All inputs are finite; a program needn't handle non-finite values.
Results may differ from a plain program's by a relative error of at most 0.012.
Values may be sent and summed in bfloat16 or wider, within the bound.
No kernel may reach another device: no remote copies, remote signals or barrier semaphores. Data moves between devices by JAX's collectives and lax.ppermute only.
A program may use at most 64 MiB of HBM per device.

v0:
```python
from functools import reduce

import jax
import jax.numpy as jnp
from jax import lax
from jax.sharding import PartitionSpec as P

HEAD_DIM = 128


NEG_FILL = -1e30


def in_one_piece(arrays, axis, dim, along):
    both = jnp.concatenate(arrays, axis=along)
    whole, at, finished = (lax.all_gather(both, axis, axis=dim, tiled=True), 0, [])
    for a in arrays:
        finished.append(lax.slice_in_dim(whole, at, at + a.shape[along], axis=along))
        at += a.shape[along]
    return tuple(finished)


def merged_2(value, axis, join):
    pieces = jax.tree.map(lambda part: lax.all_gather(part, axis), value)
    head = jax.tree.map(lambda part: part[0], pieces)
    tail = jax.tree.map(lambda part: part[1:], pieces)
    total, _ = lax.scan(lambda total, section: (join(total, section), None), head, tail)
    return total


def in_blocks(x, dim, count):
    before, after = (x.shape[:dim], x.shape[dim + 1 :])
    return jnp.moveaxis(x.reshape(*before, count, -1, *after), dim, 0)


def sum_at_owner(x, axis, dim):
    count = lax.axis_size(axis)
    blocks = lax.all_to_all(in_blocks(x, dim, count), axis, 0, 0, tiled=True)
    return jnp.sum(blocks.astype(jnp.float32), axis=0)


def partial_block(query_rows, key_rows, value_rows, allowed):
    score_scale = query_rows.shape[-1] ** (-0.5)
    scores = (
        jnp.einsum("qhd,khd->hqk", query_rows, key_rows, preferred_element_type=jnp.float32)
        * score_scale
    )
    scores = jnp.where(allowed, scores, NEG_FILL)
    peak_score = jnp.max(scores, axis=-1)
    weights = jnp.where(allowed, jnp.exp(scores - peak_score[..., None]), 0.0)
    weight_sum = jnp.sum(weights, axis=-1)
    value_sum = jnp.einsum(
        "hqk,khd->hqd", weights.astype(jnp.bfloat16), value_rows, preferred_element_type=jnp.float32
    )
    return (peak_score, weight_sum, value_sum)


def pick_rows(field, stride, residue):
    row_count, head_count, width = field.shape
    shaped = field.reshape(row_count // stride, stride, head_count, width)
    member = (jnp.arange(stride)[:, None] == residue[None, :])[None, :, :, None]
    return jnp.sum(jnp.where(member, shaped, jnp.zeros((), field.dtype)), axis=1)


def spread_rows(level_term, stride, residue):
    peak_score, weight_sum, value_sum = level_term
    head_count, sparse_count = peak_score.shape
    member = jnp.arange(stride)[:, None] == residue[None, :]
    peak_rows = jnp.where(member[None], peak_score.T[:, None, :], NEG_FILL).reshape(
        sparse_count * stride, head_count
    )
    sum_rows = jnp.where(member[None], weight_sum.T[:, None, :], 0.0).reshape(
        sparse_count * stride, head_count
    )
    value_rows = jnp.where(member[None, :, :, None], jnp.swapaxes(value_sum, 0, 1)[:, None], 0.0)
    return (peak_rows, sum_rows, value_rows.reshape(sparse_count * stride, head_count, -1))


def combine_levels(levels):
    top_all = reduce(jnp.maximum, [level_term[0] for level_term in levels])
    numerator = 0.0
    denominator = 0.0
    for peak_score, weight_sum, value_sum in levels:
        factor = jnp.exp(peak_score - top_all)
        denominator = denominator + weight_sum * factor
        numerator = numerator + value_sum * factor[..., None]
    return numerator / denominator[..., None]


def merge_pair(earlier_part, later_part):
    top_both = jnp.maximum(earlier_part[0], later_part[0])
    factor_one = jnp.exp(earlier_part[0] - top_both)
    factor_two = jnp.exp(later_part[0] - top_both)
    weight_sum = earlier_part[1] * factor_one + later_part[1] * factor_two
    value_sum = earlier_part[2] * factor_one[..., None] + later_part[2] * factor_two[..., None]
    return (top_both, weight_sum, value_sum)


def causal_mask(query_count, key_count, offset):
    return jnp.arange(key_count)[None, :] <= (offset + jnp.arange(query_count))[:, None]


def prefill_block(pre_qkv):
    seq_index = lax.axis_index("seq")
    seq_count = lax.axis_size("seq")
    head_index = lax.axis_index(("head", "req"))
    row_count = pre_qkv.shape[0]
    width = pre_qkv.shape[2]
    head_count = width // HEAD_DIM
    head_ids = head_index * head_count + jnp.arange(head_count)
    query_rows = pre_qkv[:, 0].reshape(row_count, head_count, HEAD_DIM)
    key_rows = pre_qkv[:, 1].reshape(row_count, head_count, HEAD_DIM)
    value_rows = pre_qkv[:, 2].reshape(row_count, head_count, HEAD_DIM)
    zero_residue = jnp.zeros((head_count,), jnp.int32)
    residue_four = head_ids % 4
    residue_far = head_ids % seq_count
    block_rows = min(512, row_count)
    block_count = row_count // block_rows

    def near_part(packed):
        query_block, start_row = packed
        return partial_block(
            query_block, key_rows, value_rows, causal_mask(block_rows, row_count, start_row)
        )

    block_starts = jnp.arange(block_count, dtype=jnp.int32) * block_rows
    near_peak, near_sum, near_value = lax.map(
        near_part, (query_rows.reshape(block_count, block_rows, head_count, HEAD_DIM), block_starts)
    )
    near_term = (
        jnp.moveaxis(near_peak, 0, 1).reshape(head_count, row_count),
        jnp.moveaxis(near_sum, 0, 1).reshape(head_count, row_count),
        jnp.moveaxis(near_value, 0, 1).reshape(head_count, row_count, HEAD_DIM),
    )
    levels = [spread_rows(near_term, 1, zero_residue)]
    keys_four = pick_rows(key_rows, 4, residue_four)
    values_four = pick_rows(value_rows, 4, residue_four)
    every_keys, every_values = in_one_piece((keys_four, values_four), "seq", 0, 1)
    start_row = seq_index // 4 * row_count
    group_keys = lax.dynamic_slice_in_dim(every_keys, start_row, row_count, 0)
    group_values = lax.dynamic_slice_in_dim(every_values, start_row, row_count, 0)
    inner_residue = residue_far // 4
    far_keys = pick_rows(every_keys, seq_count // 4, inner_residue)
    far_values = pick_rows(every_values, seq_count // 4, inner_residue)
    quarter = row_count // 4
    query_four = pick_rows(query_rows, 4, residue_four)
    mid_term = partial_block(
        query_four,
        group_keys,
        group_values,
        causal_mask(quarter, row_count, seq_index % 4 * quarter),
    )
    levels.append(spread_rows(mid_term, 4, residue_four))
    far_count = row_count // seq_count
    query_far = pick_rows(query_rows, seq_count, residue_far)
    far_term = partial_block(
        query_far, far_keys, far_values, causal_mask(far_count, row_count, seq_index * far_count)
    )
    levels.append(spread_rows(far_term, seq_count, residue_far))
    attended = combine_levels(levels)
    return attended.reshape(row_count, width).astype(jnp.bfloat16)


def decode_core(fresh_rows, cache_rows, item_ids, prompt_lengths, out_weight):
    seq_index = lax.axis_index("seq")
    groups, item_count = item_ids.shape
    width = fresh_rows.shape[-1]
    head_count = width // HEAD_DIM
    rows_here = cache_rows.shape[3]
    query_rows = fresh_rows[:, :, 0].reshape(groups, item_count, 2, head_count, HEAD_DIM)
    new_keys = fresh_rows[:, :, 1].reshape(groups, item_count, 2, head_count, HEAD_DIM)
    new_values = fresh_rows[:, :, 2].reshape(groups, item_count, 2, head_count, HEAD_DIM)
    cache_keys = cache_rows[:, :, 0].reshape(groups, item_count, rows_here, head_count, HEAD_DIM)
    cache_values = cache_rows[:, :, 1].reshape(groups, item_count, rows_here, head_count, HEAD_DIM)
    lengths = prompt_lengths[jnp.maximum(item_ids, 0)]
    position = seq_index * rows_here + jnp.arange(rows_here)
    allowed = (position[None, None, :] < lengths[:, :, None])[:, :, None, None, :]
    score_scale = HEAD_DIM ** (-0.5)
    scores = (
        jnp.einsum("githa,gikha->githk", query_rows, cache_keys, preferred_element_type=jnp.float32)
        * score_scale
    )
    scores = jnp.where(allowed, scores, NEG_FILL)
    peak_score = jnp.max(scores, axis=-1)
    weights = jnp.where(allowed, jnp.exp(scores - peak_score[..., None]), 0.0)
    weight_sum = jnp.sum(weights, axis=-1)
    value_sum = jnp.einsum(
        "githk,gikha->githa",
        weights.astype(jnp.bfloat16),
        cache_values,
        preferred_element_type=jnp.float32,
    )
    merged = merged_2((peak_score, weight_sum, value_sum), "seq", merge_pair)
    causal = (jnp.arange(2)[None, :] <= jnp.arange(2)[:, None])[:, None, :]
    fresh_scores = (
        jnp.einsum("githa,gisha->giths", query_rows, new_keys, preferred_element_type=jnp.float32)
        * score_scale
    )
    fresh_scores = jnp.where(causal, fresh_scores, NEG_FILL)
    fresh_peak = jnp.max(fresh_scores, axis=-1)
    fresh_weights = jnp.where(causal, jnp.exp(fresh_scores - fresh_peak[..., None]), 0.0)
    fresh_sum = jnp.sum(fresh_weights, axis=-1)
    fresh_values = jnp.einsum(
        "giths,gisha->githa",
        fresh_weights.astype(jnp.bfloat16),
        new_values,
        preferred_element_type=jnp.float32,
    )
    attended = combine_levels([merged, (fresh_peak, fresh_sum, fresh_values)])
    mixed_rows = attended.reshape(groups, item_count, 2, width).astype(jnp.bfloat16)
    projected = jnp.einsum(
        "gitw,wc->gitc", mixed_rows, out_weight, preferred_element_type=jnp.float32
    )
    return sum_at_owner(projected.astype(jnp.bfloat16), "head", 3)


def route_table(owner_slot, req_count, req_dev, slot_dev, capacity):
    target = (owner_slot // slot_dev).reshape(req_count, req_dev)
    earlier = jnp.arange(req_dev)[None, :] < jnp.arange(req_dev)[:, None]
    same_target = target[:, :, None] == target[:, None, :]
    rank_within = jnp.sum(same_target & earlier[None], axis=2)
    match_table = (target[:, :, None, None] == jnp.arange(req_count)[None, None, :, None]) & (
        rank_within[:, :, None, None] == jnp.arange(capacity)[None, None, None, :]
    )
    request_ids = jnp.arange(req_count * req_dev).reshape(req_count, req_dev)
    return jnp.sum(jnp.where(match_table, request_ids[:, :, None, None] + 1, 0), axis=1) - 1


def on_device(pre_qkv, cache_kv, dec_new, out_weight, owner_slot, prompt_lengths):
    prefill_out = prefill_block(pre_qkv)
    req_index = lax.axis_index("req")
    req_count = lax.axis_size("req")
    req_dev = cache_kv.shape[0]
    slot_dev = dec_new.shape[0]
    capacity = slot_dev // req_count
    routing = route_table(owner_slot, req_count, req_dev, slot_dev, capacity)
    outgoing = routing[req_index]
    landed = routing[:, req_index]
    local_rows = jnp.clip(outgoing - req_index * req_dev, 0, req_dev - 1)
    slot_rows = jnp.clip(owner_slot[jnp.maximum(landed, 0)] - req_index * slot_dev, 0, slot_dev - 1)
    arrived = lax.all_to_all(dec_new[slot_rows], "req", split_axis=0, concat_axis=0, tiled=True)
    answers = decode_core(
        arrived, cache_kv[local_rows], outgoing, prompt_lengths, out_weight
    ).astype(jnp.bfloat16)
    results = lax.all_to_all(answers, "req", split_axis=0, concat_axis=0, tiled=True)
    slot_target = jnp.where(
        landed >= 0, owner_slot[jnp.maximum(landed, 0)] - req_index * slot_dev, slot_dev
    )
    columns = results.shape[-1]
    decode_out = (
        jnp.zeros((slot_dev, 2, columns), jnp.bfloat16)
        .at[slot_target.reshape(-1)]
        .set(results.reshape(-1, 2, columns), mode="drop")
    )
    return (prefill_out, decode_out)


def solution(mesh):
    return jax.shard_map(
        on_device,
        mesh=mesh,
        in_specs=(
            P("seq", None, ("head", "req")),
            P("req", None, "seq", "head"),
            P("req", None, None, "head"),
            P("head", "seq"),
            P(),
            P(),
        ),
        out_specs=(P("seq", ("head", "req")), P("req", None, ("seq", "head"))),
        check_vma=False,
    )
```

profile of v0, /device:TPU:6, one launch (start us, length us, event | category | flops | bytes accessed | tf_op | source)
XLA Modules:
  0.0 218.2 jit_solution(3885818324266351442)
XLA Ops:
  10.8 1.6 gather_fusion.3
  12.4 9.1 %all-to-all-start = ((bf16[8,2,3,2,1024]{4,3,2,1,0:T(2,128)(2,1)}), bf16[8,2,3,2,1024]{4,3,2,1,0:T(2,128)(2,1)S(1)}, u32[]{:S(2)}, u32[]{:S(2)}) async-start(bf16[8,2,3,2,1024]{4,3,2,1,0:T(2,128)(2,1)} %bitcast.35), calls=%async_computation | async-start | bytes 393216 | tf_op jit(solution)/shard_map/all_to_all | solution.py:241
  22.6 2.7 %gather_fusion.2 = bf16[16,2,64,1024]{3,2,1,0:T(8,128)(2,1)} fusion(bf16[4,2,64,1024]{3,2,1,0:T(8,128)(2,1)S(1)} %copy-done, s32[1024]{0:T(1024)S(1)} %pad_clamp_fusion.1), kind=kCustom, calls=%fused_computation.2 | custom fusion | bytes 8388672 | tf_op jit(solution)/shard_map/gather | solution.py:243
  25.3 2.7 %fusion.90 = (bf16[8,2,1,64,1024]{4,3,2,1,0:T(8,128)(2,1)S(1)}, bf16[8,2,1,64,1024]{4,3,2,1,0:T(8,128)(2,1)S(1)}) fusion(bf16[8,2,2,64,1024]{4,3,2,1,0:T(8,128)(2,1)} %bitcast.198), kind=kLoop, calls=%fused_computation.152 | loop fusion | bytes 8388608 | tf_op jit(solution)/shard_map/slice | solution.py:174
  28.7 2.0 copy.232
  30.7 2.9 %fusion.94 = (f32[8,2,2,8]{2,3,1,0:T(8,128)S(1)}, f32[8,2,2,8,64]{4,2,3,1,0:T(2,128)S(1)}) fusion(bf16[8,2,3,2,1024]{4,3,2,1,0:T(2,128)(2,1)S(1)} %all-to-all-done, bf16[8,2,64,8,128]{4,3,2,1,0:T(8,128)(2,1)} %bitcast.209, pred[8,2,64]{2,1,0:T(4,128)(4,1)S(1)} %broadcast_compare_fusion), kind=kOutput, calls=%fused_computation.156 | convolution fusion | flops 4243200 | bytes 2233344 | tf_op jit(solution)/shard_map/githa,gikha->githk/dot_general | solution.py:180
  35.2 1.5 fusion.92
  36.7 2.9 %select_reduce_fusion.4 = (bf16[512,128]{1,0:T(8,128)(2,1)S(1)}, bf16[512,128]{1,0:T(8,128)(2,1)S(1)}, bf16[512,128]{1,0:T(8,128)(2,1)}) fusion(bf16[512,4,1,128]{3,1,0,2:T(4,128)(2,1)S(1)} %bitcast.211, pred[4]{0:T(512)(128)(4,1)S(1)} %iota_compare_fusion.9, bf16[512,4,1,128]{3,1,0,2:T(4,128)(2,1)S(1)} %bitcast.210, bf16[512,4,1,128]{3,1,0,2:T(4,128)(2,1)S(1)} %bitcast.203), kind=kLoop, calls=%fused_computation.77 | loop fusion | flops 1376256 | bytes 1966084 | tf_op jit(solution)/shard_map/reduce_sum | solution.py:62
  40.6 22.7 %while.28 = (s32[]{:T(128)}, f32[4,1,512]{2,1,0:T(1,128)S(1)}, f32[4,1,512]{2,1,0:T(1,128)S(1)}, f32[4,1,512,128]{3,2,1,0:T(8,128)}, s32[4]{0:T(128)S(1)}, /*ind...) while((s32[]{:T(128)}, f32[4,1,512]{2,1,0:T(1,128)S(1)}, ...), condition=%wide.region_3.4_spmd, body=%wide.region_0.3_spmd.sunk | while | flops 553647616 | bytes 14049409 | solution.py:127
  44.4 2.0 fusion.112
  50.0 2.0 fusion.112
  55.7 2.0 fusion.112
  61.3 2.0 fusion.112
  64.5 33.6 %all-gather.1 = f32[128,2,2,8]{3,2,1,0:T(2,128)S(1)} all-gather(f32[8,2,2,8]{3,2,1,0:T(2,128)S(1)} %copy.197), channel_id=3, replica_groups=mesh['seq'=16,'head'=4,'req'=8] {'seq'}, dimensions={0}, use_global_device_ids=true | all-gather | bytes 17408 | tf_op jit(solution)/shard_map/all_gather | solution.py:24
  98.1 27.8 %all-gather = f32[128,2,2,8]{3,2,1,0:T(2,128)S(1)} all-gather(f32[8,2,2,8]{3,2,1,0:T(2,128)S(1)} %copy.196), channel_id=2, replica_groups=mesh['seq'=16,'head'=4,'req'=8] {'seq'}, dimensions={0}, use_global_device_ids=true | all-gather | bytes 17408 | tf_op jit(solution)/shard_map/all_gather | solution.py:24
  130.2 14.2 %while.29 = (s32[]{:T(128)}, f32[8,2,2,8]{3,2,1,0:T(2,128)S(1)}, f32[8,2,2,8]{3,2,1,0:T(2,128)S(1)}, f32[8,2,2,8,128]{4,3,2,1,0:T(8,128)S(1)}, f32[15,8,2,2,8]{4...) while((s32[]{:T(128)}, f32[8,2,2,8]{3,2,1,0:T(2,128)S(1)}, ...), condition=%wide.region_19.20_spmd, body=%wide.region_18.19_spmd.sunk | while | flops 99842 | bytes 403557 | solution.py:27
  147.6 4.3 %all-to-all-start.1 = ((bf16[4,2,1024]{2,1,0:T(2,128)(2,1)}), bf16[4,2,1024]{2,1,0:T(2,128)(2,1)S(1)}, u32[]{:S(2)}, u32[]{:S(2)}) async-start(bf16[4,2,1024]{2,1,0:T(2,128)(2,1)} %reshape.849), calls=%async_computation.1 | async-start | bytes 32768 | tf_op jit(solution)/shard_map/all_to_all | solution.py:38
  151.9 5.4 %all-to-all-done.1 = bf16[4,2,1024]{2,1,0:T(2,128)(2,1)S(1)} async-done(((bf16[4,2,1024]{2,1,0:T(2,128)(2,1)}), bf16[4,2,1024]{2,1,0:T(2,128)(2,1)S(1)}, u32[]{:S(2)}, u32[]{:S(2)}) %all-to-all-start.1) | async-done | bytes 16416 | tf_op jit(solution)/shard_map/all_to_all | solution.py:38
  158.1 5.0 %all-to-all-start.2 = ((bf16[8,2,128]{2,1,0:T(2,128)(2,1)}), bf16[8,2,128]{2,1,0:T(2,128)(2,1)S(1)}, u32[]{:S(2)}, u32[]{:S(2)}) async-start(bf16[8,2,128]{2,1,0:T(2,128)(2,1)} %reshape.851), calls=%async_computation.2 | async-start | bytes 8192 | tf_op jit(solution)/shard_map/all_to_all | solution.py:245
  163.7 2.5 %all-to-all-done.2 = bf16[8,2,128]{2,1,0:T(2,128)(2,1)S(1)} async-done(((bf16[8,2,128]{2,1,0:T(2,128)(2,1)}), bf16[8,2,128]{2,1,0:T(2,128)(2,1)S(1)}, u32[]{:S(2)}, u32[]{:S(2)}) %all-to-all-start.2) | async-done | bytes 4128 | tf_op jit(solution)/shard_map/all_to_all | solution.py:245
  167.4 18.6 %all-gather.6.cloned.1.call-done = bf16[8192,2,128]{2,0,1:T(8,128)(2,1)} async-done(((bf16[512,2,128]{2,0,1:T(8,128)(2,1)}), bf16[8192,2,128]{2,0,1:T(8,128)(2,1)}) %all-gather.6.cloned.1.call-update) | async-done | bytes 4194320 | tf_op jit(solution)/shard_map/all_gather | solution.py:16
  185.9 2.5 %fusion.91 = (bf16[8192,1,128]{2,0,1:T(8,128)(2,1)S(1)}, bf16[8192,1,128]{2,0,1:T(8,128)(2,1)S(1)}) fusion(bf16[8192,2,128]{2,0,1:T(8,128)(2,1)} %all-gather.6.cloned.1.call-done), kind=kLoop, calls=%fused_computation.153 | loop fusion | bytes 8388608 | tf_op jit(solution)/shard_map/slice | solution.py:18
  192.1 14.0 %select_reduce_fusion = (bf16[2048,128]{1,0:T(8,128)(2,1)S(1)}, bf16[2048,128]{1,0:T(8,128)(2,1)S(1)}) fusion(bf16[2048,4,1,128]{3,1,0,2:T(4,128)(2,1)S(1)} %bitcast.199, pred[4]{0:T(512)(128)(4,1)S(1)} %iota_compare_fusion.7, bf16[2048,4,1,128]{3,1,0,2:T(4,128)(2,1)S(1)} %bitcast.200), kind=kLoop, calls=%fused_computation.46 | loop fusion | flops 3670016 | bytes 5242884 | tf_op jit(solution)/shard_map/reduce_sum | solution.py:62
  208.4 3.0 %fusion.49 = bf16[2048,128]{1,0:T(8,128)(2,1)} fusion(f32[2048,128]{1,0:T(8,128)S(1)} %bitcast.206, f32[4,1,512,128]{3,2,1,0:T(8,128)S(1)} %copy-done.2, f32[2048]{0:T(1024)S(1)} %get-tuple-element.203, f32[2048]{0:T(1024)S(1)} %get-tuple-element.206, f32[128,128]{1,0:T(8,128)S(1)} %fusion.52, f32[2048]{0:T(1024)S(1)} %get-tuple-element.205, ...), kind=kLoop, calls=%fused_computation.62 | loop fusion | flops 2359296 | bytes 2723840 | tf_op jit(solution)/shard_map/convert_element_type | solution.py:161
  (186 shorter events, 53.5 us)
Async XLA Ops:
  7.2 15.4 %copy-start = (bf16[4,2,64,1024]{3,2,1,0:T(8,128)(2,1)S(1)}, bf16[4,2,64,1024]{3,2,1,0:T(8,128)(2,1)}, u32[]{:S(2)}) copy-start(bf16[4,2,64,1024]{3,2,1,0:T(8,128)(2,1)} %param.11) | copy-start | bytes 3145732
  7.2 3.6 %copy-start.3 = (bf16[16,3,2,1024]{3,2,1,0:T(2,128)(2,1)S(1)}, bf16[16,3,2,1024]{3,2,1,0:T(2,128)(2,1)}, u32[]{:S(2)}) copy-start(bf16[16,3,2,1024]{3,2,1,0:T(2,128)(2,1)} %param.12) | copy-start | bytes 589828
  7.2 14.4 %copy-start.1 = (s32[32]{0:T(128)S(1)}, s32[32]{0:T(128)}, u32[]{:S(2)}) copy-start(s32[32]{0:T(128)} %param.15) | copy-start | bytes 388
  12.4 18.3 %all-to-all-start = ((bf16[8,2,3,2,1024]{4,3,2,1,0:T(2,128)(2,1)}), bf16[8,2,3,2,1024]{4,3,2,1,0:T(2,128)(2,1)S(1)}, u32[]{:S(2)}, u32[]{:S(2)}) async-start(bf16[8,2,3,2,1024]{4,3,2,1,0:T(2,128)(2,1)} %bitcast.35), calls=%async_computation | async-start | bytes 393216 | tf_op jit(solution)/shard_map/all_to_all | solution.py:241
  21.5 107.0 %all-gather.8.cloned.1.call-start = ((), (), s32[]{:S(2)}) async-start(), calls=%async_computation.4 | async-start | bytes 2228224 | tf_op jit(solution)/shard_map/all_gather | solution.py:24
  30.7 5.9 %copy-start.4 = (bf16[8,2,3,2,1024]{4,3,2,1,0:T(2,128)(2,1)}, bf16[8,2,3,2,1024]{4,3,2,1,0:T(2,128)(2,1)S(1)}, u32[]{:S(2)}) copy-start(bf16[8,2,3,2,1024]{4,3,2,1,0:T(2,128)(2,1)S(1)} %all-to-all-done) | copy-start | bytes 589828
  33.7 0.7 copy-start.7
  35.1 150.8 %all-gather.6.cloned.1.call-start = ((), (), s32[]{:S(2)}) async-start(), calls=%async_computation.3 | async-start | bytes 4456448 | tf_op jit(solution)/shard_map/all_gather | solution.py:16
  40.6 23.1 %copy-start.8 = (f32[8,2,2,8,64]{4,2,3,1,0:T(2,128)S(1)}, f32[8,2,2,8,64]{4,2,3,1,0:T(2,128)}, u32[]{:S(2)}) copy-start(f32[8,2,2,8,64]{4,2,3,1,0:T(2,128)} %copy-done.7) | copy-start | bytes 196612
  40.6 86.0 %copy-start.5 = (bf16[8,2,3,2,1024]{4,3,2,1,0:T(2,128)(2,1)S(1)}, bf16[8,2,3,2,1024]{4,3,2,1,0:T(2,128)(2,1)}, u32[]{:S(2)}) copy-start(bf16[8,2,3,2,1024]{4,3,2,1,0:T(2,128)(2,1)} %copy-done.4) | copy-start | bytes 589828
  128.5 1.6 slice-start
  147.6 9.6 %all-to-all-start.1 = ((bf16[4,2,1024]{2,1,0:T(2,128)(2,1)}), bf16[4,2,1024]{2,1,0:T(2,128)(2,1)S(1)}, u32[]{:S(2)}, u32[]{:S(2)}) async-start(bf16[4,2,1024]{2,1,0:T(2,128)(2,1)} %reshape.849), calls=%async_computation.1 | async-start | bytes 32768 | tf_op jit(solution)/shard_map/all_to_all | solution.py:38
  158.1 8.1 %all-to-all-start.2 = ((bf16[8,2,128]{2,1,0:T(2,128)(2,1)}), bf16[8,2,128]{2,1,0:T(2,128)(2,1)S(1)}, u32[]{:S(2)}, u32[]{:S(2)}) async-start(bf16[8,2,128]{2,1,0:T(2,128)(2,1)} %reshape.851), calls=%async_computation.2 | async-start | bytes 8192 | tf_op jit(solution)/shard_map/all_to_all | solution.py:245
  167.3 21.1 %copy-start.9 = (bf16[16,2,64]{2,1,0:T(2,128)(2,1)}, bf16[16,2,64]{2,1,0:T(2,128)(2,1)S(1)}, u32[]{:S(2)}) copy-start(bf16[16,2,64]{2,1,0:T(2,128)(2,1)S(1)} %scatter_fusion) | copy-start | bytes 12292
  167.3 21.1 %copy-start.6 = (bf16[512,128]{1,0:T(8,128)(2,1)S(1)}, bf16[512,128]{1,0:T(8,128)(2,1)}, u32[]{:S(2)}) copy-start(bf16[512,128]{1,0:T(8,128)(2,1)} %get-tuple-element.165) | copy-start | bytes 393220
  206.0 2.3 %copy-start.2 = (f32[4,1,512,128]{3,2,1,0:T(8,128)S(1)}, f32[4,1,512,128]{3,2,1,0:T(8,128)}, u32[]{:S(2)}) copy-start(f32[4,1,512,128]{3,2,1,0:T(8,128)} %get-tuple-element.85) | copy-start | bytes 3145732
Sparse Core Ops, SparseCore 0:
  35.2 73.1 all-gather.7
  111.1 74.8 all-gather.5
where the time goes:
time: 220 us; the launch traced here: 218 us
  blocking collectives  61.4 us (28%)
  other arithmetic  48.1 us (22%)
  local copies, waits for them, and re-layouts  28.1 us (13%)
  waiting for transfers between devices  26.4 us (12%)
  matrix products  20.9 us (10%)
  starting transfers between devices  18.4 us (8%)
  between operations  14.6 us (7%)
    all_gather x2, blocking collectives, merged_2(): pieces = jax.tree.map(lambda part: lax.all_gather(part, axis), value)  61.4 us
    all_gather x1, waiting for transfers between devices, in_one_piece(): lax.all_gather(both, axis, axis=dim, tiled=True)  18.6 us
    reduce_sum x3, other arithmetic, pick_rows(): jnp.sum(jnp.where(member, shaped, jnp.zeros((), field.dtype)), axis=1)  17.3 us
    add x15, other arithmetic, merge_pair(): weight_sum = earlier_part[1] * factor_one + later_part[1] * factor_two  11.5 us
    dot_general x6, matrix products, partial_block(): jnp.einsum('hqk,khd->hqd', weights.astype(jnp.bfloat16), value_rows, pref...  9.46 us
    all_to_all x1, starting transfers between devices, on_device(): lax.all_to_all(dec_new[slot_rows], 'req', split_axis=0, concat_axis=0, ti...  9.15 us
    reduce_sum x6, other arithmetic, partial_block(): weight_sum = jnp.sum(weights, axis=-1)  7.2 us
    all_to_all x1, waiting for transfers between devices, sum_at_owner(): blocks = lax.all_to_all(in_blocks(x, dim, count), axis, 0, 0, tiled=True)  5.36 us
  transfers between devices with their start and end apart: 5, of which 3 were waited for; matrix products, arithmetic and copies ran while one was open for 28% of the time, Pallas kernels for 0%

commit v1 on v0

v1 whole, which is shorter than its diff:
```python
import functools
import math

import jax
import jax.numpy as jnp
from jax import lax
from jax.experimental import pallas as pl
from jax.experimental.pallas import tpu as pltpu
from jax.sharding import PartitionSpec as P

HD = 128
NEG = -1e30
EXP_SCALE = HD**-0.5 * math.log2(math.e)
F32 = jnp.float32
BF16 = jnp.bfloat16

VMEM = pltpu.VMEM
SMEM = pltpu.SMEM


def vspec():
    return pl.BlockSpec(memory_space=pltpu.VMEM)


def sspec():
    return pl.BlockSpec(memory_space=pltpu.SMEM)


def dot_t(a, b):
    return lax.dot_general(a, b, (((1,), (1,)), ((), ())), preferred_element_type=F32)


def dot_n(a, b):
    return lax.dot_general(a, b, (((1,), (0,)), ((), ())), preferred_element_type=F32)


def call(body, out_shape, ins, specs, scratch=(), flops=0, nbytes=0, trans=0):
    single = not isinstance(out_shape, (tuple, list))
    return pl.pallas_call(
        body,
        out_shape=out_shape,
        in_specs=specs,
        out_specs=vspec() if single else tuple(vspec() for _ in out_shape),
        scratch_shapes=list(scratch),
        compiler_params=pltpu.CompilerParams(vmem_limit_bytes=56 * 1024 * 1024),
        cost_estimate=pl.CostEstimate(flops=flops, bytes_accessed=nbytes, transcendentals=trans),
    )(*ins)


def head_id():
    return lax.axis_index("head") * lax.axis_size("req") + lax.axis_index("req")


def class_residue(c):
    j = head_id()
    r4 = lax.rem(j, 4)
    inner = lax.div(lax.rem(j, 16), 4)
    return 4 * lax.rem(c + inner, 4) + r4


def rank_in_block(own, first, k):
    grp = lax.shift_right_logical(own[first + k], 4)
    rank = jnp.int32(0)
    for e in range(k):
        rank += (lax.shift_right_logical(own[first + e], 4) == grp).astype(jnp.int32)
    return grp, rank


def route_kernel(own, dec, out, sem):
    me = lax.axis_index("req")
    copies = []
    for b in range(8):
        src = [jnp.int32(0), jnp.int32(0)]
        for k in range(4):
            slot = own[4 * b + k]
            grp, rank = rank_in_block(own, 4 * b, k)
            mine = grp == me
            for r in range(2):
                src[r] = jnp.where(mine & (rank == r), lax.rem(slot, 16), src[r])
        for r in range(2):
            cp = pltpu.make_async_copy(dec.at[src[r]], out.at[2 * b + r], sem.at[2 * b + r])
            cp.start()
            copies.append(cp)
    for cp in copies:
        cp.wait()


def pick_kernel(qkv, qm, kvm, kvf, wide):
    rows = qkv.shape[1]
    for part in range(3):
        wide[...] = qkv[part].astype(F32)
        for c in range(4):
            start = class_residue(c)
            got = wide[pl.ds(start, rows // 16, stride=16), :].astype(BF16)
            if part == 0:
                qm[pl.ds(128 * c, 128), :] = got
            else:
                kvm[pl.ds(128 * c, 128), pl.ds(128 * (part - 1), 128)] = got
                if c == 0:
                    kvf[:, pl.ds(128 * (part - 1), 128)] = got


def softmax_step(m, l, acc, s, v, mult=None):
    m_new = jnp.maximum(m, jnp.max(s, axis=1, keepdims=True))
    alpha = jnp.exp2((m - m_new) * EXP_SCALE)
    p = jnp.exp2((s - m_new) * EXP_SCALE)
    if mult is not None:
        p = p * mult
    l_new = l * alpha + jnp.sum(p, axis=1, keepdims=True)
    acc_new = acc * alpha + dot_n(p.astype(BF16), v)
    return m_new, l_new, acc_new


def near_kernel(qkv, qm, kvm, near_o, acc_o, m_o, l_o, acc_s, m_s, l_s):
    rows = qkv.shape[1]
    step = 256
    tri = lax.broadcasted_iota(jnp.int32, (step, step), 1) <= lax.broadcasted_iota(
        jnp.int32, (step, step), 0
    )
    for b in range(rows // step):
        at = pl.ds(step * b, step)
        q = qkv[0, at, :]
        s_d = jnp.where(tri, dot_t(q, qkv[1, at, :]), NEG)
        m = jnp.max(s_d, axis=1, keepdims=True)
        if b:
            s_f = dot_t(q, qkv[1, pl.ds(0, step * b), :])
            m = jnp.maximum(m, jnp.max(s_f, axis=1, keepdims=True))
        p_d = jnp.exp2((s_d - m) * EXP_SCALE)
        l = jnp.sum(p_d, axis=1, keepdims=True)
        acc = dot_n(p_d.astype(BF16), qkv[2, at, :])
        if b:
            p_f = jnp.exp2((s_f - m) * EXP_SCALE)
            l = l + jnp.sum(p_f, axis=1, keepdims=True)
            acc = acc + dot_n(p_f.astype(BF16), qkv[2, pl.ds(0, step * b), :])
        near_o[at, :] = (acc / l).astype(BF16)
        acc_s[at, :] = acc
        m_s[at, :] = jnp.broadcast_to(m, (step, HD))
        l_s[at, :] = jnp.broadcast_to(l, (step, HD))
    inner = lax.div(lax.rem(head_id(), 16), 4)

    def order(shape, dim):
        a = lax.broadcasted_iota(jnp.int32, shape, dim)
        return 4 * (a & 127) + ((lax.shift_right_logical(a, 7) + inner) & 3)

    for c in range(4):
        at = pl.ds(128 * c, 128)
        pick = pl.ds(class_residue(c), 128, stride=16)
        s = dot_t(qm[at, :], kvm[:, pl.ds(0, HD)])
        rows_at = lax.broadcasted_iota(jnp.int32, (128, 1), 0)
        row_order = 4 * rows_at + ((c + inner) & 3)
        s = jnp.where(order((1, 512), 1) <= row_order, s, NEG)
        mult = None
        if c == 0:
            mult = jnp.where(lax.broadcasted_iota(jnp.int32, (1, 512), 1) < 128, 2.0, 1.0)
        m, l, acc = softmax_step(
            m_s[pick, :][:, :1], l_s[pick, :][:, :1], acc_s[pick, :], s, kvm[:, pl.ds(HD, HD)], mult
        )
        acc_o[at, :] = acc
        m_o[at, :] = jnp.broadcast_to(m, (128, HD))
        l_o[at, :] = jnp.broadcast_to(l, (128, HD))


def far_kernel(qm, kv1, kv2, kv3, kvf, near_o, acc_i, m_i, l_i, out, acc_s, m_s, l_s, wide):
    z = lax.axis_index("seq")
    local = lax.rem(z, 4)
    group = lax.div(z, 4)
    acc_s[...] = acc_i[...]
    m_s[...] = m_i[...]
    l_s[...] = l_i[...]

    def update(rows, keys, values, mask_from=None):
        at = pl.ds(0, rows)
        s = dot_t(qm[at, :], keys)
        if mask_from is not None:
            col = lax.broadcasted_iota(jnp.int32, (1, s.shape[1]), 1)
            s = jnp.where(col < mask_from, s, NEG)
        m, l, acc = softmax_step(m_s[at, :][:, :1], l_s[at, :][:, :1], acc_s[at, :], s, values)
        acc_s[at, :] = acc
        m_s[at, :] = jnp.broadcast_to(m, (rows, HD))
        l_s[at, :] = jnp.broadcast_to(l, (rows, HD))

    for d, kv in ((1, kv1), (2, kv2), (3, kv3)):

        @pl.when(local >= d)
        def _(kv=kv):
            update(512, kv[:, pl.ds(0, HD)], kv[:, pl.ds(HD, HD)])

    for g in range(4):
        at = pl.ds(512 * g, 512)

        @pl.when(z > 4 * g)
        def _(at=at, g=g):
            update(128, kvf[at, pl.ds(0, HD)], kvf[at, pl.ds(HD, HD)], 128 * z - 512 * g)

    wide[...] = near_o[...].astype(F32)
    for c in range(4):
        at = pl.ds(128 * c, 128)
        wide[pl.ds(class_residue(c), 128, stride=16), :] = acc_s[at, :] / l_s[at, :]
    out[...] = wide[...].astype(BF16)


def pieces(x):
    hi = x.astype(BF16).astype(F32)
    rest = x - hi
    mid = rest.astype(BF16).astype(F32)
    return hi, mid, (rest - mid).astype(BF16).astype(F32)


def cache_kernel(own, lens, arr, cache, out, o_s, st_s):
    z = lax.axis_index("seq")
    me = lax.axis_index("req")
    per = cache.shape[2]
    width = cache.shape[3]
    diag = lax.shift_right_logical(
        lax.broadcasted_iota(jnp.int32, (16, width), 1), 7
    ) == lax.shift_right_logical(lax.broadcasted_iota(jnp.int32, (16, width), 0), 1)
    token = lax.broadcasted_iota(jnp.int32, (16, 16), 0) & 1
    new_col = lax.broadcasted_iota(jnp.int32, (16, 16), 1)
    new_ok = (new_col <= token) & (z == 0)
    col = z * per + lax.broadcasted_iota(jnp.int32, (16, per), 1)
    row_head = lax.shift_right_logical(lax.broadcasted_iota(jnp.int32, (16, HD), 0), 1)
    lane = lax.broadcasted_iota(jnp.int32, (16, HD), 1)
    pad = jnp.zeros((14, width), F32)
    for k in range(4):
        grp, rank = rank_in_block(own, 4 * me, k)
        row = 2 * grp + rank
        q = arr[row, 0].astype(F32)
        qd = jnp.where(diag, jnp.concatenate([q] * 8, axis=0), 0.0).astype(BF16)
        kn = jnp.concatenate([arr[row, 1].astype(F32), pad], axis=0).astype(BF16)
        vn = jnp.concatenate([arr[row, 2].astype(F32), pad], axis=0).astype(BF16)
        c_ok = col < lens[4 * me + k]
        s_c = jnp.where(c_ok, dot_t(qd, cache[k, 0]), NEG)
        s_n = jnp.where(new_ok, dot_t(qd, kn), NEG)
        m = jnp.maximum(
            jnp.max(s_c, axis=1, keepdims=True), jnp.max(s_n, axis=1, keepdims=True)
        )
        p_c = jnp.where(c_ok, jnp.exp2((s_c - m) * EXP_SCALE), 0.0)
        p_n = jnp.where(new_ok, jnp.exp2((s_n - m) * EXP_SCALE), 0.0)
        l = jnp.sum(p_c, axis=1, keepdims=True) + jnp.sum(p_n, axis=1, keepdims=True)
        full = dot_n(p_c.astype(BF16), cache[k, 1]) + dot_n(p_n.astype(BF16), vn)
        o = jnp.zeros((16, HD), F32)
        for h in range(8):
            o = jnp.where(row_head == h, full[:, HD * h : HD * (h + 1)], o)
        o = o / jnp.where(l > 0.0, l, 1.0)
        st = jnp.zeros((16, HD), F32)
        for at, piece in enumerate(pieces(m) + pieces(l)):
            st = jnp.where(lane == at, piece, st)
        for h in range(8):
            o_s[pl.ds(8 * h + 2 * k, 2), :] = o[2 * h : 2 * h + 2]
            st_s[pl.ds(8 * h + 2 * k, 2), :] = st[2 * h : 2 * h + 2]
    values = o_s[...].astype(BF16)
    turned = st_s[...].T
    stats = jnp.concatenate([turned[:16, :], jnp.zeros((16, 64), F32)], axis=1).astype(BF16)
    for t in range(out.shape[0]):
        out[t, pl.ds(0, 64), :] = values
        out[t, pl.ds(64, 16), :] = stats


def project_kernel(own, got, weight, out):
    me = lax.axis_index("req")
    count = got.shape[0]
    ms, ls = [], []
    for t in range(count):
        st = got[t, pl.ds(64, 16), :].astype(F32)
        ms.append(st[0:1] + st[1:2] + st[2:3])
        ls.append(st[3:4] + st[4:5] + st[5:6])
    m = jnp.concatenate(ms, axis=0)
    l = jnp.concatenate(ls, axis=0)
    share = jnp.exp2((m - jnp.max(m, axis=0, keepdims=True)) * EXP_SCALE) * l
    share = share / jnp.sum(share, axis=0, keepdims=True)
    share = jnp.concatenate([share, jnp.zeros((128 - count, HD), F32)], axis=0).T
    total = jnp.zeros((64, HD), F32)
    for t in range(count):
        total = total + share[:64, t : t + 1] * got[t, pl.ds(0, 64), :].astype(F32)
    rows = jnp.concatenate([total[8 * h : 8 * h + 8] for h in range(8)], axis=1)
    y = dot_n(rows.astype(BF16), weight[...])
    out[...] = jnp.zeros(out.shape, BF16)
    for k in range(4):
        grp, rank = rank_in_block(own, 4 * me, k)
        for h in range(4):
            out[16 * h + 2 * grp + rank] = y[2 * k : 2 * k + 2, 64 * h : 64 * h + 64].astype(BF16)


def settle_kernel(own, got, out):
    me = lax.axis_index("req")
    out[...] = jnp.zeros(out.shape, BF16)
    for b in range(8):
        for k in range(4):
            slot = own[4 * b + k]
            grp, rank = rank_in_block(own, 4 * b, k)

            @pl.when(grp == me)
            def _(b=b, slot=slot, rank=rank):
                total = got[2 * b + rank].astype(F32)
                for h in range(1, 4):
                    total = total + got[16 * h + 2 * b + rank].astype(F32)
                out[lax.rem(slot, 16)] = total.astype(BF16)


def shape(dims, dtype=BF16):
    return jax.ShapeDtypeStruct(dims, dtype)


def on_device(pre_qkv, cache_kv, dec_new, out_weight, owner_slot, prompt_lengths):
    qkv = jnp.swapaxes(pre_qkv, 0, 1)
    sent = pl.pallas_call(
        route_kernel,
        out_shape=shape(dec_new.shape),
        in_specs=[sspec(), pl.BlockSpec(memory_space=pl.ANY)],
        out_specs=vspec(),
        scratch_shapes=[pltpu.SemaphoreType.DMA((16,))],
        cost_estimate=pl.CostEstimate(flops=0, bytes_accessed=400000, transcendentals=0),
    )(owner_slot, dec_new)
    arrived = lax.all_to_all(sent, "req", 0, 0, tiled=True)
    qm, kvm, kvf = call(
        pick_kernel,
        (shape((512, HD)), shape((512, 2 * HD)), shape((128, 2 * HD))),
        (qkv,),
        [vspec()],
        [VMEM((2048, HD), F32)],
        nbytes=2000000,
    )
    far = lax.all_gather(kvf, "seq", axis=0, tiled=True)
    mids = [
        lax.ppermute(kvm, "seq", [(i, i + d) for i in range(16) if i % 4 + d < 4])
        for d in (1, 2, 3)
    ]
    partial = call(
        cache_kernel,
        shape((16, 80, HD)),
        (owner_slot, prompt_lengths, arrived, cache_kv),
        [sspec(), sspec(), vspec(), vspec()],
        [VMEM((64, HD), F32), VMEM((64, HD), F32)],
        flops=10**8,
        nbytes=2000000,
    )
    parts = lax.all_to_all(partial, "seq", 0, 0, tiled=True)
    state = [shape((512, HD), F32)] * 3
    near_o, acc, m, l = call(
        near_kernel,
        (shape((2048, HD)), *state),
        (qkv, qm, kvm),
        [vspec()] * 3,
        [VMEM((2048, HD), F32)] * 3,
        flops=2 * 10**9,
        nbytes=3000000,
        trans=2 * 10**6,
    )
    answers = call(
        project_kernel,
        shape((64, 2, 64)),
        (owner_slot, parts, out_weight),
        [sspec(), vspec(), vspec()],
        flops=10**7,
        nbytes=1000000,
    )
    results = lax.all_to_all(answers, ("head", "req"), 0, 0, tiled=True)
    prefill_out = call(
        far_kernel,
        shape((2048, HD)),
        (qm, *mids, far, near_o, acc, m, l),
        [vspec()] * 9,
        [VMEM((512, HD), F32)] * 3 + [VMEM((2048, HD), F32)],
        flops=10**9,
        nbytes=4000000,
        trans=10**6,
    )
    decode_out = call(
        settle_kernel,
        shape((16, 2, 64)),
        (owner_slot, results),
        [sspec(), vspec()],
        nbytes=100000,
    )
    return prefill_out, decode_out


def solution(mesh):
    return jax.shard_map(
        on_device,
        mesh=mesh,
        in_specs=(
            P("seq", None, ("head", "req")),
            P("req", None, "seq", "head"),
            P("req", None, None, "head"),
            P("head", "seq"),
            P(),
            P(),
        ),
        out_specs=(P("seq", ("head", "req")), P("req", None, ("seq", "head"))),
        check_vma=False,
    )
```

time: 220 us -> 112 us (0.51)
  the two profiles are of different devices: /device:TPU:6 before, /device:TPU:70 now
where the time goes in v1:
time: 112 us; the launch traced here: 111 us
  waiting for transfers between devices  28.5 us (25%)
  Pallas kernels  28.4 us (25%)
  starting transfers between devices  27.3 us (24%)
  between operations  14.1 us (13%)
  blocking collectives  9.45 us (8%)
  local copies, waits for them, and re-layouts  2.89 us (3%)
    pallas_call x6, Pallas kernels, call(): pl.pallas_call(body, out_shape=out_shape, in_specs=specs, out_specs=vspec...  25.5 us
    all_to_all x1, waiting for transfers between devices, on_device(): parts = lax.all_to_all(partial, 'seq', 0, 0, tiled=True)  16.8 us
    all_to_all x1, starting transfers between devices, on_device(): parts = lax.all_to_all(partial, 'seq', 0, 0, tiled=True)  14.8 us
    all_gather x1, waiting for transfers between devices, on_device(): far = lax.all_gather(kvf, 'seq', axis=0, tiled=True)  11.7 us
    all_to_all x1, blocking collectives, on_device(): arrived = lax.all_to_all(sent, 'req', 0, 0, tiled=True)  9.45 us
    all_to_all x1, starting transfers between devices, on_device(): results = lax.all_to_all(answers, ('head', 'req'), 0, 0, tiled=True)  7.13 us
    ppermute x3, starting transfers between devices, on_device(): lax.ppermute(kvm, 'seq', [(i, i + d) for i in range(16) if i % 4 + d < 4])  5.34 us
    pallas_call x1, Pallas kernels, on_device(): pl.pallas_call(route_kernel, out_shape=shape(dec_new.shape), in_specs=[ss...  2.92 us
  transfers between devices with their start and end apart: 6, of which 2 were waited for; matrix products, arithmetic and copies ran while one was open for 2% of the time, Pallas kernels for 17%

profile of v1, /device:TPU:70, one launch (start us, length us, event | category | flops | bytes accessed | tf_op | source)
XLA Modules:
  0.0 110.6 jit_solution(10522579785314208680)
XLA Ops:
  7.2 0.0 all-gather.2.cloned.1.call-start
  7.2 2.8 %shard_map.77 = (bf16[512,128]{1,0:T(8,128)(2,1)}, bf16[512,256]{1,0:T(8,128)(2,1)}, bf16[128,256]{1,0:T(8,128)(2,1)}) custom-call(bf16[3,2048,128]{2,1,0:T(8,128)(2,1)} %bitcast.1), custom_call_target="tpu_custom_call" | custom-call | bytes 2000000 | tf_op jit(solution)/shard_map/pallas_call | solution.py:39
  10.1 0.0 all-gather.2.cloned.1.call-update
  10.1 2.9 %shard_map.80 = bf16[16,3,2,1024]{3,2,1,0:T(2,128)(2,1)} custom-call(s32[32]{0:T(128)} %own.7, bf16[16,3,2,1024]{3,2,1,0:T(2,128)(2,1)} %dec.1), custom_call_target="tpu_custom_call" | custom-call | bytes 400000 | tf_op jit(solution)/shard_map/pallas_call | solution.py:306
  13.0 9.5 %all_to_all.15.arr = bf16[16,3,2,1024]{3,2,1,0:T(2,128)(2,1)} all-to-all(bf16[16,3,2,1024]{3,2,1,0:T(2,128)(2,1)} %shard_map.80), channel_id=1, replica_groups=mesh['seq'=16,'head'=4,'req'=8] {'req'}, dimensions={0} | all-to-all | bytes 393216 | tf_op jit(solution)/shard_map/all_to_all | solution.py:314
  22.5 3.4 %shard_map.81 = bf16[16,80,128]{2,1,0:T(8,128)(2,1)} custom-call(s32[32]{0:T(128)} %own.7, s32[32]{0:T(128)} %lens.1, bf16[16,3,2,1024]{3,2,1,0:T(2,128)(2,1)} %all_to_all.15.arr, bf16[4,2,64,1024]{3,2,1,0:T(8,128)(2,1)} %cache.1), custom_call_target="tpu_custom_call" | custom-call | flops 100000000 | bytes 2000000 | tf_op jit(solution)/shard_map/pallas_call | solution.py:39
  25.8 14.8 %all-to-all-start.1 = ((bf16[16,80,128]{2,1,0:T(8,128)(2,1)}), bf16[16,80,128]{2,1,0:T(8,128)(2,1)S(1)}, u32[]{:S(2)}, u32[]{:S(2)}) async-start(bf16[16,80,128]{2,1,0:T(8,128)(2,1)} %shard_map.81), calls=%async_computation.1 | async-start | bytes 655360 | tf_op jit(solution)/shard_map/all_to_all | solution.py:337
  40.6 3.4 %collective-permute-start = (bf16[512,256]{1,0:T(8,128)(2,1)S(1)}, bf16[512,256]{1,0:T(8,128)(2,1)S(1)}, u32[]{:S(2)}, u32[]{:S(2)}) collective-permute-start(bf16[512,256]{1,0:T(8,128)(2,1)S(1)} %copy-done.4), channel_id=1, source_target_pairs={{0,32},{32,64},{64,96},{128,160},{160,192},{192,224},{256,288},{28... | collective-permute-start | bytes 786440 | tf_op jit(solution)/shard_map/ppermute | solution.py:325
  44.0 1.3 %collective-permute-start.1 = (bf16[512,256]{1,0:T(8,128)(2,1)S(1)}, bf16[512,256]{1,0:T(8,128)(2,1)S(1)}, u32[]{:S(2)}, u32[]{:S(2)}) collective-permute-start(bf16[512,256]{1,0:T(8,128)(2,1)S(1)} %copy-done.4), channel_id=1, source_target_pairs={{0,64},{32,96},{128,192},{160,224},{256,320},{288,352},{384,448},{... | collective-permute-start | bytes 786440 | tf_op jit(solution)/shard_map/ppermute | solution.py:325
  45.3 0.7 collective-permute-start.2
  45.9 16.8 %all-to-all-done.1.got = bf16[16,80,128]{2,1,0:T(8,128)(2,1)S(1)} async-done(((bf16[16,80,128]{2,1,0:T(8,128)(2,1)}), bf16[16,80,128]{2,1,0:T(8,128)(2,1)S(1)}, u32[]{:S(2)}, u32[]{:S(2)}) %all-to-all-start.1) | async-done | bytes 327712 | tf_op jit(solution)/shard_map/all_to_all | solution.py:337
  62.7 0.7 copy-done
  63.5 2.3 %shard_map.82 = bf16[64,2,64]{2,1,0:T(2,128)(2,1)} custom-call(s32[32]{0:T(128)} %own.7, bf16[16,80,128]{2,1,0:T(8,128)(2,1)} %copy-done, bf16[1024,256]{1,0:T(8,128)(2,1)} %weight.1), custom_call_target="tpu_custom_call" | custom-call | flops 10000000 | bytes 1000000 | tf_op jit(solution)/shard_map/pallas_call | solution.py:39
  65.8 1.5 %reshape.4 = bf16[32,2,128]{2,1,0:T(2,128)(2,1)} reshape(bf16[64,2,64]{2,1,0:T(2,128)(2,1)} %shard_map.82) | data formatting | bytes 32768
  67.3 7.1 %all-to-all-start.2 = ((bf16[32,2,128]{2,1,0:T(2,128)(2,1)}), bf16[32,2,128]{2,1,0:T(2,128)(2,1)S(1)}, u32[]{:S(2)}, u32[]{:S(2)}) async-start(bf16[32,2,128]{2,1,0:T(2,128)(2,1)} %reshape.4), calls=%async_computation.2 | async-start | bytes 32768 | tf_op jit(solution)/shard_map/all_to_all | solution.py:357
  74.4 8.4 %shard_map.78 = (bf16[2048,128]{1,0:T(8,128)(2,1)}, f32[512,128]{1,0:T(8,128)}, f32[512,128]{1,0:T(8,128)}, f32[512,128]{1,0:T(8,128)}) custom-call(bf16[3,2048,128]{2,1,0:T(8,128)(2,1)} %bitcast.2, bf16[512,128]{1,0:T(8,128)(2,1)} %get-tuple-element.9.qm, bf16[512,256]{1,0:T(8,128)(2,1)} %get-tuple-element.10.kvm), custom_call_target="tpu_custom_call" | custom-call | flops 2000000000 | bytes 3000000 | tf_op jit(solution)/shard_map/pallas_call | solution.py:39
  82.7 0.0 all-to-all-done.2
  82.7 0.7 reshape.5.got
  83.4 1.7 %shard_map.83 = bf16[16,2,64]{2,1,0:T(2,128)(2,1)} custom-call(s32[32]{0:T(128)} %own.7, bf16[64,2,64]{2,1,0:T(2,128)(2,1)} %reshape.5.got), custom_call_target="tpu_custom_call" | custom-call | bytes 100000 | tf_op jit(solution)/shard_map/pallas_call | solution.py:39
  85.1 0.0 collective-permute-done.kv1
  85.1 0.0 collective-permute-done.1.kv2
  85.2 0.0 collective-permute-done.2.kv3
  85.2 11.7 %all-gather.2.cloned.1.call-done.kvf = bf16[2048,256]{1,0:T(8,128)(2,1)} async-done(((bf16[128,256]{1,0:T(8,128)(2,1)}), bf16[2048,256]{1,0:T(8,128)(2,1)}) %all-gather.2.cloned.1.call-update) | async-done | bytes 1048592 | tf_op jit(solution)/shard_map/all_gather | solution.py:323
  96.8 6.9 %shard_map.79 = bf16[2048,128]{1,0:T(8,128)(2,1)} custom-call(bf16[512,128]{1,0:T(8,128)(2,1)} %get-tuple-element.9.qm, bf16[512,256]{1,0:T(8,128)(2,1)} %copy-done.1, bf16[512,256]{1,0:T(8,128)(2,1)} %copy-done.2, bf16[512,256]{1,0:T(8,128)(2,1)} %copy-done.3, bf16[2048,256]{1,0:T(8,128)(2,1)} %all-gather.2.cloned.1.call-done.kvf, ...), custom_call_target="tpu_custom_call" | custom-call | flops 1000000000 | bytes 4000000 | tf_op jit(solution)/shard_map/pallas_call | solution.py:39
  (9 shorter events, 0.0 us)
Async XLA Ops:
  7.2 89.7 %all-gather.2.cloned.1.call-start = ((), (), s32[]{:S(2)}) async-start(), calls=%async_computation.3 | async-start | bytes 1114112 | tf_op jit(solution)/shard_map/all_gather | solution.py:323
  10.0 30.5 %copy-start.4 = (bf16[512,256]{1,0:T(8,128)(2,1)S(1)}, bf16[512,256]{1,0:T(8,128)(2,1)}, u32[]{:S(2)}) copy-start(bf16[512,256]{1,0:T(8,128)(2,1)} %get-tuple-element.10.kvm) | copy-start | bytes 786436
  25.8 36.9 %all-to-all-start.1 = ((bf16[16,80,128]{2,1,0:T(8,128)(2,1)}), bf16[16,80,128]{2,1,0:T(8,128)(2,1)S(1)}, u32[]{:S(2)}, u32[]{:S(2)}) async-start(bf16[16,80,128]{2,1,0:T(8,128)(2,1)} %shard_map.81), calls=%async_computation.1 | async-start | bytes 655360 | tf_op jit(solution)/shard_map/all_to_all | solution.py:337
  40.6 44.6 %collective-permute-start = (bf16[512,256]{1,0:T(8,128)(2,1)S(1)}, bf16[512,256]{1,0:T(8,128)(2,1)S(1)}, u32[]{:S(2)}, u32[]{:S(2)}) collective-permute-start(bf16[512,256]{1,0:T(8,128)(2,1)S(1)} %copy-done.4), channel_id=1, source_target_pairs={{0,32},{32,64},{64,96},{128,160},{160,192},{192,224},{256,288},{28... | collective-permute-start | bytes 786440 | tf_op jit(solution)/shard_map/ppermute | solution.py:325
  44.0 41.2 %collective-permute-start.1 = (bf16[512,256]{1,0:T(8,128)(2,1)S(1)}, bf16[512,256]{1,0:T(8,128)(2,1)S(1)}, u32[]{:S(2)}, u32[]{:S(2)}) collective-permute-start(bf16[512,256]{1,0:T(8,128)(2,1)S(1)} %copy-done.4), channel_id=1, source_target_pairs={{0,64},{32,96},{128,192},{160,224},{256,320},{288,352},{384,448},{... | collective-permute-start | bytes 786440 | tf_op jit(solution)/shard_map/ppermute | solution.py:325
  45.3 39.9 %collective-permute-start.2 = (bf16[512,256]{1,0:T(8,128)(2,1)S(1)}, bf16[512,256]{1,0:T(8,128)(2,1)S(1)}, u32[]{:S(2)}, u32[]{:S(2)}) collective-permute-start(bf16[512,256]{1,0:T(8,128)(2,1)S(1)} %copy-done.4), channel_id=1, source_target_pairs={{0,96},{128,224},{256,352},{384,480},{1,97},{129,225},{257,353},{3... | collective-permute-start | bytes 786440 | tf_op jit(solution)/shard_map/ppermute | solution.py:325
  62.7 0.7 copy-start
  67.3 15.5 %all-to-all-start.2 = ((bf16[32,2,128]{2,1,0:T(2,128)(2,1)}), bf16[32,2,128]{2,1,0:T(2,128)(2,1)S(1)}, u32[]{:S(2)}, u32[]{:S(2)}) async-start(bf16[32,2,128]{2,1,0:T(2,128)(2,1)} %reshape.4), calls=%async_computation.2 | async-start | bytes 32768 | tf_op jit(solution)/shard_map/all_to_all | solution.py:357
  85.1 11.7 %copy-start.1 = (bf16[512,256]{1,0:T(8,128)(2,1)}, bf16[512,256]{1,0:T(8,128)(2,1)S(1)}, u32[]{:S(2)}) copy-start(bf16[512,256]{1,0:T(8,128)(2,1)S(1)} %collective-permute-done.kv1) | copy-start | bytes 786436
  85.1 11.7 %copy-start.2 = (bf16[512,256]{1,0:T(8,128)(2,1)}, bf16[512,256]{1,0:T(8,128)(2,1)S(1)}, u32[]{:S(2)}) copy-start(bf16[512,256]{1,0:T(8,128)(2,1)S(1)} %collective-permute-done.1.kv2) | copy-start | bytes 786436
  85.2 11.7 %copy-start.3 = (bf16[512,256]{1,0:T(8,128)(2,1)}, bf16[512,256]{1,0:T(8,128)(2,1)S(1)}, u32[]{:S(2)}) copy-start(bf16[512,256]{1,0:T(8,128)(2,1)S(1)} %collective-permute-done.2.kv3) | copy-start | bytes 786436
Sparse Core Ops, SparseCore 0:
  10.2 86.5 all-gather.1

commit v2 on v1

--- a/solution.py
+++ b/solution.py
@@ -15,7 +15,6 @@
 BF16 = jnp.bfloat16
 
 VMEM = pltpu.VMEM
-SMEM = pltpu.SMEM
 
 
 def vspec():
@@ -34,7 +33,7 @@
     return lax.dot_general(a, b, (((1,), (0,)), ((), ())), preferred_element_type=F32)
 
 
-def call(body, out_shape, ins, specs, scratch=(), flops=0, nbytes=0, trans=0):
+def call(body, out_shape, ins, specs, scratch=(), vmem=24, flops=0, nbytes=0, trans=0):
     single = not isinstance(out_shape, (tuple, list))
     return pl.pallas_call(
         body,
@@ -42,7 +41,7 @@
         in_specs=specs,
         out_specs=vspec() if single else tuple(vspec() for _ in out_shape),
         scratch_shapes=list(scratch),
-        compiler_params=pltpu.CompilerParams(vmem_limit_bytes=56 * 1024 * 1024),
+        compiler_params=pltpu.CompilerParams(vmem_limit_bytes=vmem * 1024 * 1024),
         cost_estimate=pl.CostEstimate(flops=flops, bytes_accessed=nbytes, transcendentals=trans),
     )(*ins)
 
@@ -85,19 +84,26 @@
         cp.wait()
 
 
-def pick_kernel(qkv, qm, kvm, kvf, wide):
+def pick_kernel(qkv, qm, kvm, ask, msg, far, wide):
     rows = qkv.shape[1]
     for part in range(3):
         wide[...] = qkv[part].astype(F32)
         for c in range(4):
             start = class_residue(c)
             got = wide[pl.ds(start, rows // 16, stride=16), :].astype(BF16)
+            at = pl.ds(128 * c, 128)
             if part == 0:
-                qm[pl.ds(128 * c, 128), :] = got
+                qm[at, :] = got
+                if c == 0:
+                    ask[...] = got
+                    msg[pl.ds(512, 64), pl.ds(0, HD)] = got[:64]
+                    msg[pl.ds(512, 64), pl.ds(HD, HD)] = got[64:]
             else:
-                kvm[pl.ds(128 * c, 128), pl.ds(128 * (part - 1), 128)] = got
+                lanes = pl.ds(HD * (part - 1), HD)
+                kvm[at, lanes] = got
+                msg[at, lanes] = got
                 if c == 0:
-                    kvf[:, pl.ds(128 * (part - 1), 128)] = got
+                    far[:, lanes] = got
 
 
 def softmax_step(m, l, acc, s, v, mult=None):
@@ -160,42 +166,117 @@
         l_o[at, :] = jnp.broadcast_to(l, (128, HD))
 
 
-def far_kernel(qm, kv1, kv2, kv3, kvf, near_o, acc_i, m_i, l_i, out, acc_s, m_s, l_s, wide):
+def pack(rows_m, rows_l):
+    count = rows_m.shape[0]
+    lane = lax.broadcasted_iota(jnp.int32, (count, HD), 1)
+    st = jnp.zeros((count, HD), F32)
+    for at, piece in enumerate(pieces(rows_m) + pieces(rows_l)):
+        st = jnp.where(lane == at, piece, st)
+    blocks = [st[128 * i : 128 * i + 128].T[:8] for i in range(count // 128)]
+    if len(blocks) % 2:
+        blocks.append(jnp.zeros((8, HD), F32))
+    return jnp.concatenate(blocks, axis=0).astype(BF16)
+
+
+def unpack(rows):
+    st = rows.astype(F32)
+    m = st[0:1] + st[1:2] + st[2:3]
+    l = st[3:4] + st[4:5] + st[5:6]
+    turned = jnp.concatenate([m, l, jnp.zeros((126, HD), F32)], axis=0).T
+    return turned[:, 0:1], turned[:, 1:2]
+
+
+def share_kernel(
+    qm, kvm, got1, got2, got3, col1, col2, col3, acc_i, m_i, l_i,
+    acc_o, m_o, l_o, back1, back2, back3, acc_s, m_s, l_s,
+):
     z = lax.axis_index("seq")
     local = lax.rem(z, 4)
     group = lax.div(z, 4)
-    acc_s[...] = acc_i[...]
-    m_s[...] = m_i[...]
-    l_s[...] = l_i[...]
-
-    def update(rows, keys, values, mask_from=None):
-        at = pl.ds(0, rows)
-        s = dot_t(qm[at, :], keys)
-        if mask_from is not None:
-            col = lax.broadcasted_iota(jnp.int32, (1, s.shape[1]), 1)
-            s = jnp.where(col < mask_from, s, NEG)
-        m, l, acc = softmax_step(m_s[at, :][:, :1], l_s[at, :][:, :1], acc_s[at, :], s, values)
+    acc_s[pl.ds(0, 512), :] = acc_i[...]
+    m_s[pl.ds(0, 512), :] = m_i[...]
+    l_s[pl.ds(0, 512), :] = l_i[...]
+    acc_s[pl.ds(512, 768), :] = jnp.zeros((768, HD), F32)
+    m_s[pl.ds(512, 768), :] = jnp.full((768, HD), NEG, F32)
+    l_s[pl.ds(512, 768), :] = jnp.zeros((768, HD), F32)
+
+    def update(first, q, keys, values, twice=False):
+        count = q.shape[0]
+        at = pl.ds(first, count)
+        s = dot_t(q, keys)
+        mult = None
+        if twice:
+            width = s.shape[1]
+            mult = jnp.where(
+                (lax.broadcasted_iota(jnp.int32, (count, width), 0) < 128)
+                & ((lax.broadcasted_iota(jnp.int32, (count, width), 1) & 511) < 128),
+                2.0,
+                1.0,
+            )
+        m, l, acc = softmax_step(
+            m_s[at, :][:, :1], l_s[at, :][:, :1], acc_s[at, :], s, values, mult
+        )
         acc_s[at, :] = acc
-        m_s[at, :] = jnp.broadcast_to(m, (rows, HD))
-        l_s[at, :] = jnp.broadcast_to(l, (rows, HD))
-
-    for d, kv in ((1, kv1), (2, kv2), (3, kv3)):
-
-        @pl.when(local >= d)
-        def _(kv=kv):
-            update(512, kv[:, pl.ds(0, HD)], kv[:, pl.ds(HD, HD)])
-
-    for g in range(4):
-        at = pl.ds(512 * g, 512)
-
-        @pl.when(z > 4 * g)
-        def _(at=at, g=g):
-            update(128, kvf[at, pl.ds(0, HD)], kvf[at, pl.ds(HD, HD)], 128 * z - 512 * g)
-
+        m_s[at, :] = jnp.broadcast_to(m, (count, HD))
+        l_s[at, :] = jnp.broadcast_to(l, (count, HD))
+
+    own_k, own_v = kvm[:, pl.ds(0, HD)], kvm[:, pl.ds(HD, HD)]
+    one = pl.ds(0, 512)
+    one_k, one_v = got1[one, pl.ds(0, HD)], got1[one, pl.ds(HD, HD)]
+
+    @pl.when((local & 1) == 1)
+    def _():
+        update(0, qm[...], one_k, one_v, True)
+
+    @pl.when(local < 2)
+    def _():
+        update(512, got2[...], own_k, own_v, True)
+        update(512, got2[...], one_k, one_v, True)
+
+    half = pl.ds(512, 64)
+    head = pl.ds(0, 128)
+    queries = ((0, qm), (512, got2), (1152, got3))
+    for depth, col in ((1, col1), (2, col2), (3, col3)):
+
+        @pl.when(group >= depth)
+        def _(col=col):
+            k, v = col[:, pl.ds(0, HD)], col[:, pl.ds(HD, HD)]
+            for first, q in queries:
+                update(first, q[head, :], k, v)
+            near_q = jnp.concatenate(
+                [got1[half, pl.ds(0, HD)], got1[half, pl.ds(HD, HD)]], axis=0
+            )
+            update(1024, near_q, k, v)
+
+    acc_o[...] = acc_s[one, :]
+    m_o[...] = m_s[one, :]
+    l_o[...] = l_s[one, :]
+    for out, first, count in ((back2, 512, 512), (back1, 1024, 128), (back3, 1152, 128)):
+        at = pl.ds(first, count)
+        l = l_s[at, :]
+        out[pl.ds(0, count), :] = (acc_s[at, :] / jnp.where(l > 0.0, l, 1.0)).astype(BF16)
+        packed = pack(m_s[at, :], l)
+        out[pl.ds(count, packed.shape[0]), :] = packed
+
+
+def merge_kernel(near_o, acc, m, l, back1, back2, back3, out, wide):
     wide[...] = near_o[...].astype(F32)
     for c in range(4):
         at = pl.ds(128 * c, 128)
-        wide[pl.ds(class_residue(c), 128, stride=16), :] = acc_s[at, :] / l_s[at, :]
+        terms = [(m[at, :][:, :1], l[at, :][:, :1], acc[at, :])]
+        for part, rows, stat in ((back2, 128 * c, 512 + 8 * c), (back1, 0, 128), (back3, 0, 128)):
+            if c and part is not back2:
+                continue
+            pm, plen = unpack(part[pl.ds(stat // 16 * 16, 16), :][stat % 16 : stat % 16 + 8])
+            terms.append((pm, plen, part[pl.ds(rows, 128), :].astype(F32) * plen))
+        top = functools.reduce(jnp.maximum, [t[0] for t in terms])
+        total = 0.0
+        length = 0.0
+        for tm, tl, ta in terms:
+            w = jnp.exp2((tm - top) * EXP_SCALE)
+            length = length + tl * w
+            total = total + ta * w
+        wide[pl.ds(class_residue(c), 128, stride=16), :] = total / length
     out[...] = wide[...].astype(BF16)
 
 
@@ -301,7 +382,7 @@
     return jax.ShapeDtypeStruct(dims, dtype)
 
 
-def on_device(pre_qkv, cache_kv, dec_new, out_weight, owner_slot, prompt_lengths):
+def staged(pre_qkv, cache_kv, dec_new, out_weight, owner_slot, prompt_lengths):
     qkv = jnp.swapaxes(pre_qkv, 0, 1)
     sent = pl.pallas_call(
         route_kernel,
@@ -312,19 +393,31 @@
         cost_estimate=pl.CostEstimate(flops=0, bytes_accessed=400000, transcendentals=0),
     )(owner_slot, dec_new)
     arrived = lax.all_to_all(sent, "req", 0, 0, tiled=True)
-    qm, kvm, kvf = call(
+    qm, kvm, ask, msg, far = call(
         pick_kernel,
-        (shape((512, HD)), shape((512, 2 * HD)), shape((128, 2 * HD))),
+        (
+            shape((512, HD)),
+            shape((512, 2 * HD)),
+            shape((128, HD)),
+            shape((576, 2 * HD)),
+            shape((128, 2 * HD)),
+        ),
         (qkv,),
         [vspec()],
         [VMEM((2048, HD), F32)],
-        nbytes=2000000,
-    )
-    far = lax.all_gather(kvf, "seq", axis=0, tiled=True)
-    mids = [
-        lax.ppermute(kvm, "seq", [(i, i + d) for i in range(16) if i % 4 + d < 4])
-        for d in (1, 2, 3)
-    ]
+        nbytes=4000000,
+    )
+
+    def swap(x, bits):
+        return lax.ppermute(x, "seq", [(i, i ^ bits) for i in range(16)])
+
+    def relay(x, first):
+        return lax.ppermute(x, "seq", [(i, i + 4) for i in range(first, 12)])
+
+    col1 = relay(far, 0)
+    got1 = swap(msg, 1)
+    got2 = swap(qm, 2)
+    got3 = swap(ask, 3)
     partial = call(
         cache_kernel,
         shape((16, 80, HD)),
@@ -335,6 +428,7 @@
         nbytes=2000000,
     )
     parts = lax.all_to_all(partial, "seq", 0, 0, tiled=True)
+    col2 = relay(col1, 4)
     state = [shape((512, HD), F32)] * 3
     near_o, acc, m, l = call(
         near_kernel,
@@ -346,6 +440,20 @@
         nbytes=3000000,
         trans=2 * 10**6,
     )
+    col3 = relay(col2, 8)
+    acc, m, l, back1, back2, back3 = call(
+        share_kernel,
+        (*state, shape((144, HD)), shape((544, HD)), shape((144, HD))),
+        (qm, kvm, got1, got2, got3, col1, col2, col3, acc, m, l),
+        [vspec()] * 11,
+        [VMEM((1280, HD), F32)] * 3,
+        flops=10**9,
+        nbytes=4000000,
+        trans=10**6,
+    )
+    back1 = swap(back1, 1)
+    back2 = swap(back2, 2)
+    back3 = swap(back3, 3)
     answers = call(
         project_kernel,
         shape((64, 2, 64)),
@@ -356,14 +464,13 @@
     )
     results = lax.all_to_all(answers, ("head", "req"), 0, 0, tiled=True)
     prefill_out = call(
-        far_kernel,
+        merge_kernel,
         shape((2048, HD)),
-        (qm, *mids, far, near_o, acc, m, l),
-        [vspec()] * 9,
-        [VMEM((512, HD), F32)] * 3 + [VMEM((2048, HD), F32)],
-        flops=10**9,
+        (near_o, acc, m, l, back1, back2, back3),
+        [vspec()] * 7,
+        [VMEM((2048, HD), F32)],
+        flops=10**8,
         nbytes=4000000,
-        trans=10**6,
     )
     decode_out = call(
         settle_kernel,
@@ -377,7 +484,7 @@
 
 def solution(mesh):
     return jax.shard_map(
-        on_device,
+        staged,
         mesh=mesh,
         in_specs=(
             P("seq", None, ("head", "req")),

time: 112 us -> 113 us (level)
  the two profiles are of different devices: /device:TPU:70 before, /device:TPU:385 now
where the time goes in v2:
time: 113 us; the launch traced here: 112 us
  starting transfers between devices  39.6 us (35%)
  waiting for transfers between devices  33.1 us (29%)
  Pallas kernels  24.6 us (22%)
  blocking collectives  10.9 us (10%)
  local copies, waits for them, and re-layouts  3.33 us (3%)
    ppermute x3, waiting for transfers between devices, relay(): return lax.ppermute(x, 'seq', [(i, i + 4) for i in range(first, 12)])  28.2 us
    pallas_call x7, Pallas kernels, call(): pl.pallas_call(body, out_shape=out_shape, in_specs=specs, out_specs=vspec...  21.8 us
    ppermute x6, starting transfers between devices, swap(): return lax.ppermute(x, 'seq', [(i, i ^ bits) for i in range(16)])  16 us
    all_to_all x1, blocking collectives, staged(): arrived = lax.all_to_all(sent, 'req', 0, 0, tiled=True)  10.9 us
    all_to_all x1, starting transfers between devices, staged(): results = lax.all_to_all(answers, ('head', 'req'), 0, 0, tiled=True)  10.1 us
    all_to_all x1, starting transfers between devices, staged(): parts = lax.all_to_all(partial, 'seq', 0, 0, tiled=True)  9.65 us
    all_to_all x1, waiting for transfers between devices, staged(): results = lax.all_to_all(answers, ('head', 'req'), 0, 0, tiled=True)  4.82 us
    ppermute x3, starting transfers between devices, relay(): return lax.ppermute(x, 'seq', [(i, i + 4) for i in range(first, 12)])  3.85 us
  transfers between devices with their start and end apart: 11, of which 4 were waited for; matrix products, arithmetic and copies ran while one was open for 1% of the time, Pallas kernels for 16%

profile of v2, /device:TPU:385, one launch (start us, length us, event | category | flops | bytes accessed | tf_op | source)
XLA Modules:
  0.0 112.3 jit_solution(15158291517877458512)
XLA Ops:
  0.6 2.8 %shard_map.81 = bf16[16,3,2,1024]{3,2,1,0:T(2,128)(2,1)} custom-call(s32[32]{0:T(128)} %own.7, bf16[16,3,2,1024]{3,2,1,0:T(2,128)(2,1)} %dec.1), custom_call_target="tpu_custom_call" | custom-call | bytes 400000 | tf_op jit(solution)/shard_map/pallas_call | solution.py:387
  3.5 10.9 %all_to_all.15.arr = bf16[16,3,2,1024]{3,2,1,0:T(2,128)(2,1)S(1)} all-to-all(bf16[16,3,2,1024]{3,2,1,0:T(2,128)(2,1)} %shard_map.81), channel_id=1, replica_groups=mesh['seq'=16,'head'=4,'req'=8] {'req'}, dimensions={0} | all-to-all | bytes 393216 | tf_op jit(solution)/shard_map/all_to_all | solution.py:395
  14.3 1.2 %copy-done.1 = bf16[4,2,64,1024]{3,2,1,0:T(8,128)(2,1)S(1)} copy-done((bf16[4,2,64,1024]{3,2,1,0:T(8,128)(2,1)S(1)}, bf16[4,2,64,1024]{3,2,1,0:T(8,128)(2,1)}, u32[]{:S(2)}) %copy-start.1) | copy-done | bytes 1048600
  16.9 2.6 %shard_map.82 = bf16[16,80,128]{2,1,0:T(8,128)(2,1)} custom-call(s32[32]{0:T(128)S(1)} %copy-done.3, s32[32]{0:T(128)S(1)} %copy-done.5, bf16[16,3,2,1024]{3,2,1,0:T(2,128)(2,1)S(1)} %all_to_all.15.arr, bf16[4,2,64,1024]{3,2,1,0:T(8,128)(2,1)S(1)} %copy-done.1), custom_call_target="tpu_custom_call" | custom-call | flops 100000000 | bytes 2000000 | tf_op jit(solution)/shard_map/pallas_call | solution.py:38
  19.4 9.7 %all-to-all-start.1 = ((bf16[16,80,128]{2,1,0:T(8,128)(2,1)}), bf16[16,80,128]{2,1,0:T(8,128)(2,1)S(1)}, u32[]{:S(2)}, u32[]{:S(2)}) async-start(bf16[16,80,128]{2,1,0:T(8,128)(2,1)} %shard_map.82), calls=%async_computation.1 | async-start | bytes 655360 | tf_op jit(solution)/shard_map/all_to_all | solution.py:430
  29.7 1.3 %collective-permute-start.3 = (bf16[128,256]{1,0:T(8,128)(2,1)S(1)}, bf16[128,256]{1,0:T(8,128)(2,1)S(1)}, u32[]{:S(2)}, u32[]{:S(2)}) collective-permute-start(bf16[128,256]{1,0:T(8,128)(2,1)S(1)} %get-tuple-element.22), channel_id=1, source_target_pairs={{0,128},{32,160},{64,192},{96,224},{128,256},{160,288},{192,320},{... | collective-permute-start | bytes 196616 | tf_op jit(solution)/shard_map/ppermute | solution.py:415
  31.0 2.2 %collective-permute-start = (bf16[576,256]{1,0:T(8,128)(2,1)S(1)}, bf16[576,256]{1,0:T(8,128)(2,1)S(1)}, u32[]{:S(2)}, u32[]{:S(2)}) collective-permute-start(bf16[576,256]{1,0:T(8,128)(2,1)S(1)} %get-tuple-element.20), channel_id=1, source_target_pairs={{0,32},{32,0},{64,96},{96,64},{128,160},{160,128},{192,224},{224,1... | collective-permute-start | bytes 884744 | tf_op jit(solution)/shard_map/ppermute | solution.py:412
  33.2 19.0 %collective-permute-done.3.col1 = bf16[128,256]{1,0:T(8,128)(2,1)S(1)} collective-permute-done((bf16[128,256]{1,0:T(8,128)(2,1)S(1)}, bf16[128,256]{1,0:T(8,128)(2,1)S(1)}, u32[]{:S(2)}, u32[]{:S(2)}) %collective-permute-start.3) | collective-permute-done | bytes 65568 | tf_op jit(solution)/shard_map/ppermute | solution.py:415
  52.2 1.3 %collective-permute-start.4 = (bf16[128,256]{1,0:T(8,128)(2,1)S(1)}, bf16[128,256]{1,0:T(8,128)(2,1)S(1)}, u32[]{:S(2)}, u32[]{:S(2)}) collective-permute-start(bf16[128,256]{1,0:T(8,128)(2,1)S(1)} %collective-permute-done.3.col1), channel_id=1, source_target_pairs={{128,256},{160,288},{192,320},{224,352},{256,384},{288,416},{320,4... | collective-permute-start | bytes 196616 | tf_op jit(solution)/shard_map/ppermute | solution.py:415
  53.5 1.9 %collective-permute-start.1 = (bf16[512,128]{1,0:T(8,128)(2,1)S(1)}, bf16[512,128]{1,0:T(8,128)(2,1)S(1)}, u32[]{:S(2)}, u32[]{:S(2)}) collective-permute-start(bf16[512,128]{1,0:T(8,128)(2,1)S(1)} %get-tuple-element.17.qm), channel_id=1, source_target_pairs={{0,64},{32,96},{64,0},{96,32},{128,192},{160,224},{192,128},{224,1... | collective-permute-start | bytes 393224 | tf_op jit(solution)/shard_map/ppermute | solution.py:412
  55.5 1.9 %collective-permute-start.2 = (bf16[128,128]{1,0:T(8,128)(2,1)S(1)}, bf16[128,128]{1,0:T(8,128)(2,1)S(1)}, u32[]{:S(2)}, u32[]{:S(2)}) collective-permute-start(bf16[128,128]{1,0:T(8,128)(2,1)S(1)} %get-tuple-element.21), channel_id=1, source_target_pairs={{0,96},{32,64},{64,32},{96,0},{128,224},{160,192},{192,160},{224,1... | collective-permute-start | bytes 98312 | tf_op jit(solution)/shard_map/ppermute | solution.py:412
  57.4 7.4 %collective-permute-done.4.col2 = bf16[128,256]{1,0:T(8,128)(2,1)S(1)} collective-permute-done((bf16[128,256]{1,0:T(8,128)(2,1)S(1)}, bf16[128,256]{1,0:T(8,128)(2,1)S(1)}, u32[]{:S(2)}, u32[]{:S(2)}) %collective-permute-start.4) | collective-permute-done | bytes 65568 | tf_op jit(solution)/shard_map/ppermute | solution.py:415
  64.8 1.3 %collective-permute-start.5 = (bf16[128,256]{1,0:T(8,128)(2,1)S(1)}, bf16[128,256]{1,0:T(8,128)(2,1)S(1)}, u32[]{:S(2)}, u32[]{:S(2)}) collective-permute-start(bf16[128,256]{1,0:T(8,128)(2,1)S(1)} %collective-permute-done.4.col2), channel_id=1, source_target_pairs={{256,384},{288,416},{320,448},{352,480},{257,385},{289,417},{321,4... | collective-permute-start | bytes 196616 | tf_op jit(solution)/shard_map/ppermute | solution.py:415
  66.1 5.9 %shard_map.78 = (bf16[2048,128]{1,0:T(8,128)(2,1)S(1)}, f32[512,128]{1,0:T(8,128)S(1)}, f32[512,128]{1,0:T(8,128)S(1)}, f32[512,128]{1,0:T(8,128)S(1)}) custom-call(bf16[3,2048,128]{2,1,0:T(8,128)(2,1)S(1)} %bitcast.2, bf16[512,128]{1,0:T(8,128)(2,1)S(1)} %get-tuple-element.17.qm, bf16[512,256]{1,0:T(8,128)(2,1)S(1)} %get-tuple-element.18.kvm), custom_call_target="tpu_custom_call" | custom-call | flops 2000000000 | bytes 3000000 | tf_op jit(solution)/shard_map/pallas_call | solution.py:38
  72.0 1.8 %collective-permute-done.5.col3 = bf16[128,256]{1,0:T(8,128)(2,1)S(1)} collective-permute-done((bf16[128,256]{1,0:T(8,128)(2,1)S(1)}, bf16[128,256]{1,0:T(8,128)(2,1)S(1)}, u32[]{:S(2)}, u32[]{:S(2)}) %collective-permute-start.5) | collective-permute-done | bytes 65568 | tf_op jit(solution)/shard_map/ppermute | solution.py:415
  73.8 8.0 %shard_map.79 = (f32[512,128]{1,0:T(8,128)S(1)}, f32[512,128]{1,0:T(8,128)S(1)}, f32[512,128]{1,0:T(8,128)S(1)}, bf16[144,128]{1,0:T(8,128)(2,1)S(1)}, bf16[544,...) custom-call(bf16[512,128]{1,0:T(8,128)(2,1)S(1)} %get-tuple-element.17.qm, bf16[512,256]{1,0:T(8,128)(2,1)S(1)} %get-tuple-element.18.kvm, ...), custom_call_target="tpu_custom_call" | custom-call | flops 1000000000 | bytes 4000000 | tf_op jit(solution)/shard_map/pallas_call | solution.py:38
  81.8 1.9 %collective-permute-start.7 = (bf16[544,128]{1,0:T(8,128)(2,1)S(1)}, bf16[544,128]{1,0:T(8,128)(2,1)S(1)}, u32[]{:S(2)}, u32[]{:S(2)}) collective-permute-start(bf16[544,128]{1,0:T(8,128)(2,1)S(1)} %get-tuple-element.30), channel_id=1, source_target_pairs={{0,64},{32,96},{64,0},{96,32},{128,192},{160,224},{192,128},{224,1... | collective-permute-start | bytes 417800 | tf_op jit(solution)/shard_map/ppermute | solution.py:412
  83.7 4.0 %collective-permute-start.6 = (bf16[144,128]{1,0:T(8,128)(2,1)S(1)}, bf16[144,128]{1,0:T(8,128)(2,1)S(1)}, u32[]{:S(2)}, u32[]{:S(2)}) collective-permute-start(bf16[144,128]{1,0:T(8,128)(2,1)S(1)} %get-tuple-element.29), channel_id=1, source_target_pairs={{0,32},{32,0},{64,96},{96,64},{128,160},{160,128},{192,224},{224,1... | collective-permute-start | bytes 110600 | tf_op jit(solution)/shard_map/ppermute | solution.py:412
  87.8 4.0 %collective-permute-start.8 = (bf16[144,128]{1,0:T(8,128)(2,1)S(1)}, bf16[144,128]{1,0:T(8,128)(2,1)S(1)}, u32[]{:S(2)}, u32[]{:S(2)}) collective-permute-start(bf16[144,128]{1,0:T(8,128)(2,1)S(1)} %get-tuple-element.31), channel_id=1, source_target_pairs={{0,96},{32,64},{64,32},{96,0},{128,224},{160,192},{192,160},{224,1... | collective-permute-start | bytes 110600 | tf_op jit(solution)/shard_map/ppermute | solution.py:412
  91.8 1.1 %shard_map.83 = bf16[64,2,64]{2,1,0:T(2,128)(2,1)S(1)} custom-call(s32[32]{0:T(128)S(1)} %copy-done.4, bf16[16,80,128]{2,1,0:T(8,128)(2,1)S(1)} %all-to-all-done.1.got, bf16[1024,256]{1,0:T(8,128)(2,1)S(1)} %copy-done.2), custom_call_target="tpu_custom_call" | custom-call | flops 10000000 | bytes 1000000 | tf_op jit(solution)/shard_map/pallas_call | solution.py:38
  93.6 10.1 %all-to-all-start.2 = ((bf16[32,2,128]{2,1,0:T(2,128)(2,1)}), bf16[32,2,128]{2,1,0:T(2,128)(2,1)S(1)}, u32[]{:S(2)}, u32[]{:S(2)}) async-start(bf16[32,2,128]{2,1,0:T(2,128)(2,1)} %reshape.4), calls=%async_computation.2 | async-start | bytes 32768 | tf_op jit(solution)/shard_map/all_to_all | solution.py:465
  103.8 2.1 %shard_map.80 = bf16[2048,128]{1,0:T(8,128)(2,1)} custom-call(bf16[2048,128]{1,0:T(8,128)(2,1)S(1)} %get-tuple-element.19.near_o, f32[512,128]{1,0:T(8,128)S(1)} %get-tuple-element.26.acc, f32[512,128]{1,0:T(8,128)S(1)} %get-tuple-element.27.m, f32[512,128]{1,0:T(8,128)S(1)} %get-tuple-element.28.l, bf16[144,128]{1,0:T(8,128)(2,1)S(1)} %collective-permute-done.6.back1, ...), custom_call_target="tpu_custom_call" | custom-call | flops 100000000 | bytes 4000000 | tf_op jit(solution)/shard_map/pallas_call | solution.py:38
  105.9 4.8 %all-to-all-done.2 = bf16[32,2,128]{2,1,0:T(2,128)(2,1)S(1)} async-done(((bf16[32,2,128]{2,1,0:T(2,128)(2,1)}), bf16[32,2,128]{2,1,0:T(2,128)(2,1)S(1)}, u32[]{:S(2)}, u32[]{:S(2)}) %all-to-all-start.2) | async-done | bytes 16416 | tf_op jit(solution)/shard_map/all_to_all | solution.py:465
  110.8 1.5 %shard_map.84 = bf16[16,2,64]{2,1,0:T(2,128)(2,1)} custom-call(s32[32]{0:T(128)S(1)} %copy-done.4, bf16[64,2,64]{2,1,0:T(2,128)(2,1)S(1)} %reshape.5.got), custom_call_target="tpu_custom_call" | custom-call | bytes 100000 | tf_op jit(solution)/shard_map/pallas_call | solution.py:38
  (21 shorter events, 2.8 us)
Async XLA Ops:
  0.6 28.5 %copy-start = (bf16[2048,3,128]{2,0,1:T(8,128)(2,1)S(1)}, bf16[2048,3,128]{2,0,1:T(8,128)(2,1)}, u32[]{:S(2)}) copy-start(bf16[2048,3,128]{2,0,1:T(8,128)(2,1)} %param.6) | copy-start | bytes 4718596
  14.3 1.2 %copy-start.1 = (bf16[4,2,64,1024]{3,2,1,0:T(8,128)(2,1)S(1)}, bf16[4,2,64,1024]{3,2,1,0:T(8,128)(2,1)}, u32[]{:S(2)}) copy-start(bf16[4,2,64,1024]{3,2,1,0:T(8,128)(2,1)} %cache.1) | copy-start | bytes 3145732
  15.6 0.7 copy-start.3
  16.2 0.7 copy-start.5
  19.4 72.3 %all-to-all-start.1 = ((bf16[16,80,128]{2,1,0:T(8,128)(2,1)}), bf16[16,80,128]{2,1,0:T(8,128)(2,1)S(1)}, u32[]{:S(2)}, u32[]{:S(2)}) async-start(bf16[16,80,128]{2,1,0:T(8,128)(2,1)} %shard_map.82), calls=%async_computation.1 | async-start | bytes 655360 | tf_op jit(solution)/shard_map/all_to_all | solution.py:430
  29.7 22.5 %collective-permute-start.3 = (bf16[128,256]{1,0:T(8,128)(2,1)S(1)}, bf16[128,256]{1,0:T(8,128)(2,1)S(1)}, u32[]{:S(2)}, u32[]{:S(2)}) collective-permute-start(bf16[128,256]{1,0:T(8,128)(2,1)S(1)} %get-tuple-element.22), channel_id=1, source_target_pairs={{0,128},{32,160},{64,192},{96,224},{128,256},{160,288},{192,320},{... | collective-permute-start | bytes 196616 | tf_op jit(solution)/shard_map/ppermute | solution.py:415
  31.0 42.8 %collective-permute-start = (bf16[576,256]{1,0:T(8,128)(2,1)S(1)}, bf16[576,256]{1,0:T(8,128)(2,1)S(1)}, u32[]{:S(2)}, u32[]{:S(2)}) collective-permute-start(bf16[576,256]{1,0:T(8,128)(2,1)S(1)} %get-tuple-element.20), channel_id=1, source_target_pairs={{0,32},{32,0},{64,96},{96,64},{128,160},{160,128},{192,224},{224,1... | collective-permute-start | bytes 884744 | tf_op jit(solution)/shard_map/ppermute | solution.py:412
  52.2 12.6 %collective-permute-start.4 = (bf16[128,256]{1,0:T(8,128)(2,1)S(1)}, bf16[128,256]{1,0:T(8,128)(2,1)S(1)}, u32[]{:S(2)}, u32[]{:S(2)}) collective-permute-start(bf16[128,256]{1,0:T(8,128)(2,1)S(1)} %collective-permute-done.3.col1), channel_id=1, source_target_pairs={{128,256},{160,288},{192,320},{224,352},{256,384},{288,416},{320,4... | collective-permute-start | bytes 196616 | tf_op jit(solution)/shard_map/ppermute | solution.py:415
  53.5 18.5 %collective-permute-start.1 = (bf16[512,128]{1,0:T(8,128)(2,1)S(1)}, bf16[512,128]{1,0:T(8,128)(2,1)S(1)}, u32[]{:S(2)}, u32[]{:S(2)}) collective-permute-start(bf16[512,128]{1,0:T(8,128)(2,1)S(1)} %get-tuple-element.17.qm), channel_id=1, source_target_pairs={{0,64},{32,96},{64,0},{96,32},{128,192},{160,224},{192,128},{224,1... | collective-permute-start | bytes 393224 | tf_op jit(solution)/shard_map/ppermute | solution.py:412
  55.5 16.6 %collective-permute-start.2 = (bf16[128,128]{1,0:T(8,128)(2,1)S(1)}, bf16[128,128]{1,0:T(8,128)(2,1)S(1)}, u32[]{:S(2)}, u32[]{:S(2)}) collective-permute-start(bf16[128,128]{1,0:T(8,128)(2,1)S(1)} %get-tuple-element.21), channel_id=1, source_target_pairs={{0,96},{32,64},{64,32},{96,0},{128,224},{160,192},{192,160},{224,1... | collective-permute-start | bytes 98312 | tf_op jit(solution)/shard_map/ppermute | solution.py:412
  64.8 9.0 %collective-permute-start.5 = (bf16[128,256]{1,0:T(8,128)(2,1)S(1)}, bf16[128,256]{1,0:T(8,128)(2,1)S(1)}, u32[]{:S(2)}, u32[]{:S(2)}) collective-permute-start(bf16[128,256]{1,0:T(8,128)(2,1)S(1)} %collective-permute-done.4.col2), channel_id=1, source_target_pairs={{256,384},{288,416},{320,448},{352,480},{257,385},{289,417},{321,4... | collective-permute-start | bytes 196616 | tf_op jit(solution)/shard_map/ppermute | solution.py:415
  73.8 18.0 %copy-start.2 = (bf16[1024,256]{1,0:T(8,128)(2,1)S(1)}, bf16[1024,256]{1,0:T(8,128)(2,1)}, u32[]{:S(2)}) copy-start(bf16[1024,256]{1,0:T(8,128)(2,1)} %weight.1) | copy-start | bytes 1572868
  73.8 18.0 %copy-start.4 = (s32[32]{0:T(128)S(1)}, s32[32]{0:T(128)}, u32[]{:S(2)}) copy-start(s32[32]{0:T(128)} %own.7) | copy-start | bytes 388
  81.8 22.0 %collective-permute-start.7 = (bf16[544,128]{1,0:T(8,128)(2,1)S(1)}, bf16[544,128]{1,0:T(8,128)(2,1)S(1)}, u32[]{:S(2)}, u32[]{:S(2)}) collective-permute-start(bf16[544,128]{1,0:T(8,128)(2,1)S(1)} %get-tuple-element.30), channel_id=1, source_target_pairs={{0,64},{32,96},{64,0},{96,32},{128,192},{160,224},{192,128},{224,1... | collective-permute-start | bytes 417800 | tf_op jit(solution)/shard_map/ppermute | solution.py:412
  83.7 20.0 %collective-permute-start.6 = (bf16[144,128]{1,0:T(8,128)(2,1)S(1)}, bf16[144,128]{1,0:T(8,128)(2,1)S(1)}, u32[]{:S(2)}, u32[]{:S(2)}) collective-permute-start(bf16[144,128]{1,0:T(8,128)(2,1)S(1)} %get-tuple-element.29), channel_id=1, source_target_pairs={{0,32},{32,0},{64,96},{96,64},{128,160},{160,128},{192,224},{224,1... | collective-permute-start | bytes 110600 | tf_op jit(solution)/shard_map/ppermute | solution.py:412
  87.8 16.0 %collective-permute-start.8 = (bf16[144,128]{1,0:T(8,128)(2,1)S(1)}, bf16[144,128]{1,0:T(8,128)(2,1)S(1)}, u32[]{:S(2)}, u32[]{:S(2)}) collective-permute-start(bf16[144,128]{1,0:T(8,128)(2,1)S(1)} %get-tuple-element.31), channel_id=1, source_target_pairs={{0,96},{32,64},{64,32},{96,0},{128,224},{160,192},{192,160},{224,1... | collective-permute-start | bytes 110600 | tf_op jit(solution)/shard_map/ppermute | solution.py:412
  93.6 17.1 %all-to-all-start.2 = ((bf16[32,2,128]{2,1,0:T(2,128)(2,1)}), bf16[32,2,128]{2,1,0:T(2,128)(2,1)S(1)}, u32[]{:S(2)}, u32[]{:S(2)}) async-start(bf16[32,2,128]{2,1,0:T(2,128)(2,1)} %reshape.4), calls=%async_computation.2 | async-start | bytes 32768 | tf_op jit(solution)/shard_map/all_to_all | solution.py:465

commit v3 on v2

--- a/solution.py
+++ b/solution.py
@@ -21,6 +21,14 @@
     return pl.BlockSpec(memory_space=pltpu.VMEM)
 
 
+def far_memory(x):
+    return pltpu.with_memory_space_constraint(x, pltpu.HBM)
+
+
+def hspec():
+    return pl.BlockSpec(memory_space=pltpu.HBM)
+
+
 def sspec():
     return pl.BlockSpec(memory_space=pltpu.SMEM)
 
@@ -33,13 +41,13 @@
     return lax.dot_general(a, b, (((1,), (0,)), ((), ())), preferred_element_type=F32)
 
 
-def call(body, out_shape, ins, specs, scratch=(), vmem=24, flops=0, nbytes=0, trans=0):
+def call(body, out_shape, ins, specs, scratch=(), vmem=24, flops=0, nbytes=0, trans=0, outs=None):
     single = not isinstance(out_shape, (tuple, list))
     return pl.pallas_call(
         body,
         out_shape=out_shape,
         in_specs=specs,
-        out_specs=vspec() if single else tuple(vspec() for _ in out_shape),
+        out_specs=vspec() if single else tuple(outs or [vspec() for _ in out_shape]),
         scratch_shapes=list(scratch),
         compiler_params=pltpu.CompilerParams(vmem_limit_bytes=vmem * 1024 * 1024),
         cost_estimate=pl.CostEstimate(flops=flops, bytes_accessed=nbytes, transcendentals=trans),
@@ -65,8 +73,14 @@
     return grp, rank
 
 
-def route_kernel(own, dec, out, sem):
+def start_kernel(own, dec, qkv, sent, qm, kvm, ask, msg, far, raw, wide, sem, part_sem):
     me = lax.axis_index("req")
+    rows = qkv.shape[1]
+    parts = []
+    for part in range(3):
+        cp = pltpu.make_async_copy(qkv.at[part], raw.at[part], part_sem.at[part])
+        cp.start()
+        parts.append(cp)
     copies = []
     for b in range(8):
         src = [jnp.int32(0), jnp.int32(0)]
@@ -75,19 +89,14 @@
             grp, rank = rank_in_block(own, 4 * b, k)
             mine = grp == me
             for r in range(2):
-                src[r] = jnp.where(mine & (rank == r), lax.rem(slot, 16), src[r])
+                src[r] = jnp.where(mine & (rank == r), slot & 15, src[r])
         for r in range(2):
-            cp = pltpu.make_async_copy(dec.at[src[r]], out.at[2 * b + r], sem.at[2 * b + r])
+            cp = pltpu.make_async_copy(dec.at[src[r]], sent.at[2 * b + r], sem.at[2 * b + r])
             cp.start()
             copies.append(cp)
-    for cp in copies:
-        cp.wait()
-
-
-def pick_kernel(qkv, qm, kvm, ask, msg, far, wide):
-    rows = qkv.shape[1]
     for part in range(3):
-        wide[...] = qkv[part].astype(F32)
+        parts[part].wait()
+        wide[...] = raw[part].astype(F32)
         for c in range(4):
             start = class_residue(c)
             got = wide[pl.ds(start, rows // 16, stride=16), :].astype(BF16)
@@ -104,6 +113,8 @@
                 msg[at, lanes] = got
                 if c == 0:
                     far[:, lanes] = got
+    for cp in copies:
+        cp.wait()
 
 
 def softmax_step(m, l, acc, s, v, mult=None):
@@ -117,31 +128,48 @@
     return m_new, l_new, acc_new
 
 
-def near_kernel(qkv, qm, kvm, near_o, acc_o, m_o, l_o, acc_s, m_s, l_s):
+def both(m, l):
+    count = m.shape[0]
+    lane = lax.broadcasted_iota(jnp.int32, (count, HD), 1)
+    return jnp.where(lane == 0, m, l)
+
+
+def near_kernel(
+    qkv, qm, kvm, near_h, acc_h, ml_h, raw, acc_s, ml_s, near_o, acc_o, ml_o, sem, out_sem
+):
     rows = qkv.shape[1]
     step = 256
+    copies = []
+    for b in range(rows // step):
+        at = pl.ds(step * b, step)
+        cp = pltpu.make_async_copy(qkv.at[:, at, :], raw.at[:, at, :], sem.at[b])
+        cp.start()
+        copies.append(cp)
     tri = lax.broadcasted_iota(jnp.int32, (step, step), 1) <= lax.broadcasted_iota(
         jnp.int32, (step, step), 0
     )
     for b in range(rows // step):
         at = pl.ds(step * b, step)
-        q = qkv[0, at, :]
-        s_d = jnp.where(tri, dot_t(q, qkv[1, at, :]), NEG)
+        copies[b].wait()
+        q = raw[0, at, :]
+        s_d = jnp.where(tri, dot_t(q, raw[1, at, :]), NEG)
         m = jnp.max(s_d, axis=1, keepdims=True)
         if b:
-            s_f = dot_t(q, qkv[1, pl.ds(0, step * b), :])
+            s_f = dot_t(q, raw[1, pl.ds(0, step * b), :])
             m = jnp.maximum(m, jnp.max(s_f, axis=1, keepdims=True))
         p_d = jnp.exp2((s_d - m) * EXP_SCALE)
         l = jnp.sum(p_d, axis=1, keepdims=True)
-        acc = dot_n(p_d.astype(BF16), qkv[2, at, :])
+        acc = dot_n(p_d.astype(BF16), raw[2, at, :])
         if b:
             p_f = jnp.exp2((s_f - m) * EXP_SCALE)
             l = l + jnp.sum(p_f, axis=1, keepdims=True)
-            acc = acc + dot_n(p_f.astype(BF16), qkv[2, pl.ds(0, step * b), :])
+            acc = acc + dot_n(p_f.astype(BF16), raw[2, pl.ds(0, step * b), :])
         near_o[at, :] = (acc / l).astype(BF16)
+        cp = pltpu.make_async_copy(near_o.at[at], near_h.at[at], out_sem.at[b])
+        cp.start()
+        copies.append(cp)
         acc_s[at, :] = acc
-        m_s[at, :] = jnp.broadcast_to(m, (step, HD))
-        l_s[at, :] = jnp.broadcast_to(l, (step, HD))
+        ml_s[at, :] = both(m, l)
     inner = lax.div(lax.rem(head_id(), 16), 4)
 
     def order(shape, dim):
@@ -158,12 +186,18 @@
         mult = None
         if c == 0:
             mult = jnp.where(lax.broadcasted_iota(jnp.int32, (1, 512), 1) < 128, 2.0, 1.0)
+        ml = ml_s[pick, :]
         m, l, acc = softmax_step(
-            m_s[pick, :][:, :1], l_s[pick, :][:, :1], acc_s[pick, :], s, kvm[:, pl.ds(HD, HD)], mult
+            ml[:, 0:1], ml[:, 1:2], acc_s[pick, :], s, kvm[:, pl.ds(HD, HD)], mult
         )
         acc_o[at, :] = acc
-        m_o[at, :] = jnp.broadcast_to(m, (128, HD))
-        l_o[at, :] = jnp.broadcast_to(l, (128, HD))
+        ml_o[at, :] = both(m, l)
+    for i, (src, dst) in enumerate(((acc_o, acc_h), (ml_o, ml_h))):
+        cp = pltpu.make_async_copy(src, dst, sem.at[i])
+        cp.start()
+        copies.append(cp)
+    for cp in copies[rows // step :]:
+        cp.wait()
 
 
 def pack(rows_m, rows_l):
@@ -187,18 +221,20 @@
 
 
 def share_kernel(
-    qm, kvm, got1, got2, got3, col1, col2, col3, acc_i, m_i, l_i,
-    acc_o, m_o, l_o, back1, back2, back3, acc_s, m_s, l_s,
+    qm, kvm, got1, got2, got3, col1, col2, col3, acc_i, ml_i,
+    acc_o, ml_o, back1, back2, back3, acc_s, ml_s, sem,
 ):
     z = lax.axis_index("seq")
     local = lax.rem(z, 4)
     group = lax.div(z, 4)
-    acc_s[pl.ds(0, 512), :] = acc_i[...]
-    m_s[pl.ds(0, 512), :] = m_i[...]
-    l_s[pl.ds(0, 512), :] = l_i[...]
-    acc_s[pl.ds(512, 768), :] = jnp.zeros((768, HD), F32)
-    m_s[pl.ds(512, 768), :] = jnp.full((768, HD), NEG, F32)
-    l_s[pl.ds(512, 768), :] = jnp.zeros((768, HD), F32)
+    one = pl.ds(0, 512)
+    load_acc = pltpu.make_async_copy(acc_i, acc_s.at[one], sem.at[0])
+    load_ml = pltpu.make_async_copy(ml_i, ml_s.at[one], sem.at[1])
+    load_acc.start()
+    load_ml.start()
+    rest = pl.ds(512, 768)
+    acc_s[rest, :] = jnp.zeros((768, HD), F32)
+    ml_s[rest, :] = both(jnp.full((768, 1), NEG, F32), jnp.zeros((768, 1), F32))
 
     def update(first, q, keys, values, twice=False):
         count = q.shape[0]
@@ -213,25 +249,25 @@
                 2.0,
                 1.0,
             )
-        m, l, acc = softmax_step(
-            m_s[at, :][:, :1], l_s[at, :][:, :1], acc_s[at, :], s, values, mult
-        )
+        ml = ml_s[at, :]
+        m, l, acc = softmax_step(ml[:, 0:1], ml[:, 1:2], acc_s[at, :], s, values, mult)
         acc_s[at, :] = acc
-        m_s[at, :] = jnp.broadcast_to(m, (count, HD))
-        l_s[at, :] = jnp.broadcast_to(l, (count, HD))
+        ml_s[at, :] = both(m, l)
 
     own_k, own_v = kvm[:, pl.ds(0, HD)], kvm[:, pl.ds(HD, HD)]
-    one = pl.ds(0, 512)
     one_k, one_v = got1[one, pl.ds(0, HD)], got1[one, pl.ds(HD, HD)]
-
-    @pl.when((local & 1) == 1)
-    def _():
-        update(0, qm[...], one_k, one_v, True)
 
     @pl.when(local < 2)
     def _():
         update(512, got2[...], own_k, own_v, True)
         update(512, got2[...], one_k, one_v, True)
+
+    load_acc.wait()
+    load_ml.wait()
+
+    @pl.when((local & 1) == 1)
+    def _():
+        update(0, qm[...], one_k, one_v, True)
 
     half = pl.ds(512, 64)
     head = pl.ds(0, 128)
@@ -248,22 +284,34 @@
             )
             update(1024, near_q, k, v)
 
-    acc_o[...] = acc_s[one, :]
-    m_o[...] = m_s[one, :]
-    l_o[...] = l_s[one, :]
+    save_acc = pltpu.make_async_copy(acc_s.at[one], acc_o, sem.at[0])
+    save_ml = pltpu.make_async_copy(ml_s.at[one], ml_o, sem.at[1])
+    save_acc.start()
+    save_ml.start()
     for out, first, count in ((back2, 512, 512), (back1, 1024, 128), (back3, 1152, 128)):
         at = pl.ds(first, count)
-        l = l_s[at, :]
+        ml = ml_s[at, :]
+        m, l = ml[:, 0:1], ml[:, 1:2]
         out[pl.ds(0, count), :] = (acc_s[at, :] / jnp.where(l > 0.0, l, 1.0)).astype(BF16)
-        packed = pack(m_s[at, :], l)
+        packed = pack(m, l)
         out[pl.ds(count, packed.shape[0]), :] = packed
-
-
-def merge_kernel(near_o, acc, m, l, back1, back2, back3, out, wide):
-    wide[...] = near_o[...].astype(F32)
+    save_acc.wait()
+    save_ml.wait()
+
+
+def merge_kernel(near_h, acc_h, ml_h, back1, back2, back3, out, near, acc, ml, wide, sem):
+    copies = [
+        pltpu.make_async_copy(src, dst, sem.at[i])
+        for i, (src, dst) in enumerate(((near_h, near), (acc_h, acc), (ml_h, ml)))
+    ]
+    for cp in copies:
+        cp.start()
+    for cp in copies:
+        cp.wait()
+    wide[...] = near[...].astype(F32)
     for c in range(4):
         at = pl.ds(128 * c, 128)
-        terms = [(m[at, :][:, :1], l[at, :][:, :1], acc[at, :])]
+        terms = [(ml[at, :][:, 0:1], ml[at, :][:, 1:2], acc[at, :])]
         for part, rows, stat in ((back2, 128 * c, 512 + 8 * c), (back1, 0, 128), (back3, 0, 128)):
             if c and part is not back2:
                 continue
@@ -287,7 +335,12 @@
     return hi, mid, (rest - mid).astype(BF16).astype(F32)
 
 
-def cache_kernel(own, lens, arr, cache, out, o_s, st_s):
+def cache_kernel(own, lens, arr, cache_h, out, cache, o_s, st_s, sem):
+    copies = []
+    for k in range(4):
+        cp = pltpu.make_async_copy(cache_h.at[k], cache.at[k], sem.at[k])
+        cp.start()
+        copies.append(cp)
     z = lax.axis_index("seq")
     me = lax.axis_index("req")
     per = cache.shape[2]
@@ -310,6 +363,7 @@
         kn = jnp.concatenate([arr[row, 1].astype(F32), pad], axis=0).astype(BF16)
         vn = jnp.concatenate([arr[row, 2].astype(F32), pad], axis=0).astype(BF16)
         c_ok = col < lens[4 * me + k]
+        copies[k].wait()
         s_c = jnp.where(c_ok, dot_t(qd, cache[k, 0]), NEG)
         s_n = jnp.where(new_ok, dot_t(qd, kn), NEG)
         m = jnp.maximum(
@@ -356,26 +410,37 @@
     rows = jnp.concatenate([total[8 * h : 8 * h + 8] for h in range(8)], axis=1)
     y = dot_n(rows.astype(BF16), weight[...])
     out[...] = jnp.zeros(out.shape, BF16)
-    for k in range(4):
-        grp, rank = rank_in_block(own, 4 * me, k)
-        for h in range(4):
-            out[16 * h + 2 * grp + rank] = y[2 * k : 2 * k + 2, 64 * h : 64 * h + 64].astype(BF16)
+    seats = [rank_in_block(own, 4 * me, k) for k in range(4)]
+    for h in range(4):
+        cols = slice(64 * h, 64 * h + 64)
+        lines = [
+            jnp.concatenate([y[2 * k : 2 * k + 1, cols], y[2 * k + 1 : 2 * k + 2, cols]], axis=1)
+            for k in range(4)
+        ]
+        for grp, _ in seats:
+            pair = [jnp.zeros((1, HD), F32)] * 2
+            for (other, rank), line in zip(seats, lines):
+                for r in range(2):
+                    pair[r] = jnp.where((other == grp) & (rank == r), line, pair[r])
+            out[8 * h + grp] = jnp.concatenate(pair, axis=0).astype(BF16)
 
 
 def settle_kernel(own, got, out):
     me = lax.axis_index("req")
+    total = got[pl.ds(0, 8)].astype(F32)
+    for h in range(1, 4):
+        total = total + got[pl.ds(8 * h, 8)].astype(F32)
     out[...] = jnp.zeros(out.shape, BF16)
     for b in range(8):
+        first = total[b]
         for k in range(4):
             slot = own[4 * b + k]
             grp, rank = rank_in_block(own, 4 * b, k)
 
             @pl.when(grp == me)
-            def _(b=b, slot=slot, rank=rank):
-                total = got[2 * b + rank].astype(F32)
-                for h in range(1, 4):
-                    total = total + got[16 * h + 2 * b + rank].astype(F32)
-                out[lax.rem(slot, 16)] = total.astype(BF16)
+            def _(first=first, slot=slot, rank=rank):
+                row = jnp.where(rank == 0, first[0:1], first[1:2])
+                out[slot & 15] = jnp.concatenate([row[:, :64], row[:, 64:]], axis=0).astype(BF16)
 
 
 def shape(dims, dtype=BF16):
@@ -384,29 +449,27 @@
 
 def staged(pre_qkv, cache_kv, dec_new, out_weight, owner_slot, prompt_lengths):
     qkv = jnp.swapaxes(pre_qkv, 0, 1)
-    sent = pl.pallas_call(
-        route_kernel,
-        out_shape=shape(dec_new.shape),
-        in_specs=[sspec(), pl.BlockSpec(memory_space=pl.ANY)],
-        out_specs=vspec(),
-        scratch_shapes=[pltpu.SemaphoreType.DMA((16,))],
-        cost_estimate=pl.CostEstimate(flops=0, bytes_accessed=400000, transcendentals=0),
-    )(owner_slot, dec_new)
-    arrived = lax.all_to_all(sent, "req", 0, 0, tiled=True)
-    qm, kvm, ask, msg, far = call(
-        pick_kernel,
+    sent, qm, kvm, ask, msg, far = call(
+        start_kernel,
         (
+            shape(dec_new.shape),
             shape((512, HD)),
             shape((512, 2 * HD)),
             shape((128, HD)),
             shape((576, 2 * HD)),
             shape((128, 2 * HD)),
         ),
-        (qkv,),
-        [vspec()],
-        [VMEM((2048, HD), F32)],
+        (owner_slot, far_memory(dec_new), far_memory(qkv)),
+        [sspec(), hspec(), hspec()],
+        [
+            VMEM((3, 2048, HD), BF16),
+            VMEM((2048, HD), F32),
+            pltpu.SemaphoreType.DMA((16,)),
+            pltpu.SemaphoreType.DMA((3,)),
+        ],
         nbytes=4000000,
     )
+    arrived = lax.all_to_all(sent, "req", 0, 0, tiled=True)
 
     def swap(x, bits):
         return lax.ppermute(x, "seq", [(i, i ^ bits) for i in range(16)])
@@ -415,48 +478,64 @@
         return lax.ppermute(x, "seq", [(i, i + 4) for i in range(first, 12)])
 
     col1 = relay(far, 0)
+    got3 = swap(ask, 3)
+    got2 = swap(qm, 2)
     got1 = swap(msg, 1)
-    got2 = swap(qm, 2)
-    got3 = swap(ask, 3)
     partial = call(
         cache_kernel,
         shape((16, 80, HD)),
-        (owner_slot, prompt_lengths, arrived, cache_kv),
-        [sspec(), sspec(), vspec(), vspec()],
-        [VMEM((64, HD), F32), VMEM((64, HD), F32)],
+        (owner_slot, prompt_lengths, arrived, far_memory(cache_kv)),
+        [sspec(), sspec(), vspec(), hspec()],
+        [
+            VMEM(cache_kv.shape, BF16),
+            VMEM((64, HD), F32),
+            VMEM((64, HD), F32),
+            pltpu.SemaphoreType.DMA((4,)),
+        ],
         flops=10**8,
         nbytes=2000000,
     )
     parts = lax.all_to_all(partial, "seq", 0, 0, tiled=True)
     col2 = relay(col1, 4)
-    state = [shape((512, HD), F32)] * 3
-    near_o, acc, m, l = call(
+    state = [pltpu.HBM((512, HD), F32)] * 2
+    near_o, acc, ml = call(
         near_kernel,
-        (shape((2048, HD)), *state),
-        (qkv, qm, kvm),
-        [vspec()] * 3,
-        [VMEM((2048, HD), F32)] * 3,
+        (pltpu.HBM((2048, HD), BF16), *state),
+        (far_memory(qkv), qm, kvm),
+        [hspec(), vspec(), vspec()],
+        [
+            VMEM((3, 2048, HD), BF16),
+            VMEM((2048, HD), F32),
+            VMEM((2048, HD), F32),
+            VMEM((2048, HD), BF16),
+            VMEM((512, HD), F32),
+            VMEM((512, HD), F32),
+            pltpu.SemaphoreType.DMA((8,)),
+            pltpu.SemaphoreType.DMA((8,)),
+        ],
         flops=2 * 10**9,
         nbytes=3000000,
         trans=2 * 10**6,
+        outs=[hspec(), hspec(), hspec()],
     )
     col3 = relay(col2, 8)
-    acc, m, l, back1, back2, back3 = call(
+    acc, ml, back1, back2, back3 = call(
         share_kernel,
         (*state, shape((144, HD)), shape((544, HD)), shape((144, HD))),
-        (qm, kvm, got1, got2, got3, col1, col2, col3, acc, m, l),
-        [vspec()] * 11,
-        [VMEM((1280, HD), F32)] * 3,
+        (qm, kvm, got1, got2, got3, col1, col2, col3, far_memory(acc), far_memory(ml)),
+        [vspec()] * 8 + [hspec()] * 2,
+        [VMEM((1280, HD), F32)] * 2 + [pltpu.SemaphoreType.DMA((2,))],
         flops=10**9,
         nbytes=4000000,
         trans=10**6,
+        outs=[hspec()] * 2 + [vspec()] * 3,
     )
     back1 = swap(back1, 1)
+    back3 = swap(back3, 3)
     back2 = swap(back2, 2)
-    back3 = swap(back3, 3)
     answers = call(
         project_kernel,
-        shape((64, 2, 64)),
+        shape((32, 2, HD)),
         (owner_slot, parts, out_weight),
         [sspec(), vspec(), vspec()],
         flops=10**7,
@@ -466,9 +545,15 @@
     prefill_out = call(
         merge_kernel,
         shape((2048, HD)),
-        (near_o, acc, m, l, back1, back2, back3),
-        [vspec()] * 7,
-        [VMEM((2048, HD), F32)],
+        (far_memory(near_o), far_memory(acc), far_memory(ml), back1, back2, back3),
+        [hspec()] * 3 + [vspec()] * 3,
+        [
+            VMEM((2048, HD), BF16),
+            VMEM((512, HD), F32),
+            VMEM((512, HD), F32),
+            VMEM((2048, HD), F32),
+            pltpu.SemaphoreType.DMA((3,)),
+        ],
         flops=10**8,
         nbytes=4000000,
     )

time: 113 us -> 115 us (1.018)
  the two profiles are of different devices: /device:TPU:385 before, /device:TPU:257 now
where the time goes in v3:
time: 115 us; the launch traced here: 114 us
  starting transfers between devices  54.6 us (47%)
  Pallas kernels  29.7 us (26%)
  waiting for transfers between devices  17.8 us (15%)
  blocking collectives  10.6 us (9%)
    pallas_call x7, Pallas kernels, call(): pl.pallas_call(body, out_shape=out_shape, in_specs=specs, out_specs=vspec...  29.7 us
    ppermute x3, starting transfers between devices, relay(): return lax.ppermute(x, 'seq', [(i, i + 4) for i in range(first, 12)])  17.6 us
    ppermute x6, starting transfers between devices, swap(): return lax.ppermute(x, 'seq', [(i, i ^ bits) for i in range(16)])  15.4 us
    ppermute x3, waiting for transfers between devices, relay(): return lax.ppermute(x, 'seq', [(i, i + 4) for i in range(first, 12)])  14.1 us
    all_to_all x1, starting transfers between devices, staged(): parts = lax.all_to_all(partial, 'seq', 0, 0, tiled=True)  11.5 us
    all_to_all x1, blocking collectives, staged(): arrived = lax.all_to_all(sent, 'req', 0, 0, tiled=True)  10.6 us
    all_to_all x1, starting transfers between devices, staged(): results = lax.all_to_all(answers, ('head', 'req'), 0, 0, tiled=True)  10.1 us
    all_to_all x1, waiting for transfers between devices, staged(): results = lax.all_to_all(answers, ('head', 'req'), 0, 0, tiled=True)  3.74 us
  transfers between devices with their start and end apart: 11, of which 2 were waited for; matrix products, arithmetic and copies ran while one was open for 0% of the time, Pallas kernels for 19%

profile of v3, /device:TPU:257, one launch (start us, length us, event | category | flops | bytes accessed | tf_op | source)
XLA Modules:
  0.0 114.3 jit_solution(6909068895379202055)
XLA Ops:
  0.6 0.0 copy-start.1
  0.7 0.7 copy-done.1
  1.3 2.6 %shard_map.77 = (bf16[16,3,2,1024]{3,2,1,0:T(2,128)(2,1)S(1)}, bf16[512,128]{1,0:T(8,128)(2,1)S(1)}, bf16[512,256]{1,0:T(8,128)(2,1)S(1)}, bf16[128,128]{1,0:T(8...) custom-call(s32[32]{0:T(128)S(1)} %copy-done.1, bf16[16,3,2,1024]{3,2,1,0:T(2,128)(2,1)} %dec.1, ...), custom_call_target="tpu_custom_call" | custom-call | bytes 4000000 | tf_op jit(solution)/shard_map/pallas_call | solution.py:46
  4.0 10.6 %all_to_all.15.arr = bf16[16,3,2,1024]{3,2,1,0:T(2,128)(2,1)S(1)} all-to-all(bf16[16,3,2,1024]{3,2,1,0:T(2,128)(2,1)S(1)} %get-tuple-element.29), channel_id=1, replica_groups=mesh['seq'=16,'head'=4,'req'=8] {'req'}, dimensions={0} | all-to-all | bytes 393216 | tf_op jit(solution)/shard_map/all_to_all | solution.py:472
  14.6 4.0 %shard_map.81 = bf16[16,80,128]{2,1,0:T(8,128)(2,1)} custom-call(s32[32]{0:T(128)S(1)} %copy-done.1, s32[32]{0:T(128)S(1)} %copy-done.3, bf16[16,3,2,1024]{3,2,1,0:T(2,128)(2,1)S(1)} %all_to_all.15.arr, bf16[4,2,64,1024]{3,2,1,0:T(8,128)(2,1)} %cache_h.1), custom_call_target="tpu_custom_call" | custom-call | flops 100000000 | bytes 2000000 | tf_op jit(solution)/shard_map/pallas_call | solution.py:46
  18.6 11.5 %all-to-all-start.1 = ((bf16[16,80,128]{2,1,0:T(8,128)(2,1)}), bf16[16,80,128]{2,1,0:T(8,128)(2,1)S(1)}, u32[]{:S(2)}, u32[]{:S(2)}) async-start(bf16[16,80,128]{2,1,0:T(8,128)(2,1)} %shard_map.81), calls=%async_computation.1 | async-start | bytes 655360 | tf_op jit(solution)/shard_map/all_to_all | solution.py:498
  30.1 2.2 %collective-permute-start.3 = (bf16[128,256]{1,0:T(8,128)(2,1)S(1)}, bf16[128,256]{1,0:T(8,128)(2,1)S(1)}, u32[]{:S(2)}, u32[]{:S(2)}) collective-permute-start(bf16[128,256]{1,0:T(8,128)(2,1)S(1)} %get-tuple-element.21), channel_id=1, source_target_pairs={{0,128},{32,160},{64,192},{96,224},{128,256},{160,288},{192,320},{... | collective-permute-start | bytes 196616 | tf_op jit(solution)/shard_map/ppermute | solution.py:478
  32.3 2.2 %collective-permute-start = (bf16[576,256]{1,0:T(8,128)(2,1)S(1)}, bf16[576,256]{1,0:T(8,128)(2,1)S(1)}, u32[]{:S(2)}, u32[]{:S(2)}) collective-permute-start(bf16[576,256]{1,0:T(8,128)(2,1)S(1)} %get-tuple-element.19), channel_id=1, source_target_pairs={{0,32},{32,0},{64,96},{96,64},{128,160},{160,128},{192,224},{224,1... | collective-permute-start | bytes 884744 | tf_op jit(solution)/shard_map/ppermute | solution.py:475
  34.5 14.1 %collective-permute-done.3.col1 = bf16[128,256]{1,0:T(8,128)(2,1)S(1)} collective-permute-done((bf16[128,256]{1,0:T(8,128)(2,1)S(1)}, bf16[128,256]{1,0:T(8,128)(2,1)S(1)}, u32[]{:S(2)}, u32[]{:S(2)}) %collective-permute-start.3) | collective-permute-done | bytes 65568 | tf_op jit(solution)/shard_map/ppermute | solution.py:478
  48.5 6.9 %collective-permute-start.4 = (bf16[128,256]{1,0:T(8,128)(2,1)S(1)}, bf16[128,256]{1,0:T(8,128)(2,1)S(1)}, u32[]{:S(2)}, u32[]{:S(2)}) collective-permute-start(bf16[128,256]{1,0:T(8,128)(2,1)S(1)} %collective-permute-done.3.col1), channel_id=1, source_target_pairs={{128,256},{160,288},{192,320},{224,352},{256,384},{288,416},{320,4... | collective-permute-start | bytes 196616 | tf_op jit(solution)/shard_map/ppermute | solution.py:478
  55.4 2.0 %collective-permute-start.2 = (bf16[128,128]{1,0:T(8,128)(2,1)S(1)}, bf16[128,128]{1,0:T(8,128)(2,1)S(1)}, u32[]{:S(2)}, u32[]{:S(2)}) collective-permute-start(bf16[128,128]{1,0:T(8,128)(2,1)S(1)} %get-tuple-element.20), channel_id=1, source_target_pairs={{0,96},{32,64},{64,32},{96,0},{128,224},{160,192},{192,160},{224,1... | collective-permute-start | bytes 98312 | tf_op jit(solution)/shard_map/ppermute | solution.py:475
  57.5 1.9 %collective-permute-start.1 = (bf16[512,128]{1,0:T(8,128)(2,1)S(1)}, bf16[512,128]{1,0:T(8,128)(2,1)S(1)}, u32[]{:S(2)}, u32[]{:S(2)}) collective-permute-start(bf16[512,128]{1,0:T(8,128)(2,1)S(1)} %get-tuple-element.16.qm), channel_id=1, source_target_pairs={{0,64},{32,96},{64,0},{96,32},{128,192},{160,224},{192,128},{224,1... | collective-permute-start | bytes 393224 | tf_op jit(solution)/shard_map/ppermute | solution.py:475
  59.4 8.5 %collective-permute-start.5 = (bf16[128,256]{1,0:T(8,128)(2,1)S(1)}, bf16[128,256]{1,0:T(8,128)(2,1)S(1)}, u32[]{:S(2)}, u32[]{:S(2)}) collective-permute-start(bf16[128,256]{1,0:T(8,128)(2,1)S(1)} %collective-permute-done.4.col2), channel_id=1, source_target_pairs={{256,384},{288,416},{320,448},{352,480},{257,385},{289,417},{321,4... | collective-permute-start | bytes 196616 | tf_op jit(solution)/shard_map/ppermute | solution.py:478
  67.9 9.3 %shard_map.78 = (bf16[2048,128]{1,0:T(8,128)(2,1)}, f32[512,128]{1,0:T(8,128)}, f32[512,128]{1,0:T(8,128)}) custom-call(bf16[3,2048,128]{2,1,0:T(8,128)(2,1)} %bitcast.2, bf16[512,128]{1,0:T(8,128)(2,1)S(1)} %get-tuple-element.16.qm, bf16[512,256]{1,0:T(8,128)(2,1)S(1)} %get-tuple-element.17.kvm), custom_call_target="tpu_custom_call" | custom-call | flops 2000000000 | bytes 3000000 | tf_op jit(solution)/shard_map/pallas_call | solution.py:46
  77.2 0.0 copy-start
  77.3 7.3 %shard_map.79 = (f32[512,128]{1,0:T(8,128)}, f32[512,128]{1,0:T(8,128)}, bf16[144,128]{1,0:T(8,128)(2,1)S(1)}, bf16[544,128]{1,0:T(8,128)(2,1)S(1)}, bf16[144,128]{1,0:T(8,128)(2,1)S(1)}) custom-call(bf16[512,128]{1,0:T(8,128)(2,1)S(1)} %get-tuple-element.16.qm, bf16[512,256]{1,0:T(8,128)(2,1)S(1)} %get-tuple-element.17.kvm, ...), custom_call_target="tpu_custom_call" | custom-call | flops 1000000000 | bytes 4000000 | tf_op jit(solution)/shard_map/pallas_call | solution.py:46
  84.5 1.9 %collective-permute-start.7 = (bf16[544,128]{1,0:T(8,128)(2,1)S(1)}, bf16[544,128]{1,0:T(8,128)(2,1)S(1)}, u32[]{:S(2)}, u32[]{:S(2)}) collective-permute-start(bf16[544,128]{1,0:T(8,128)(2,1)S(1)} %get-tuple-element.27), channel_id=1, source_target_pairs={{0,64},{32,96},{64,0},{96,32},{128,192},{160,224},{192,128},{224,1... | collective-permute-start | bytes 417800 | tf_op jit(solution)/shard_map/ppermute | solution.py:475
  86.5 1.9 %collective-permute-start.6 = (bf16[144,128]{1,0:T(8,128)(2,1)S(1)}, bf16[144,128]{1,0:T(8,128)(2,1)S(1)}, u32[]{:S(2)}, u32[]{:S(2)}) collective-permute-start(bf16[144,128]{1,0:T(8,128)(2,1)S(1)} %get-tuple-element.26), channel_id=1, source_target_pairs={{0,32},{32,0},{64,96},{96,64},{128,160},{160,128},{192,224},{224,1... | collective-permute-start | bytes 110600 | tf_op jit(solution)/shard_map/ppermute | solution.py:475
  88.4 5.4 %collective-permute-start.8 = (bf16[144,128]{1,0:T(8,128)(2,1)S(1)}, bf16[144,128]{1,0:T(8,128)(2,1)S(1)}, u32[]{:S(2)}, u32[]{:S(2)}) collective-permute-start(bf16[144,128]{1,0:T(8,128)(2,1)S(1)} %get-tuple-element.28), channel_id=1, source_target_pairs={{0,96},{32,64},{64,32},{96,0},{128,224},{160,192},{192,160},{224,1... | collective-permute-start | bytes 110600 | tf_op jit(solution)/shard_map/ppermute | solution.py:475
  93.9 1.8 %shard_map.82 = bf16[32,2,128]{2,1,0:T(2,128)(2,1)} custom-call(s32[32]{0:T(128)S(1)} %copy-done.2, bf16[16,80,128]{2,1,0:T(8,128)(2,1)S(1)} %all-to-all-done.1.got, bf16[1024,256]{1,0:T(8,128)(2,1)S(1)} %copy-done), custom_call_target="tpu_custom_call" | custom-call | flops 10000000 | bytes 1000000 | tf_op jit(solution)/shard_map/pallas_call | solution.py:46
  95.6 10.1 %all-to-all-start.2 = ((bf16[32,2,128]{2,1,0:T(2,128)(2,1)}), bf16[32,2,128]{2,1,0:T(2,128)(2,1)S(1)}, u32[]{:S(2)}, u32[]{:S(2)}) async-start(bf16[32,2,128]{2,1,0:T(2,128)(2,1)} %shard_map.82), calls=%async_computation.2 | async-start | bytes 32768 | tf_op jit(solution)/shard_map/all_to_all | solution.py:544
  105.8 3.2 %shard_map.80 = bf16[2048,128]{1,0:T(8,128)(2,1)} custom-call(bf16[2048,128]{1,0:T(8,128)(2,1)} %get-tuple-element.18.near_h, f32[512,128]{1,0:T(8,128)} %get-tuple-element.24.acc_h, f32[512,128]{1,0:T(8,128)} %get-tuple-element.25.ml_h, bf16[144,128]{1,0:T(8,128)(2,1)S(1)} %collective-permute-done.6.back1, ...), custom_call_target="tpu_custom_call" | custom-call | flops 100000000 | bytes 4000000 | tf_op jit(solution)/shard_map/pallas_call | solution.py:46
  109.0 3.7 %all-to-all-done.2.got = bf16[32,2,128]{2,1,0:T(2,128)(2,1)S(1)} async-done(((bf16[32,2,128]{2,1,0:T(2,128)(2,1)}), bf16[32,2,128]{2,1,0:T(2,128)(2,1)S(1)}, u32[]{:S(2)}, u32[]{:S(2)}) %all-to-all-start.2) | async-done | bytes 16416 | tf_op jit(solution)/shard_map/all_to_all | solution.py:544
  112.7 1.6 %shard_map.83 = bf16[16,2,64]{2,1,0:T(2,128)(2,1)} custom-call(s32[32]{0:T(128)S(1)} %copy-done.2, bf16[32,2,128]{2,1,0:T(2,128)(2,1)S(1)} %all-to-all-done.2.got), custom_call_target="tpu_custom_call" | custom-call | bytes 100000 | tf_op jit(solution)/shard_map/pallas_call | solution.py:46
  (14 shorter events, 0.0 us)
Async XLA Ops:
  0.6 13.9 %copy-start.3 = (s32[32]{0:T(128)S(1)}, s32[32]{0:T(128)}, u32[]{:S(2)}) copy-start(s32[32]{0:T(128)} %lens.1) | copy-start | bytes 388
  0.6 0.7 copy-start.1
  18.6 75.2 %all-to-all-start.1 = ((bf16[16,80,128]{2,1,0:T(8,128)(2,1)}), bf16[16,80,128]{2,1,0:T(8,128)(2,1)S(1)}, u32[]{:S(2)}, u32[]{:S(2)}) async-start(bf16[16,80,128]{2,1,0:T(8,128)(2,1)} %shard_map.81), calls=%async_computation.1 | async-start | bytes 655360 | tf_op jit(solution)/shard_map/all_to_all | solution.py:498
  30.1 18.5 %collective-permute-start.3 = (bf16[128,256]{1,0:T(8,128)(2,1)S(1)}, bf16[128,256]{1,0:T(8,128)(2,1)S(1)}, u32[]{:S(2)}, u32[]{:S(2)}) collective-permute-start(bf16[128,256]{1,0:T(8,128)(2,1)S(1)} %get-tuple-element.21), channel_id=1, source_target_pairs={{0,128},{32,160},{64,192},{96,224},{128,256},{160,288},{192,320},{... | collective-permute-start | bytes 196616 | tf_op jit(solution)/shard_map/ppermute | solution.py:478
  32.3 45.0 %collective-permute-start = (bf16[576,256]{1,0:T(8,128)(2,1)S(1)}, bf16[576,256]{1,0:T(8,128)(2,1)S(1)}, u32[]{:S(2)}, u32[]{:S(2)}) collective-permute-start(bf16[576,256]{1,0:T(8,128)(2,1)S(1)} %get-tuple-element.19), channel_id=1, source_target_pairs={{0,32},{32,0},{64,96},{96,64},{128,160},{160,128},{192,224},{224,1... | collective-permute-start | bytes 884744 | tf_op jit(solution)/shard_map/ppermute | solution.py:475
  48.5 10.9 %collective-permute-start.4 = (bf16[128,256]{1,0:T(8,128)(2,1)S(1)}, bf16[128,256]{1,0:T(8,128)(2,1)S(1)}, u32[]{:S(2)}, u32[]{:S(2)}) collective-permute-start(bf16[128,256]{1,0:T(8,128)(2,1)S(1)} %collective-permute-done.3.col1), channel_id=1, source_target_pairs={{128,256},{160,288},{192,320},{224,352},{256,384},{288,416},{320,4... | collective-permute-start | bytes 196616 | tf_op jit(solution)/shard_map/ppermute | solution.py:478
  55.4 21.8 %collective-permute-start.2 = (bf16[128,128]{1,0:T(8,128)(2,1)S(1)}, bf16[128,128]{1,0:T(8,128)(2,1)S(1)}, u32[]{:S(2)}, u32[]{:S(2)}) collective-permute-start(bf16[128,128]{1,0:T(8,128)(2,1)S(1)} %get-tuple-element.20), channel_id=1, source_target_pairs={{0,96},{32,64},{64,32},{96,0},{128,224},{160,192},{192,160},{224,1... | collective-permute-start | bytes 98312 | tf_op jit(solution)/shard_map/ppermute | solution.py:475
  57.5 19.7 %collective-permute-start.1 = (bf16[512,128]{1,0:T(8,128)(2,1)S(1)}, bf16[512,128]{1,0:T(8,128)(2,1)S(1)}, u32[]{:S(2)}, u32[]{:S(2)}) collective-permute-start(bf16[512,128]{1,0:T(8,128)(2,1)S(1)} %get-tuple-element.16.qm), channel_id=1, source_target_pairs={{0,64},{32,96},{64,0},{96,32},{128,192},{160,224},{192,128},{224,1... | collective-permute-start | bytes 393224 | tf_op jit(solution)/shard_map/ppermute | solution.py:475
  59.4 17.8 %collective-permute-start.5 = (bf16[128,256]{1,0:T(8,128)(2,1)S(1)}, bf16[128,256]{1,0:T(8,128)(2,1)S(1)}, u32[]{:S(2)}, u32[]{:S(2)}) collective-permute-start(bf16[128,256]{1,0:T(8,128)(2,1)S(1)} %collective-permute-done.4.col2), channel_id=1, source_target_pairs={{256,384},{288,416},{320,448},{352,480},{257,385},{289,417},{321,4... | collective-permute-start | bytes 196616 | tf_op jit(solution)/shard_map/ppermute | solution.py:478
  77.2 16.6 %copy-start = (bf16[1024,256]{1,0:T(8,128)(2,1)S(1)}, bf16[1024,256]{1,0:T(8,128)(2,1)}, u32[]{:S(2)}) copy-start(bf16[1024,256]{1,0:T(8,128)(2,1)} %weight.1) | copy-start | bytes 1572868
  77.2 16.6 %copy-start.2 = (s32[32]{0:T(128)S(1)}, s32[32]{0:T(128)}, u32[]{:S(2)}) copy-start(s32[32]{0:T(128)} %own.7) | copy-start | bytes 388
  84.5 21.2 %collective-permute-start.7 = (bf16[544,128]{1,0:T(8,128)(2,1)S(1)}, bf16[544,128]{1,0:T(8,128)(2,1)S(1)}, u32[]{:S(2)}, u32[]{:S(2)}) collective-permute-start(bf16[544,128]{1,0:T(8,128)(2,1)S(1)} %get-tuple-element.27), channel_id=1, source_target_pairs={{0,64},{32,96},{64,0},{96,32},{128,192},{160,224},{192,128},{224,1... | collective-permute-start | bytes 417800 | tf_op jit(solution)/shard_map/ppermute | solution.py:475
  86.5 19.3 %collective-permute-start.6 = (bf16[144,128]{1,0:T(8,128)(2,1)S(1)}, bf16[144,128]{1,0:T(8,128)(2,1)S(1)}, u32[]{:S(2)}, u32[]{:S(2)}) collective-permute-start(bf16[144,128]{1,0:T(8,128)(2,1)S(1)} %get-tuple-element.26), channel_id=1, source_target_pairs={{0,32},{32,0},{64,96},{96,64},{128,160},{160,128},{192,224},{224,1... | collective-permute-start | bytes 110600 | tf_op jit(solution)/shard_map/ppermute | solution.py:475
  88.4 17.4 %collective-permute-start.8 = (bf16[144,128]{1,0:T(8,128)(2,1)S(1)}, bf16[144,128]{1,0:T(8,128)(2,1)S(1)}, u32[]{:S(2)}, u32[]{:S(2)}) collective-permute-start(bf16[144,128]{1,0:T(8,128)(2,1)S(1)} %get-tuple-element.28), channel_id=1, source_target_pairs={{0,96},{32,64},{64,32},{96,0},{128,224},{160,192},{192,160},{224,1... | collective-permute-start | bytes 110600 | tf_op jit(solution)/shard_map/ppermute | solution.py:475
  95.6 17.1 %all-to-all-start.2 = ((bf16[32,2,128]{2,1,0:T(2,128)(2,1)}), bf16[32,2,128]{2,1,0:T(2,128)(2,1)S(1)}, u32[]{:S(2)}, u32[]{:S(2)}) async-start(bf16[32,2,128]{2,1,0:T(2,128)(2,1)} %shard_map.82), calls=%async_computation.2 | async-start | bytes 32768 | tf_op jit(solution)/shard_map/all_to_all | solution.py:544

commit v4 on v3

--- a/solution.py
+++ b/solution.py
@@ -15,6 +15,7 @@
 BF16 = jnp.bfloat16
 
 VMEM = pltpu.VMEM
+SMEM = pltpu.SMEM
 
 
 def vspec():
@@ -73,7 +74,11 @@
     return grp, rank
 
 
-def start_kernel(own, dec, qkv, sent, qm, kvm, ask, msg, far, raw, wide, sem, part_sem):
+def start_kernel(
+    own_h, dec, qkv, raw, sent, qm, ask, msg, far, own, wide, sem, part_sem, own_sem
+):
+    own_copy = pltpu.make_async_copy(own_h, own, own_sem)
+    own_copy.start()
     me = lax.axis_index("req")
     rows = qkv.shape[1]
     parts = []
@@ -82,6 +87,7 @@
         cp.start()
         parts.append(cp)
     copies = []
+    own_copy.wait()
     for b in range(8):
         src = [jnp.int32(0), jnp.int32(0)]
         for k in range(4):
@@ -109,7 +115,6 @@
                     msg[pl.ds(512, 64), pl.ds(HD, HD)] = got[64:]
             else:
                 lanes = pl.ds(HD * (part - 1), HD)
-                kvm[at, lanes] = got
                 msg[at, lanes] = got
                 if c == 0:
                     far[:, lanes] = got
@@ -117,87 +122,93 @@
         cp.wait()
 
 
-def softmax_step(m, l, acc, s, v, mult=None):
-    m_new = jnp.maximum(m, jnp.max(s, axis=1, keepdims=True))
-    alpha = jnp.exp2((m - m_new) * EXP_SCALE)
-    p = jnp.exp2((s - m_new) * EXP_SCALE)
-    if mult is not None:
-        p = p * mult
-    l_new = l * alpha + jnp.sum(p, axis=1, keepdims=True)
-    acc_new = acc * alpha + dot_n(p.astype(BF16), v)
-    return m_new, l_new, acc_new
-
-
 def both(m, l):
     count = m.shape[0]
     lane = lax.broadcasted_iota(jnp.int32, (count, HD), 1)
     return jnp.where(lane == 0, m, l)
 
 
+def softmax_once(pieces, twice=False):
+    m = functools.reduce(jnp.maximum, [jnp.max(s, axis=1, keepdims=True) for s, _ in pieces])
+    l = 0.0
+    acc = 0.0
+    for s, v in pieces:
+        p = jnp.exp2((s - m) * EXP_SCALE)
+        if twice:
+            col = lax.broadcasted_iota(jnp.int32, (1, s.shape[1]), 1)
+            p = jnp.concatenate([p[:128] * jnp.where(col < 128, 2.0, 1.0), p[128:]], axis=0)
+        l = l + jnp.sum(p, axis=1, keepdims=True)
+        acc = acc + dot_n(p.astype(BF16), v)
+    return m, l, acc
+
+
+def combine(terms):
+    top = functools.reduce(jnp.maximum, [t[0] for t in terms])
+    length = 0.0
+    total = 0.0
+    for m, l, acc in terms:
+        w = jnp.exp2((m - top) * EXP_SCALE)
+        length = length + l * w
+        total = total + acc * w
+    return top, length, total
+
+
+def term(acc, ml, at):
+    pair = ml[at, :]
+    return pair[:, 0:1], pair[:, 1:2], acc[at, :]
+
+
 def near_kernel(
-    qkv, qm, kvm, near_h, acc_h, ml_h, raw, acc_s, ml_s, near_o, acc_o, ml_o, sem, out_sem
+    raw, qm, msg, cache_h, near_h, acc_h, ml_h, cache,
+    acc_s, ml_s, near_o, acc_o, ml_o, sem, out_sem,
 ):
-    rows = qkv.shape[1]
+    rows = raw.shape[1]
     step = 256
+    fetch = pltpu.make_async_copy(cache_h, cache, sem.at[2])
+    fetch.start()
     copies = []
+    inner = lax.div(lax.rem(head_id(), 16), 4)
+
+    def order(dims, dim):
+        a = lax.broadcasted_iota(jnp.int32, dims, dim)
+        return 4 * (a & 127) + ((lax.shift_right_logical(a, 7) + inner) & 3)
+
+    mine = pl.ds(0, 512)
+    s = dot_t(qm[...], msg[mine, pl.ds(0, HD)])
+    s = jnp.where(order((1, 512), 1) <= order((512, 1), 0), s, NEG)
+    m, l, acc = softmax_once([(s, msg[mine, pl.ds(HD, HD)])], True)
+    acc_o[...] = acc
+    ml_o[...] = both(m, l)
+    tri = lax.broadcasted_iota(jnp.int32, (step, step), 1) <= lax.broadcasted_iota(
+        jnp.int32, (step, step), 0
+    )
     for b in range(rows // step):
         at = pl.ds(step * b, step)
-        cp = pltpu.make_async_copy(qkv.at[:, at, :], raw.at[:, at, :], sem.at[b])
-        cp.start()
-        copies.append(cp)
-    tri = lax.broadcasted_iota(jnp.int32, (step, step), 1) <= lax.broadcasted_iota(
-        jnp.int32, (step, step), 0
-    )
-    for b in range(rows // step):
-        at = pl.ds(step * b, step)
-        copies[b].wait()
         q = raw[0, at, :]
-        s_d = jnp.where(tri, dot_t(q, raw[1, at, :]), NEG)
-        m = jnp.max(s_d, axis=1, keepdims=True)
+        parts = [(jnp.where(tri, dot_t(q, raw[1, at, :]), NEG), raw[2, at, :])]
         if b:
-            s_f = dot_t(q, raw[1, pl.ds(0, step * b), :])
-            m = jnp.maximum(m, jnp.max(s_f, axis=1, keepdims=True))
-        p_d = jnp.exp2((s_d - m) * EXP_SCALE)
-        l = jnp.sum(p_d, axis=1, keepdims=True)
-        acc = dot_n(p_d.astype(BF16), raw[2, at, :])
-        if b:
-            p_f = jnp.exp2((s_f - m) * EXP_SCALE)
-            l = l + jnp.sum(p_f, axis=1, keepdims=True)
-            acc = acc + dot_n(p_f.astype(BF16), raw[2, pl.ds(0, step * b), :])
+            before = pl.ds(0, step * b)
+            parts.append((dot_t(q, raw[1, before, :]), raw[2, before, :]))
+        m, l, acc = softmax_once(parts)
         near_o[at, :] = (acc / l).astype(BF16)
         cp = pltpu.make_async_copy(near_o.at[at], near_h.at[at], out_sem.at[b])
         cp.start()
         copies.append(cp)
         acc_s[at, :] = acc
         ml_s[at, :] = both(m, l)
-    inner = lax.div(lax.rem(head_id(), 16), 4)
-
-    def order(shape, dim):
-        a = lax.broadcasted_iota(jnp.int32, shape, dim)
-        return 4 * (a & 127) + ((lax.shift_right_logical(a, 7) + inner) & 3)
-
     for c in range(4):
         at = pl.ds(128 * c, 128)
         pick = pl.ds(class_residue(c), 128, stride=16)
-        s = dot_t(qm[at, :], kvm[:, pl.ds(0, HD)])
-        rows_at = lax.broadcasted_iota(jnp.int32, (128, 1), 0)
-        row_order = 4 * rows_at + ((c + inner) & 3)
-        s = jnp.where(order((1, 512), 1) <= row_order, s, NEG)
-        mult = None
-        if c == 0:
-            mult = jnp.where(lax.broadcasted_iota(jnp.int32, (1, 512), 1) < 128, 2.0, 1.0)
-        ml = ml_s[pick, :]
-        m, l, acc = softmax_step(
-            ml[:, 0:1], ml[:, 1:2], acc_s[pick, :], s, kvm[:, pl.ds(HD, HD)], mult
-        )
+        m, l, acc = combine([term(acc_s, ml_s, pick), term(acc_o, ml_o, at)])
         acc_o[at, :] = acc
         ml_o[at, :] = both(m, l)
     for i, (src, dst) in enumerate(((acc_o, acc_h), (ml_o, ml_h))):
         cp = pltpu.make_async_copy(src, dst, sem.at[i])
         cp.start()
         copies.append(cp)
-    for cp in copies[rows // step :]:
+    for cp in copies:
         cp.wait()
+    fetch.wait()
 
 
 def pack(rows_m, rows_l):
@@ -221,80 +232,91 @@
 
 
 def share_kernel(
-    qm, kvm, got1, got2, got3, col1, col2, col3, acc_i, ml_i,
-    acc_o, ml_o, back1, back2, back3, acc_s, ml_s, sem,
+    qm, msg, got1, got2, got3, col1, col2, col3, acc_h, ml_h,
+    acc_o, ml_o, back1, back2, back3,
+    acc_n, ml_n, acc_m, ml_m, acc_2, ml_2, acc_f, ml_f, qf, kf, sem,
 ):
     z = lax.axis_index("seq")
     local = lax.rem(z, 4)
     group = lax.div(z, 4)
-    one = pl.ds(0, 512)
-    load_acc = pltpu.make_async_copy(acc_i, acc_s.at[one], sem.at[0])
-    load_ml = pltpu.make_async_copy(ml_i, ml_s.at[one], sem.at[1])
+    load_acc = pltpu.make_async_copy(acc_h, acc_n, sem.at[0])
+    load_ml = pltpu.make_async_copy(ml_h, ml_n, sem.at[1])
     load_acc.start()
     load_ml.start()
-    rest = pl.ds(512, 768)
-    acc_s[rest, :] = jnp.zeros((768, HD), F32)
-    ml_s[rest, :] = both(jnp.full((768, 1), NEG, F32), jnp.zeros((768, 1), F32))
-
-    def update(first, q, keys, values, twice=False):
-        count = q.shape[0]
-        at = pl.ds(first, count)
-        s = dot_t(q, keys)
-        mult = None
-        if twice:
-            width = s.shape[1]
-            mult = jnp.where(
-                (lax.broadcasted_iota(jnp.int32, (count, width), 0) < 128)
-                & ((lax.broadcasted_iota(jnp.int32, (count, width), 1) & 511) < 128),
-                2.0,
-                1.0,
-            )
-        ml = ml_s[at, :]
-        m, l, acc = softmax_step(ml[:, 0:1], ml[:, 1:2], acc_s[at, :], s, values, mult)
-        acc_s[at, :] = acc
-        ml_s[at, :] = both(m, l)
-
-    own_k, own_v = kvm[:, pl.ds(0, HD)], kvm[:, pl.ds(HD, HD)]
-    one_k, one_v = got1[one, pl.ds(0, HD)], got1[one, pl.ds(HD, HD)]
-
-    @pl.when(local < 2)
-    def _():
-        update(512, got2[...], own_k, own_v, True)
-        update(512, got2[...], one_k, one_v, True)
-
+    one = pl.ds(0, 512)
+    head = pl.ds(0, 128)
+    tail = pl.ds(128, 384)
+    keys, values = pl.ds(0, HD), pl.ds(HD, HD)
+
+    def fill(valid, acc_r, ml_r, compute):
+        @pl.when(valid)
+        def _():
+            m, l, acc = compute()
+            acc_r[...] = acc
+            ml_r[...] = both(m, l)
+
+        @pl.when(jnp.logical_not(valid))
+        def _():
+            acc_r[...] = jnp.zeros((512, HD), F32)
+            ml_r[...] = both(jnp.full((512, 1), NEG, F32), jnp.zeros((512, 1), F32))
+
+    def other_pair():
+        q = got2[...]
+        return softmax_once(
+            [
+                (dot_t(q, msg[one, keys]), msg[one, values]),
+                (dot_t(q, got1[one, keys]), got1[one, values]),
+            ],
+            True,
+        )
+
+    def own_pair():
+        return softmax_once([(dot_t(qm[...], got1[one, keys]), got1[one, values])], True)
+
+    def far_level():
+        half = pl.ds(512, 64)
+        qf[pl.ds(0, 128), :] = qm[head, :]
+        qf[pl.ds(128, 128), :] = got2[head, :]
+        qf[pl.ds(256, 64), :] = got1[half, keys]
+        qf[pl.ds(320, 64), :] = got1[half, values]
+        qf[pl.ds(384, 128), :] = got3[...]
+        for i, col in enumerate((col1, col2, col3)):
+            kf[pl.ds(128 * i, 128), :] = col[...]
+        s = dot_t(qf[...], kf[:, keys])
+        at = lax.broadcasted_iota(jnp.int32, (1, 384), 1)
+        return softmax_once([(jnp.where(at < 128 * group, s, NEG), kf[:, values])])
+
+    fill(local < 2, acc_2, ml_2, other_pair)
+    fill((local & 1) == 1, acc_m, ml_m, own_pair)
+    fill(group > 0, acc_f, ml_f, far_level)
+
+    def give(out, terms, rows):
+        m, l, acc = combine(terms)
+        out[rows, :] = (acc / jnp.where(l > 0.0, l, 1.0)).astype(BF16)
+        return m, l
+
+    far2 = term(acc_f, ml_f, pl.ds(128, 128))
+    m_a, l_a = give(back2, [term(acc_2, ml_2, head), far2], head)
+    m_b, l_b = give(back2, [term(acc_2, ml_2, tail)], tail)
+    back2[pl.ds(512, 32), :] = pack(
+        jnp.concatenate([m_a, m_b], axis=0), jnp.concatenate([l_a, l_b], axis=0)
+    )
+    for out, first in ((back1, 256), (back3, 384)):
+        m, l = give(out, [term(acc_f, ml_f, pl.ds(first, 128))], head)
+        out[pl.ds(128, 16), :] = pack(m, l)
     load_acc.wait()
     load_ml.wait()
-
-    @pl.when((local & 1) == 1)
-    def _():
-        update(0, qm[...], one_k, one_v, True)
-
-    half = pl.ds(512, 64)
-    head = pl.ds(0, 128)
-    queries = ((0, qm), (512, got2), (1152, got3))
-    for depth, col in ((1, col1), (2, col2), (3, col3)):
-
-        @pl.when(group >= depth)
-        def _(col=col):
-            k, v = col[:, pl.ds(0, HD)], col[:, pl.ds(HD, HD)]
-            for first, q in queries:
-                update(first, q[head, :], k, v)
-            near_q = jnp.concatenate(
-                [got1[half, pl.ds(0, HD)], got1[half, pl.ds(HD, HD)]], axis=0
-            )
-            update(1024, near_q, k, v)
-
-    save_acc = pltpu.make_async_copy(acc_s.at[one], acc_o, sem.at[0])
-    save_ml = pltpu.make_async_copy(ml_s.at[one], ml_o, sem.at[1])
+    for at in (head, tail):
+        terms = [term(acc_n, ml_n, at), term(acc_m, ml_m, at)]
+        if at is head:
+            terms.append(term(acc_f, ml_f, head))
+        m, l, acc = combine(terms)
+        acc_n[at, :] = acc
+        ml_n[at, :] = both(m, l)
+    save_acc = pltpu.make_async_copy(acc_n, acc_o, sem.at[0])
+    save_ml = pltpu.make_async_copy(ml_n, ml_o, sem.at[1])
     save_acc.start()
     save_ml.start()
-    for out, first, count in ((back2, 512, 512), (back1, 1024, 128), (back3, 1152, 128)):
-        at = pl.ds(first, count)
-        ml = ml_s[at, :]
-        m, l = ml[:, 0:1], ml[:, 1:2]
-        out[pl.ds(0, count), :] = (acc_s[at, :] / jnp.where(l > 0.0, l, 1.0)).astype(BF16)
-        packed = pack(m, l)
-        out[pl.ds(count, packed.shape[0]), :] = packed
     save_acc.wait()
     save_ml.wait()
 
@@ -335,12 +357,7 @@
     return hi, mid, (rest - mid).astype(BF16).astype(F32)
 
 
-def cache_kernel(own, lens, arr, cache_h, out, cache, o_s, st_s, sem):
-    copies = []
-    for k in range(4):
-        cp = pltpu.make_async_copy(cache_h.at[k], cache.at[k], sem.at[k])
-        cp.start()
-        copies.append(cp)
+def cache_kernel(own, lens, arr, cache, out, o_s, st_s):
     z = lax.axis_index("seq")
     me = lax.axis_index("req")
     per = cache.shape[2]
@@ -363,7 +380,6 @@
         kn = jnp.concatenate([arr[row, 1].astype(F32), pad], axis=0).astype(BF16)
         vn = jnp.concatenate([arr[row, 2].astype(F32), pad], axis=0).astype(BF16)
         c_ok = col < lens[4 * me + k]
-        copies[k].wait()
         s_c = jnp.where(c_ok, dot_t(qd, cache[k, 0]), NEG)
         s_n = jnp.where(new_ok, dot_t(qd, kn), NEG)
         m = jnp.maximum(
@@ -449,23 +465,24 @@
 
 def staged(pre_qkv, cache_kv, dec_new, out_weight, owner_slot, prompt_lengths):
     qkv = jnp.swapaxes(pre_qkv, 0, 1)
-    sent, qm, kvm, ask, msg, far = call(
+    raw, sent, qm, ask, msg, far = call(
         start_kernel,
         (
+            shape((3, 2048, HD)),
             shape(dec_new.shape),
             shape((512, HD)),
-            shape((512, 2 * HD)),
             shape((128, HD)),
             shape((576, 2 * HD)),
             shape((128, 2 * HD)),
         ),
-        (owner_slot, far_memory(dec_new), far_memory(qkv)),
-        [sspec(), hspec(), hspec()],
+        (far_memory(owner_slot), far_memory(dec_new), far_memory(qkv)),
+        [hspec(), hspec(), hspec()],
         [
-            VMEM((3, 2048, HD), BF16),
+            SMEM((32,), jnp.int32),
             VMEM((2048, HD), F32),
             pltpu.SemaphoreType.DMA((16,)),
             pltpu.SemaphoreType.DMA((3,)),
+            pltpu.SemaphoreType.DMA,
         ],
         nbytes=4000000,
     )
@@ -481,30 +498,14 @@
     got3 = swap(ask, 3)
     got2 = swap(qm, 2)
     got1 = swap(msg, 1)
-    partial = call(
-        cache_kernel,
-        shape((16, 80, HD)),
-        (owner_slot, prompt_lengths, arrived, far_memory(cache_kv)),
-        [sspec(), sspec(), vspec(), hspec()],
-        [
-            VMEM(cache_kv.shape, BF16),
-            VMEM((64, HD), F32),
-            VMEM((64, HD), F32),
-            pltpu.SemaphoreType.DMA((4,)),
-        ],
-        flops=10**8,
-        nbytes=2000000,
-    )
-    parts = lax.all_to_all(partial, "seq", 0, 0, tiled=True)
     col2 = relay(col1, 4)
     state = [pltpu.HBM((512, HD), F32)] * 2
-    near_o, acc, ml = call(
+    near_o, acc, ml, cache = call(
         near_kernel,
-        (pltpu.HBM((2048, HD), BF16), *state),
-        (far_memory(qkv), qm, kvm),
-        [hspec(), vspec(), vspec()],
+        (pltpu.HBM((2048, HD), BF16), *state, shape(cache_kv.shape)),
+        (raw, qm, msg, far_memory(cache_kv)),
+        [vspec(), vspec(), vspec(), hspec()],
         [
-            VMEM((3, 2048, HD), BF16),
             VMEM((2048, HD), F32),
             VMEM((2048, HD), F32),
             VMEM((2048, HD), BF16),
@@ -516,15 +517,26 @@
         flops=2 * 10**9,
         nbytes=3000000,
         trans=2 * 10**6,
-        outs=[hspec(), hspec(), hspec()],
-    )
+        outs=[hspec(), hspec(), hspec(), vspec()],
+    )
+    partial = call(
+        cache_kernel,
+        shape((16, 80, HD)),
+        (owner_slot, prompt_lengths, arrived, cache),
+        [sspec(), sspec(), vspec(), vspec()],
+        [VMEM((64, HD), F32), VMEM((64, HD), F32)],
+        flops=10**8,
+        nbytes=2000000,
+    )
+    parts = lax.all_to_all(partial, "seq", 0, 0, tiled=True)
     col3 = relay(col2, 8)
     acc, ml, back1, back2, back3 = call(
         share_kernel,
         (*state, shape((144, HD)), shape((544, HD)), shape((144, HD))),
-        (qm, kvm, got1, got2, got3, col1, col2, col3, far_memory(acc), far_memory(ml)),
+        (qm, msg, got1, got2, got3, col1, col2, col3, far_memory(acc), far_memory(ml)),
         [vspec()] * 8 + [hspec()] * 2,
-        [VMEM((1280, HD), F32)] * 2 + [pltpu.SemaphoreType.DMA((2,))],
+        [VMEM((512, HD), F32)] * 8
+        + [VMEM((512, HD), BF16), VMEM((384, 2 * HD), BF16), pltpu.SemaphoreType.DMA((2,))],
         flops=10**9,
         nbytes=4000000,
         trans=10**6,

time: 115 us -> 116 us (level)
  the two profiles are of different devices: /device:TPU:257 before, /device:TPU:289 now
where the time goes in v4:
time: 116 us; the launch traced here: 115 us
  starting transfers between devices  66.3 us (57%)
  waiting for transfers between devices  24.8 us (21%)
  Pallas kernels  23.4 us (20%)
    ppermute x6, starting transfers between devices, swap(): return lax.ppermute(x, 'seq', [(i, i ^ bits) for i in range(16)])  29.9 us
    pallas_call x7, Pallas kernels, call(): pl.pallas_call(body, out_shape=out_shape, in_specs=specs, out_specs=vspec...  23.4 us
    ppermute x3, waiting for transfers between devices, relay(): return lax.ppermute(x, 'seq', [(i, i + 4) for i in range(first, 12)])  19.8 us
    all_to_all x1, starting transfers between devices, staged(): results = lax.all_to_all(answers, ('head', 'req'), 0, 0, tiled=True)  11.7 us
    all_to_all x1, starting transfers between devices, staged(): parts = lax.all_to_all(partial, 'seq', 0, 0, tiled=True)  11 us
    ppermute x3, starting transfers between devices, relay(): return lax.ppermute(x, 'seq', [(i, i + 4) for i in range(first, 12)])  8.56 us
    all_to_all x1, starting transfers between devices, staged(): arrived = lax.all_to_all(sent, 'req', 0, 0, tiled=True)  5.02 us
    all_to_all x1, waiting for transfers between devices, staged(): results = lax.all_to_all(answers, ('head', 'req'), 0, 0, tiled=True)  3.74 us
  transfers between devices with their start and end apart: 12, of which 4 were waited for; matrix products, arithmetic and copies ran while one was open for 0% of the time, Pallas kernels for 14%

profile of v4, /device:TPU:289, one launch (start us, length us, event | category | flops | bytes accessed | tf_op | source)
XLA Modules:
  0.0 115.3 jit_solution(17994996283825421426)
XLA Ops:
  0.6 2.9 %shard_map.77 = (bf16[3,2048,128]{2,1,0:T(8,128)(2,1)S(1)}, bf16[16,3,2,1024]{3,2,1,0:T(2,128)(2,1)}, bf16[512,128]{1,0:T(8,128)(2,1)S(1)}, bf16[128,128]{1,0:T(...) custom-call(s32[32]{0:T(128)} %own.5, bf16[16,3,2,1024]{3,2,1,0:T(2,128)(2,1)} %dec.1, ...), custom_call_target="tpu_custom_call" | custom-call | bytes 4000000 | tf_op jit(solution)/shard_map/pallas_call | solution.py:47
  3.6 5.0 %all-to-all-start = ((bf16[16,3,2,1024]{3,2,1,0:T(2,128)(2,1)}), bf16[16,3,2,1024]{3,2,1,0:T(2,128)(2,1)S(1)}, u32[]{:S(2)}, u32[]{:S(2)}) async-start(bf16[16,3,2,1024]{3,2,1,0:T(2,128)(2,1)} %get-tuple-element.30), calls=%async_computation | async-start | bytes 393216 | tf_op jit(solution)/shard_map/all_to_all | solution.py:489
  8.6 6.5 %shard_map.78 = (bf16[2048,128]{1,0:T(8,128)(2,1)}, f32[512,128]{1,0:T(8,128)}, f32[512,128]{1,0:T(8,128)}, bf16[4,2,64,1024]{3,2,1,0:T(8,128)(2,1)S(1)}) custom-call(bf16[3,2048,128]{2,1,0:T(8,128)(2,1)S(1)} %get-tuple-element.17.raw, bf16[512,128]{1,0:T(8,128)(2,1)S(1)} %get-tuple-element.18.qm, bf16[576,256]{1,0:T(8,128)(2,1)S(1)} %get-tuple-element.19.msg, ...), custom_call_target="tpu_custom_call" | custom-call | flops 2000000000 | bytes 3000000 | tf_op jit(solution)/shard_map/pallas_call | solution.py:47
  15.1 2.6 %shard_map.81 = bf16[16,80,128]{2,1,0:T(8,128)(2,1)} custom-call(s32[32]{0:T(128)S(1)} %copy-done.1, s32[32]{0:T(128)S(1)} %copy-done.2, bf16[16,3,2,1024]{3,2,1,0:T(2,128)(2,1)S(1)} %all-to-all-done.arr, bf16[4,2,64,1024]{3,2,1,0:T(8,128)(2,1)S(1)} %get-tuple-element.31.cache), custom_call_target="tpu_custom_call" | custom-call | flops 100000000 | bytes 2000000 | tf_op jit(solution)/shard_map/pallas_call | solution.py:47
  17.7 11.0 %all-to-all-start.1 = ((bf16[16,80,128]{2,1,0:T(8,128)(2,1)}), bf16[16,80,128]{2,1,0:T(8,128)(2,1)S(1)}, u32[]{:S(2)}, u32[]{:S(2)}) async-start(bf16[16,80,128]{2,1,0:T(8,128)(2,1)} %shard_map.81), calls=%async_computation.1 | async-start | bytes 655360 | tf_op jit(solution)/shard_map/all_to_all | solution.py:531
  28.7 3.1 %collective-permute-start = (bf16[576,256]{1,0:T(8,128)(2,1)S(1)}, bf16[576,256]{1,0:T(8,128)(2,1)S(1)}, u32[]{:S(2)}, u32[]{:S(2)}) collective-permute-start(bf16[576,256]{1,0:T(8,128)(2,1)S(1)} %get-tuple-element.19.msg), channel_id=1, source_target_pairs={{0,32},{32,0},{64,96},{96,64},{128,160},{160,128},{192,224},{224,1... | collective-permute-start | bytes 884744 | tf_op jit(solution)/shard_map/ppermute | solution.py:492
  31.8 2.2 %collective-permute-start.3 = (bf16[128,256]{1,0:T(8,128)(2,1)S(1)}, bf16[128,256]{1,0:T(8,128)(2,1)S(1)}, u32[]{:S(2)}, u32[]{:S(2)}) collective-permute-start(bf16[128,256]{1,0:T(8,128)(2,1)S(1)} %get-tuple-element.22), channel_id=1, source_target_pairs={{0,128},{32,160},{64,192},{96,224},{128,256},{160,288},{192,320},{... | collective-permute-start | bytes 196616 | tf_op jit(solution)/shard_map/ppermute | solution.py:495
  34.0 2.2 %collective-permute-start.1 = (bf16[512,128]{1,0:T(8,128)(2,1)S(1)}, bf16[512,128]{1,0:T(8,128)(2,1)S(1)}, u32[]{:S(2)}, u32[]{:S(2)}) collective-permute-start(bf16[512,128]{1,0:T(8,128)(2,1)S(1)} %get-tuple-element.18.qm), channel_id=1, source_target_pairs={{0,64},{32,96},{64,0},{96,32},{128,192},{160,224},{192,128},{224,1... | collective-permute-start | bytes 393224 | tf_op jit(solution)/shard_map/ppermute | solution.py:492
  36.2 9.6 %collective-permute-done.3.col1 = bf16[128,256]{1,0:T(8,128)(2,1)S(1)} collective-permute-done((bf16[128,256]{1,0:T(8,128)(2,1)S(1)}, bf16[128,256]{1,0:T(8,128)(2,1)S(1)}, u32[]{:S(2)}, u32[]{:S(2)}) %collective-permute-start.3) | collective-permute-done | bytes 65568 | tf_op jit(solution)/shard_map/ppermute | solution.py:495
  45.8 5.1 %collective-permute-start.4 = (bf16[128,256]{1,0:T(8,128)(2,1)S(1)}, bf16[128,256]{1,0:T(8,128)(2,1)S(1)}, u32[]{:S(2)}, u32[]{:S(2)}) collective-permute-start(bf16[128,256]{1,0:T(8,128)(2,1)S(1)} %collective-permute-done.3.col1), channel_id=1, source_target_pairs={{128,256},{160,288},{192,320},{224,352},{256,384},{288,416},{320,4... | collective-permute-start | bytes 196616 | tf_op jit(solution)/shard_map/ppermute | solution.py:495
  50.9 10.2 %collective-permute-done.4.col2 = bf16[128,256]{1,0:T(8,128)(2,1)S(1)} collective-permute-done((bf16[128,256]{1,0:T(8,128)(2,1)S(1)}, bf16[128,256]{1,0:T(8,128)(2,1)S(1)}, u32[]{:S(2)}, u32[]{:S(2)}) %collective-permute-start.4) | collective-permute-done | bytes 65568 | tf_op jit(solution)/shard_map/ppermute | solution.py:495
  61.0 1.3 %collective-permute-start.5 = (bf16[128,256]{1,0:T(8,128)(2,1)S(1)}, bf16[128,256]{1,0:T(8,128)(2,1)S(1)}, u32[]{:S(2)}, u32[]{:S(2)}) collective-permute-start(bf16[128,256]{1,0:T(8,128)(2,1)S(1)} %collective-permute-done.4.col2), channel_id=1, source_target_pairs={{256,384},{288,416},{320,448},{352,480},{257,385},{289,417},{321,4... | collective-permute-start | bytes 196616 | tf_op jit(solution)/shard_map/ppermute | solution.py:495
  62.3 16.3 %collective-permute-start.2 = (bf16[128,128]{1,0:T(8,128)(2,1)S(1)}, bf16[128,128]{1,0:T(8,128)(2,1)S(1)}, u32[]{:S(2)}, u32[]{:S(2)}) collective-permute-start(bf16[128,128]{1,0:T(8,128)(2,1)S(1)} %get-tuple-element.21), channel_id=1, source_target_pairs={{0,96},{32,64},{64,32},{96,0},{128,224},{160,192},{192,160},{224,1... | collective-permute-start | bytes 98312 | tf_op jit(solution)/shard_map/ppermute | solution.py:492
  78.6 1.3 %collective-permute-done.2.got3 = bf16[128,128]{1,0:T(8,128)(2,1)S(1)} collective-permute-done((bf16[128,128]{1,0:T(8,128)(2,1)S(1)}, bf16[128,128]{1,0:T(8,128)(2,1)S(1)}, u32[]{:S(2)}, u32[]{:S(2)}) %collective-permute-start.2) | collective-permute-done | bytes 32800 | tf_op jit(solution)/shard_map/ppermute | solution.py:492
  79.9 0.0 copy-start
  79.9 5.0 %shard_map.79 = (f32[512,128]{1,0:T(8,128)}, f32[512,128]{1,0:T(8,128)}, bf16[144,128]{1,0:T(8,128)(2,1)S(1)}, bf16[544,128]{1,0:T(8,128)(2,1)S(1)}, bf16[144,128]{1,0:T(8,128)(2,1)S(1)}) custom-call(bf16[512,128]{1,0:T(8,128)(2,1)S(1)} %get-tuple-element.18.qm, bf16[576,256]{1,0:T(8,128)(2,1)S(1)} %get-tuple-element.19.msg, ...), custom_call_target="tpu_custom_call" | custom-call | flops 1000000000 | bytes 4000000 | tf_op jit(solution)/shard_map/pallas_call | solution.py:47
  84.9 1.9 %collective-permute-start.7 = (bf16[544,128]{1,0:T(8,128)(2,1)S(1)}, bf16[544,128]{1,0:T(8,128)(2,1)S(1)}, u32[]{:S(2)}, u32[]{:S(2)}) collective-permute-start(bf16[544,128]{1,0:T(8,128)(2,1)S(1)} %get-tuple-element.28), channel_id=1, source_target_pairs={{0,64},{32,96},{64,0},{96,32},{128,192},{160,224},{192,128},{224,1... | collective-permute-start | bytes 417800 | tf_op jit(solution)/shard_map/ppermute | solution.py:492
  86.8 2.4 %collective-permute-start.6 = (bf16[144,128]{1,0:T(8,128)(2,1)S(1)}, bf16[144,128]{1,0:T(8,128)(2,1)S(1)}, u32[]{:S(2)}, u32[]{:S(2)}) collective-permute-start(bf16[144,128]{1,0:T(8,128)(2,1)S(1)} %get-tuple-element.27), channel_id=1, source_target_pairs={{0,32},{32,0},{64,96},{96,64},{128,160},{160,128},{192,224},{224,1... | collective-permute-start | bytes 110600 | tf_op jit(solution)/shard_map/ppermute | solution.py:492
  89.3 4.0 %collective-permute-start.8 = (bf16[144,128]{1,0:T(8,128)(2,1)S(1)}, bf16[144,128]{1,0:T(8,128)(2,1)S(1)}, u32[]{:S(2)}, u32[]{:S(2)}) collective-permute-start(bf16[144,128]{1,0:T(8,128)(2,1)S(1)} %get-tuple-element.29), channel_id=1, source_target_pairs={{0,96},{32,64},{64,32},{96,0},{128,224},{160,192},{192,160},{224,1... | collective-permute-start | bytes 110600 | tf_op jit(solution)/shard_map/ppermute | solution.py:492
  93.3 1.8 %shard_map.82 = bf16[32,2,128]{2,1,0:T(2,128)(2,1)} custom-call(s32[32]{0:T(128)S(1)} %copy-done.1, bf16[16,80,128]{2,1,0:T(8,128)(2,1)S(1)} %all-to-all-done.1.got, bf16[1024,256]{1,0:T(8,128)(2,1)S(1)} %copy-done), custom_call_target="tpu_custom_call" | custom-call | flops 10000000 | bytes 1000000 | tf_op jit(solution)/shard_map/pallas_call | solution.py:47
  95.1 11.7 %all-to-all-start.2 = ((bf16[32,2,128]{2,1,0:T(2,128)(2,1)}), bf16[32,2,128]{2,1,0:T(2,128)(2,1)S(1)}, u32[]{:S(2)}, u32[]{:S(2)}) async-start(bf16[32,2,128]{2,1,0:T(2,128)(2,1)} %shard_map.82), calls=%async_computation.2 | async-start | bytes 32768 | tf_op jit(solution)/shard_map/all_to_all | solution.py:556
  106.8 3.2 %shard_map.80 = bf16[2048,128]{1,0:T(8,128)(2,1)} custom-call(bf16[2048,128]{1,0:T(8,128)(2,1)} %get-tuple-element.20.near_h, f32[512,128]{1,0:T(8,128)} %get-tuple-element.25.acc_h, f32[512,128]{1,0:T(8,128)} %get-tuple-element.26.ml_h, bf16[144,128]{1,0:T(8,128)(2,1)S(1)} %collective-permute-done.6.back1, ...), custom_call_target="tpu_custom_call" | custom-call | flops 100000000 | bytes 4000000 | tf_op jit(solution)/shard_map/pallas_call | solution.py:47
  110.0 3.7 %all-to-all-done.2.got = bf16[32,2,128]{2,1,0:T(2,128)(2,1)S(1)} async-done(((bf16[32,2,128]{2,1,0:T(2,128)(2,1)}), bf16[32,2,128]{2,1,0:T(2,128)(2,1)S(1)}, u32[]{:S(2)}, u32[]{:S(2)}) %all-to-all-start.2) | async-done | bytes 16416 | tf_op jit(solution)/shard_map/all_to_all | solution.py:556
  113.8 1.6 %shard_map.83 = bf16[16,2,64]{2,1,0:T(2,128)(2,1)} custom-call(s32[32]{0:T(128)S(1)} %copy-done.1, bf16[32,2,128]{2,1,0:T(2,128)(2,1)S(1)} %all-to-all-done.2.got), custom_call_target="tpu_custom_call" | custom-call | bytes 100000 | tf_op jit(solution)/shard_map/pallas_call | solution.py:47
  (13 shorter events, 0.0 us)
Async XLA Ops:
  3.6 11.5 %all-to-all-start = ((bf16[16,3,2,1024]{3,2,1,0:T(2,128)(2,1)}), bf16[16,3,2,1024]{3,2,1,0:T(2,128)(2,1)S(1)}, u32[]{:S(2)}, u32[]{:S(2)}) async-start(bf16[16,3,2,1024]{3,2,1,0:T(2,128)(2,1)} %get-tuple-element.30), calls=%async_computation | async-start | bytes 393216 | tf_op jit(solution)/shard_map/all_to_all | solution.py:489
  8.6 6.5 %copy-start.1 = (s32[32]{0:T(128)S(1)}, s32[32]{0:T(128)}, u32[]{:S(2)}) copy-start(s32[32]{0:T(128)} %own.5) | copy-start | bytes 388
  8.6 6.5 %copy-start.2 = (s32[32]{0:T(128)S(1)}, s32[32]{0:T(128)}, u32[]{:S(2)}) copy-start(s32[32]{0:T(128)} %lens.1) | copy-start | bytes 388
  17.7 75.7 %all-to-all-start.1 = ((bf16[16,80,128]{2,1,0:T(8,128)(2,1)}), bf16[16,80,128]{2,1,0:T(8,128)(2,1)S(1)}, u32[]{:S(2)}, u32[]{:S(2)}) async-start(bf16[16,80,128]{2,1,0:T(8,128)(2,1)} %shard_map.81), calls=%async_computation.1 | async-start | bytes 655360 | tf_op jit(solution)/shard_map/all_to_all | solution.py:531
  28.7 51.2 %collective-permute-start = (bf16[576,256]{1,0:T(8,128)(2,1)S(1)}, bf16[576,256]{1,0:T(8,128)(2,1)S(1)}, u32[]{:S(2)}, u32[]{:S(2)}) collective-permute-start(bf16[576,256]{1,0:T(8,128)(2,1)S(1)} %get-tuple-element.19.msg), channel_id=1, source_target_pairs={{0,32},{32,0},{64,96},{96,64},{128,160},{160,128},{192,224},{224,1... | collective-permute-start | bytes 884744 | tf_op jit(solution)/shard_map/ppermute | solution.py:492
  31.8 14.0 %collective-permute-start.3 = (bf16[128,256]{1,0:T(8,128)(2,1)S(1)}, bf16[128,256]{1,0:T(8,128)(2,1)S(1)}, u32[]{:S(2)}, u32[]{:S(2)}) collective-permute-start(bf16[128,256]{1,0:T(8,128)(2,1)S(1)} %get-tuple-element.22), channel_id=1, source_target_pairs={{0,128},{32,160},{64,192},{96,224},{128,256},{160,288},{192,320},{... | collective-permute-start | bytes 196616 | tf_op jit(solution)/shard_map/ppermute | solution.py:495
  34.0 46.0 %collective-permute-start.1 = (bf16[512,128]{1,0:T(8,128)(2,1)S(1)}, bf16[512,128]{1,0:T(8,128)(2,1)S(1)}, u32[]{:S(2)}, u32[]{:S(2)}) collective-permute-start(bf16[512,128]{1,0:T(8,128)(2,1)S(1)} %get-tuple-element.18.qm), channel_id=1, source_target_pairs={{0,64},{32,96},{64,0},{96,32},{128,192},{160,224},{192,128},{224,1... | collective-permute-start | bytes 393224 | tf_op jit(solution)/shard_map/ppermute | solution.py:492
  45.8 15.3 %collective-permute-start.4 = (bf16[128,256]{1,0:T(8,128)(2,1)S(1)}, bf16[128,256]{1,0:T(8,128)(2,1)S(1)}, u32[]{:S(2)}, u32[]{:S(2)}) collective-permute-start(bf16[128,256]{1,0:T(8,128)(2,1)S(1)} %collective-permute-done.3.col1), channel_id=1, source_target_pairs={{128,256},{160,288},{192,320},{224,352},{256,384},{288,416},{320,4... | collective-permute-start | bytes 196616 | tf_op jit(solution)/shard_map/ppermute | solution.py:495
  61.0 18.9 %collective-permute-start.5 = (bf16[128,256]{1,0:T(8,128)(2,1)S(1)}, bf16[128,256]{1,0:T(8,128)(2,1)S(1)}, u32[]{:S(2)}, u32[]{:S(2)}) collective-permute-start(bf16[128,256]{1,0:T(8,128)(2,1)S(1)} %collective-permute-done.4.col2), channel_id=1, source_target_pairs={{256,384},{288,416},{320,448},{352,480},{257,385},{289,417},{321,4... | collective-permute-start | bytes 196616 | tf_op jit(solution)/shard_map/ppermute | solution.py:495
  62.3 17.6 %collective-permute-start.2 = (bf16[128,128]{1,0:T(8,128)(2,1)S(1)}, bf16[128,128]{1,0:T(8,128)(2,1)S(1)}, u32[]{:S(2)}, u32[]{:S(2)}) collective-permute-start(bf16[128,128]{1,0:T(8,128)(2,1)S(1)} %get-tuple-element.21), channel_id=1, source_target_pairs={{0,96},{32,64},{64,32},{96,0},{128,224},{160,192},{192,160},{224,1... | collective-permute-start | bytes 98312 | tf_op jit(solution)/shard_map/ppermute | solution.py:492
  79.9 13.4 %copy-start = (bf16[1024,256]{1,0:T(8,128)(2,1)S(1)}, bf16[1024,256]{1,0:T(8,128)(2,1)}, u32[]{:S(2)}) copy-start(bf16[1024,256]{1,0:T(8,128)(2,1)} %weight.1) | copy-start | bytes 1572868
  84.9 21.9 %collective-permute-start.7 = (bf16[544,128]{1,0:T(8,128)(2,1)S(1)}, bf16[544,128]{1,0:T(8,128)(2,1)S(1)}, u32[]{:S(2)}, u32[]{:S(2)}) collective-permute-start(bf16[544,128]{1,0:T(8,128)(2,1)S(1)} %get-tuple-element.28), channel_id=1, source_target_pairs={{0,64},{32,96},{64,0},{96,32},{128,192},{160,224},{192,128},{224,1... | collective-permute-start | bytes 417800 | tf_op jit(solution)/shard_map/ppermute | solution.py:492
  86.8 20.0 %collective-permute-start.6 = (bf16[144,128]{1,0:T(8,128)(2,1)S(1)}, bf16[144,128]{1,0:T(8,128)(2,1)S(1)}, u32[]{:S(2)}, u32[]{:S(2)}) collective-permute-start(bf16[144,128]{1,0:T(8,128)(2,1)S(1)} %get-tuple-element.27), channel_id=1, source_target_pairs={{0,32},{32,0},{64,96},{96,64},{128,160},{160,128},{192,224},{224,1... | collective-permute-start | bytes 110600 | tf_op jit(solution)/shard_map/ppermute | solution.py:492
  89.3 17.6 %collective-permute-start.8 = (bf16[144,128]{1,0:T(8,128)(2,1)S(1)}, bf16[144,128]{1,0:T(8,128)(2,1)S(1)}, u32[]{:S(2)}, u32[]{:S(2)}) collective-permute-start(bf16[144,128]{1,0:T(8,128)(2,1)S(1)} %get-tuple-element.29), channel_id=1, source_target_pairs={{0,96},{32,64},{64,32},{96,0},{128,224},{160,192},{192,160},{224,1... | collective-permute-start | bytes 110600 | tf_op jit(solution)/shard_map/ppermute | solution.py:492
  95.1 18.7 %all-to-all-start.2 = ((bf16[32,2,128]{2,1,0:T(2,128)(2,1)}), bf16[32,2,128]{2,1,0:T(2,128)(2,1)S(1)}, u32[]{:S(2)}, u32[]{:S(2)}) async-start(bf16[32,2,128]{2,1,0:T(2,128)(2,1)} %shard_map.82), calls=%async_computation.2 | async-start | bytes 32768 | tf_op jit(solution)/shard_map/all_to_all | solution.py:556

commit v5 on v4

--- a/solution.py
+++ b/solution.py
@@ -401,10 +401,10 @@
             st_s[pl.ds(8 * h + 2 * k, 2), :] = st[2 * h : 2 * h + 2]
     values = o_s[...].astype(BF16)
     turned = st_s[...].T
-    stats = jnp.concatenate([turned[:16, :], jnp.zeros((16, 64), F32)], axis=1).astype(BF16)
+    stats = jnp.concatenate([turned[:8, :], jnp.zeros((8, 64), F32)], axis=1).astype(BF16)
     for t in range(out.shape[0]):
         out[t, pl.ds(0, 64), :] = values
-        out[t, pl.ds(64, 16), :] = stats
+        out[t, pl.ds(64, 8), :] = stats
 
 
 def project_kernel(own, got, weight, out):
@@ -412,7 +412,7 @@
     count = got.shape[0]
     ms, ls = [], []
     for t in range(count):
-        st = got[t, pl.ds(64, 16), :].astype(F32)
+        st = got[t, pl.ds(64, 8), :].astype(F32)
         ms.append(st[0:1] + st[1:2] + st[2:3])
         ls.append(st[3:4] + st[4:5] + st[5:6])
     m = jnp.concatenate(ms, axis=0)
@@ -491,14 +491,15 @@
     def swap(x, bits):
         return lax.ppermute(x, "seq", [(i, i ^ bits) for i in range(16)])
 
-    def relay(x, first):
-        return lax.ppermute(x, "seq", [(i, i + 4) for i in range(first, 12)])
-
-    col1 = relay(far, 0)
+    def relay(x, first, stop, hop):
+        return lax.ppermute(x, "seq", [(i, i + hop) for i in range(first, stop)])
+
+    col1 = relay(far, 0, 12, 4)
+    col3 = relay(far, 0, 4, 12)
     got3 = swap(ask, 3)
     got2 = swap(qm, 2)
     got1 = swap(msg, 1)
-    col2 = relay(col1, 4)
+    col2 = relay(col1, 4, 12, 4)
     state = [pltpu.HBM((512, HD), F32)] * 2
     near_o, acc, ml, cache = call(
         near_kernel,
@@ -521,7 +522,7 @@
     )
     partial = call(
         cache_kernel,
-        shape((16, 80, HD)),
+        shape((16, 72, HD)),
         (owner_slot, prompt_lengths, arrived, cache),
         [sspec(), sspec(), vspec(), vspec()],
         [VMEM((64, HD), F32), VMEM((64, HD), F32)],
@@ -529,7 +530,6 @@
         nbytes=2000000,
     )
     parts = lax.all_to_all(partial, "seq", 0, 0, tiled=True)
-    col3 = relay(col2, 8)
     acc, ml, back1, back2, back3 = call(
         share_kernel,
         (*state, shape((144, HD)), shape((544, HD)), shape((144, HD))),

time: 116 us -> 106 us (0.914)
  the two profiles are of different devices: /device:TPU:289 before, /device:TPU:129 now
where the time goes in v5:
time: 106 us; the launch traced here: 105 us
  starting transfers between devices  62.1 us (59%)
  Pallas kernels  22.7 us (21%)
  waiting for transfers between devices  19.8 us (19%)
    pallas_call x7, Pallas kernels, call(): pl.pallas_call(body, out_shape=out_shape, in_specs=specs, out_specs=vspec...  22.7 us
    ppermute x6, starting transfers between devices, swap(): return lax.ppermute(x, 'seq', [(i, i ^ bits) for i in range(16)])  19.2 us
    ppermute x3, starting transfers between devices, relay(): return lax.ppermute(x, 'seq', [(i, i + hop) for i in range(first, stop)])  14.8 us
    all_to_all x1, starting transfers between devices, staged(): parts = lax.all_to_all(partial, 'seq', 0, 0, tiled=True)  13.3 us
    ppermute x3, waiting for transfers between devices, relay(): return lax.ppermute(x, 'seq', [(i, i + hop) for i in range(first, stop)])  11.5 us
    all_to_all x1, starting transfers between devices, staged(): results = lax.all_to_all(answers, ('head', 'req'), 0, 0, tiled=True)  9.79 us
    all_to_all x1, starting transfers between devices, staged(): arrived = lax.all_to_all(sent, 'req', 0, 0, tiled=True)  5.02 us
    ppermute x6, waiting for transfers between devices, swap(): return lax.ppermute(x, 'seq', [(i, i ^ bits) for i in range(16)])  4.54 us
  transfers between devices with their start and end apart: 12, of which 3 were waited for; matrix products, arithmetic and copies ran while one was open for 0% of the time, Pallas kernels for 15%

profile of v5, /device:TPU:129, one launch (start us, length us, event | category | flops | bytes accessed | tf_op | source)
XLA Modules:
  0.0 105.4 jit_solution(14055016900581197223)
XLA Ops:
  0.6 2.9 %shard_map.77 = (bf16[3,2048,128]{2,1,0:T(8,128)(2,1)S(1)}, bf16[16,3,2,1024]{3,2,1,0:T(2,128)(2,1)}, bf16[512,128]{1,0:T(8,128)(2,1)S(1)}, bf16[128,128]{1,0:T(...) custom-call(s32[32]{0:T(128)} %own.5, bf16[16,3,2,1024]{3,2,1,0:T(2,128)(2,1)} %dec.1, ...), custom_call_target="tpu_custom_call" | custom-call | bytes 4000000 | tf_op jit(solution)/shard_map/pallas_call | solution.py:47
  3.6 5.0 %all-to-all-start = ((bf16[16,3,2,1024]{3,2,1,0:T(2,128)(2,1)}), bf16[16,3,2,1024]{3,2,1,0:T(2,128)(2,1)S(1)}, u32[]{:S(2)}, u32[]{:S(2)}) async-start(bf16[16,3,2,1024]{3,2,1,0:T(2,128)(2,1)} %get-tuple-element.30), calls=%async_computation | async-start | bytes 393216 | tf_op jit(solution)/shard_map/all_to_all | solution.py:489
  8.6 6.5 %shard_map.78 = (bf16[2048,128]{1,0:T(8,128)(2,1)}, f32[512,128]{1,0:T(8,128)}, f32[512,128]{1,0:T(8,128)}, bf16[4,2,64,1024]{3,2,1,0:T(8,128)(2,1)S(1)}) custom-call(bf16[3,2048,128]{2,1,0:T(8,128)(2,1)S(1)} %get-tuple-element.17.raw, bf16[512,128]{1,0:T(8,128)(2,1)S(1)} %get-tuple-element.18.qm, bf16[576,256]{1,0:T(8,128)(2,1)S(1)} %get-tuple-element.19.msg, ...), custom_call_target="tpu_custom_call" | custom-call | flops 2000000000 | bytes 3000000 | tf_op jit(solution)/shard_map/pallas_call | solution.py:47
  15.1 2.6 %shard_map.81 = bf16[16,72,128]{2,1,0:T(8,128)(2,1)} custom-call(s32[32]{0:T(128)S(1)} %copy-done.1, s32[32]{0:T(128)S(1)} %copy-done.2, bf16[16,3,2,1024]{3,2,1,0:T(2,128)(2,1)S(1)} %all-to-all-done.arr, bf16[4,2,64,1024]{3,2,1,0:T(8,128)(2,1)S(1)} %get-tuple-element.31.cache), custom_call_target="tpu_custom_call" | custom-call | flops 100000000 | bytes 2000000 | tf_op jit(solution)/shard_map/pallas_call | solution.py:47
  17.7 13.3 %all-to-all-start.1 = ((bf16[16,72,128]{2,1,0:T(8,128)(2,1)}), bf16[16,72,128]{2,1,0:T(8,128)(2,1)S(1)}, u32[]{:S(2)}, u32[]{:S(2)}) async-start(bf16[16,72,128]{2,1,0:T(8,128)(2,1)} %shard_map.81), calls=%async_computation.1 | async-start | bytes 589824 | tf_op jit(solution)/shard_map/all_to_all | solution.py:532
  30.9 3.1 %collective-permute-start = (bf16[576,256]{1,0:T(8,128)(2,1)S(1)}, bf16[576,256]{1,0:T(8,128)(2,1)S(1)}, u32[]{:S(2)}, u32[]{:S(2)}) collective-permute-start(bf16[576,256]{1,0:T(8,128)(2,1)S(1)} %get-tuple-element.19.msg), channel_id=1, source_target_pairs={{0,32},{32,0},{64,96},{96,64},{128,160},{160,128},{192,224},{224,1... | collective-permute-start | bytes 884744 | tf_op jit(solution)/shard_map/ppermute | solution.py:492
  34.0 6.1 %collective-permute-start.3 = (bf16[128,256]{1,0:T(8,128)(2,1)S(1)}, bf16[128,256]{1,0:T(8,128)(2,1)S(1)}, u32[]{:S(2)}, u32[]{:S(2)}) collective-permute-start(bf16[128,256]{1,0:T(8,128)(2,1)S(1)} %get-tuple-element.22), channel_id=1, source_target_pairs={{0,128},{32,160},{64,192},{96,224},{128,256},{160,288},{192,320},{... | collective-permute-start | bytes 196616 | tf_op jit(solution)/shard_map/ppermute | solution.py:495
  40.1 2.2 %collective-permute-start.1 = (bf16[512,128]{1,0:T(8,128)(2,1)S(1)}, bf16[512,128]{1,0:T(8,128)(2,1)S(1)}, u32[]{:S(2)}, u32[]{:S(2)}) collective-permute-start(bf16[512,128]{1,0:T(8,128)(2,1)S(1)} %get-tuple-element.18.qm), channel_id=1, source_target_pairs={{0,64},{32,96},{64,0},{96,32},{128,192},{160,224},{192,128},{224,1... | collective-permute-start | bytes 393224 | tf_op jit(solution)/shard_map/ppermute | solution.py:492
  42.3 0.7 collective-permute-start.5
  43.0 11.5 %collective-permute-done.3.col1 = bf16[128,256]{1,0:T(8,128)(2,1)S(1)} collective-permute-done((bf16[128,256]{1,0:T(8,128)(2,1)S(1)}, bf16[128,256]{1,0:T(8,128)(2,1)S(1)}, u32[]{:S(2)}, u32[]{:S(2)}) %collective-permute-start.3) | collective-permute-done | bytes 65568 | tf_op jit(solution)/shard_map/ppermute | solution.py:495
  54.5 8.0 %collective-permute-start.4 = (bf16[128,256]{1,0:T(8,128)(2,1)S(1)}, bf16[128,256]{1,0:T(8,128)(2,1)S(1)}, u32[]{:S(2)}, u32[]{:S(2)}) collective-permute-start(bf16[128,256]{1,0:T(8,128)(2,1)S(1)} %collective-permute-done.3.col1), channel_id=1, source_target_pairs={{128,256},{160,288},{192,320},{224,352},{256,384},{288,416},{320,4... | collective-permute-start | bytes 196616 | tf_op jit(solution)/shard_map/ppermute | solution.py:495
  62.6 1.9 %collective-permute-start.2 = (bf16[128,128]{1,0:T(8,128)(2,1)S(1)}, bf16[128,128]{1,0:T(8,128)(2,1)S(1)}, u32[]{:S(2)}, u32[]{:S(2)}) collective-permute-start(bf16[128,128]{1,0:T(8,128)(2,1)S(1)} %get-tuple-element.21), channel_id=1, source_target_pairs={{0,96},{32,64},{64,32},{96,0},{128,224},{160,192},{192,160},{224,1... | collective-permute-start | bytes 98312 | tf_op jit(solution)/shard_map/ppermute | solution.py:492
  64.5 4.5 %collective-permute-done.2.got3 = bf16[128,128]{1,0:T(8,128)(2,1)S(1)} collective-permute-done((bf16[128,128]{1,0:T(8,128)(2,1)S(1)}, bf16[128,128]{1,0:T(8,128)(2,1)S(1)}, u32[]{:S(2)}, u32[]{:S(2)}) %collective-permute-start.2) | collective-permute-done | bytes 32800 | tf_op jit(solution)/shard_map/ppermute | solution.py:492
  69.0 0.0 collective-permute-done.5.col3
  69.0 0.0 copy-start
  69.0 4.2 %shard_map.79 = (f32[512,128]{1,0:T(8,128)}, f32[512,128]{1,0:T(8,128)}, bf16[144,128]{1,0:T(8,128)(2,1)S(1)}, bf16[544,128]{1,0:T(8,128)(2,1)S(1)}, bf16[144,128]{1,0:T(8,128)(2,1)S(1)}) custom-call(bf16[512,128]{1,0:T(8,128)(2,1)S(1)} %get-tuple-element.18.qm, bf16[576,256]{1,0:T(8,128)(2,1)S(1)} %get-tuple-element.19.msg, ...), custom_call_target="tpu_custom_call" | custom-call | flops 1000000000 | bytes 4000000 | tf_op jit(solution)/shard_map/pallas_call | solution.py:47
  73.3 5.1 %collective-permute-start.7 = (bf16[544,128]{1,0:T(8,128)(2,1)S(1)}, bf16[544,128]{1,0:T(8,128)(2,1)S(1)}, u32[]{:S(2)}, u32[]{:S(2)}) collective-permute-start(bf16[544,128]{1,0:T(8,128)(2,1)S(1)} %get-tuple-element.28), channel_id=1, source_target_pairs={{0,64},{32,96},{64,0},{96,32},{128,192},{160,224},{192,128},{224,1... | collective-permute-start | bytes 417800 | tf_op jit(solution)/shard_map/ppermute | solution.py:492
  78.4 2.9 %collective-permute-start.6 = (bf16[144,128]{1,0:T(8,128)(2,1)S(1)}, bf16[144,128]{1,0:T(8,128)(2,1)S(1)}, u32[]{:S(2)}, u32[]{:S(2)}) collective-permute-start(bf16[144,128]{1,0:T(8,128)(2,1)S(1)} %get-tuple-element.27), channel_id=1, source_target_pairs={{0,32},{32,0},{64,96},{96,64},{128,160},{160,128},{192,224},{224,1... | collective-permute-start | bytes 110600 | tf_op jit(solution)/shard_map/ppermute | solution.py:492
  81.3 4.0 %collective-permute-start.8 = (bf16[144,128]{1,0:T(8,128)(2,1)S(1)}, bf16[144,128]{1,0:T(8,128)(2,1)S(1)}, u32[]{:S(2)}, u32[]{:S(2)}) collective-permute-start(bf16[144,128]{1,0:T(8,128)(2,1)S(1)} %get-tuple-element.29), channel_id=1, source_target_pairs={{0,96},{32,64},{64,32},{96,0},{128,224},{160,192},{192,160},{224,1... | collective-permute-start | bytes 110600 | tf_op jit(solution)/shard_map/ppermute | solution.py:492
  85.3 1.8 %shard_map.82 = bf16[32,2,128]{2,1,0:T(2,128)(2,1)} custom-call(s32[32]{0:T(128)S(1)} %copy-done.1, bf16[16,72,128]{2,1,0:T(8,128)(2,1)S(1)} %all-to-all-done.1.got, bf16[1024,256]{1,0:T(8,128)(2,1)S(1)} %copy-done), custom_call_target="tpu_custom_call" | custom-call | flops 10000000 | bytes 1000000 | tf_op jit(solution)/shard_map/pallas_call | solution.py:47
  87.1 9.8 %all-to-all-start.2 = ((bf16[32,2,128]{2,1,0:T(2,128)(2,1)}), bf16[32,2,128]{2,1,0:T(2,128)(2,1)S(1)}, u32[]{:S(2)}, u32[]{:S(2)}) async-start(bf16[32,2,128]{2,1,0:T(2,128)(2,1)} %shard_map.82), calls=%async_computation.2 | async-start | bytes 32768 | tf_op jit(solution)/shard_map/all_to_all | solution.py:556
  96.9 3.2 %shard_map.80 = bf16[2048,128]{1,0:T(8,128)(2,1)} custom-call(bf16[2048,128]{1,0:T(8,128)(2,1)} %get-tuple-element.20.near_h, f32[512,128]{1,0:T(8,128)} %get-tuple-element.25.acc_h, f32[512,128]{1,0:T(8,128)} %get-tuple-element.26.ml_h, bf16[144,128]{1,0:T(8,128)(2,1)S(1)} %collective-permute-done.6.back1, ...), custom_call_target="tpu_custom_call" | custom-call | flops 100000000 | bytes 4000000 | tf_op jit(solution)/shard_map/pallas_call | solution.py:47
  100.1 3.7 %all-to-all-done.2.got = bf16[32,2,128]{2,1,0:T(2,128)(2,1)S(1)} async-done(((bf16[32,2,128]{2,1,0:T(2,128)(2,1)}), bf16[32,2,128]{2,1,0:T(2,128)(2,1)S(1)}, u32[]{:S(2)}, u32[]{:S(2)}) %all-to-all-start.2) | async-done | bytes 16416 | tf_op jit(solution)/shard_map/all_to_all | solution.py:556
  103.9 1.6 %shard_map.83 = bf16[16,2,64]{2,1,0:T(2,128)(2,1)} custom-call(s32[32]{0:T(128)S(1)} %copy-done.1, bf16[32,2,128]{2,1,0:T(2,128)(2,1)S(1)} %all-to-all-done.2.got), custom_call_target="tpu_custom_call" | custom-call | bytes 100000 | tf_op jit(solution)/shard_map/pallas_call | solution.py:47
  (13 shorter events, 0.0 us)
Async XLA Ops:
  3.6 11.5 %all-to-all-start = ((bf16[16,3,2,1024]{3,2,1,0:T(2,128)(2,1)}), bf16[16,3,2,1024]{3,2,1,0:T(2,128)(2,1)S(1)}, u32[]{:S(2)}, u32[]{:S(2)}) async-start(bf16[16,3,2,1024]{3,2,1,0:T(2,128)(2,1)} %get-tuple-element.30), calls=%async_computation | async-start | bytes 393216 | tf_op jit(solution)/shard_map/all_to_all | solution.py:489
  8.6 6.5 %copy-start.1 = (s32[32]{0:T(128)S(1)}, s32[32]{0:T(128)}, u32[]{:S(2)}) copy-start(s32[32]{0:T(128)} %own.5) | copy-start | bytes 388
  8.6 6.5 %copy-start.2 = (s32[32]{0:T(128)S(1)}, s32[32]{0:T(128)}, u32[]{:S(2)}) copy-start(s32[32]{0:T(128)} %lens.1) | copy-start | bytes 388
  17.7 67.7 %all-to-all-start.1 = ((bf16[16,72,128]{2,1,0:T(8,128)(2,1)}), bf16[16,72,128]{2,1,0:T(8,128)(2,1)S(1)}, u32[]{:S(2)}, u32[]{:S(2)}) async-start(bf16[16,72,128]{2,1,0:T(8,128)(2,1)} %shard_map.81), calls=%async_computation.1 | async-start | bytes 589824 | tf_op jit(solution)/shard_map/all_to_all | solution.py:532
  30.9 38.1 %collective-permute-start = (bf16[576,256]{1,0:T(8,128)(2,1)S(1)}, bf16[576,256]{1,0:T(8,128)(2,1)S(1)}, u32[]{:S(2)}, u32[]{:S(2)}) collective-permute-start(bf16[576,256]{1,0:T(8,128)(2,1)S(1)} %get-tuple-element.19.msg), channel_id=1, source_target_pairs={{0,32},{32,0},{64,96},{96,64},{128,160},{160,128},{192,224},{224,1... | collective-permute-start | bytes 884744 | tf_op jit(solution)/shard_map/ppermute | solution.py:492
  34.0 20.5 %collective-permute-start.3 = (bf16[128,256]{1,0:T(8,128)(2,1)S(1)}, bf16[128,256]{1,0:T(8,128)(2,1)S(1)}, u32[]{:S(2)}, u32[]{:S(2)}) collective-permute-start(bf16[128,256]{1,0:T(8,128)(2,1)S(1)} %get-tuple-element.22), channel_id=1, source_target_pairs={{0,128},{32,160},{64,192},{96,224},{128,256},{160,288},{192,320},{... | collective-permute-start | bytes 196616 | tf_op jit(solution)/shard_map/ppermute | solution.py:495
  40.1 28.9 %collective-permute-start.1 = (bf16[512,128]{1,0:T(8,128)(2,1)S(1)}, bf16[512,128]{1,0:T(8,128)(2,1)S(1)}, u32[]{:S(2)}, u32[]{:S(2)}) collective-permute-start(bf16[512,128]{1,0:T(8,128)(2,1)S(1)} %get-tuple-element.18.qm), channel_id=1, source_target_pairs={{0,64},{32,96},{64,0},{96,32},{128,192},{160,224},{192,128},{224,1... | collective-permute-start | bytes 393224 | tf_op jit(solution)/shard_map/ppermute | solution.py:492
  42.3 26.7 %collective-permute-start.5 = (bf16[128,256]{1,0:T(8,128)(2,1)S(1)}, bf16[128,256]{1,0:T(8,128)(2,1)S(1)}, u32[]{:S(2)}, u32[]{:S(2)}) collective-permute-start(bf16[128,256]{1,0:T(8,128)(2,1)S(1)} %get-tuple-element.22), channel_id=1, source_target_pairs={{0,384},{32,416},{64,448},{96,480},{1,385},{33,417},{65,449},{97,4... | collective-permute-start | bytes 196616 | tf_op jit(solution)/shard_map/ppermute | solution.py:495
  54.5 14.5 %collective-permute-start.4 = (bf16[128,256]{1,0:T(8,128)(2,1)S(1)}, bf16[128,256]{1,0:T(8,128)(2,1)S(1)}, u32[]{:S(2)}, u32[]{:S(2)}) collective-permute-start(bf16[128,256]{1,0:T(8,128)(2,1)S(1)} %collective-permute-done.3.col1), channel_id=1, source_target_pairs={{128,256},{160,288},{192,320},{224,352},{256,384},{288,416},{320,4... | collective-permute-start | bytes 196616 | tf_op jit(solution)/shard_map/ppermute | solution.py:495
  62.6 6.5 %collective-permute-start.2 = (bf16[128,128]{1,0:T(8,128)(2,1)S(1)}, bf16[128,128]{1,0:T(8,128)(2,1)S(1)}, u32[]{:S(2)}, u32[]{:S(2)}) collective-permute-start(bf16[128,128]{1,0:T(8,128)(2,1)S(1)} %get-tuple-element.21), channel_id=1, source_target_pairs={{0,96},{32,64},{64,32},{96,0},{128,224},{160,192},{192,160},{224,1... | collective-permute-start | bytes 98312 | tf_op jit(solution)/shard_map/ppermute | solution.py:492
  69.0 16.3 %copy-start = (bf16[1024,256]{1,0:T(8,128)(2,1)S(1)}, bf16[1024,256]{1,0:T(8,128)(2,1)}, u32[]{:S(2)}) copy-start(bf16[1024,256]{1,0:T(8,128)(2,1)} %weight.1) | copy-start | bytes 1572868
  73.3 23.6 %collective-permute-start.7 = (bf16[544,128]{1,0:T(8,128)(2,1)S(1)}, bf16[544,128]{1,0:T(8,128)(2,1)S(1)}, u32[]{:S(2)}, u32[]{:S(2)}) collective-permute-start(bf16[544,128]{1,0:T(8,128)(2,1)S(1)} %get-tuple-element.28), channel_id=1, source_target_pairs={{0,64},{32,96},{64,0},{96,32},{128,192},{160,224},{192,128},{224,1... | collective-permute-start | bytes 417800 | tf_op jit(solution)/shard_map/ppermute | solution.py:492
  78.4 18.5 %collective-permute-start.6 = (bf16[144,128]{1,0:T(8,128)(2,1)S(1)}, bf16[144,128]{1,0:T(8,128)(2,1)S(1)}, u32[]{:S(2)}, u32[]{:S(2)}) collective-permute-start(bf16[144,128]{1,0:T(8,128)(2,1)S(1)} %get-tuple-element.27), channel_id=1, source_target_pairs={{0,32},{32,0},{64,96},{96,64},{128,160},{160,128},{192,224},{224,1... | collective-permute-start | bytes 110600 | tf_op jit(solution)/shard_map/ppermute | solution.py:492
  81.3 15.6 %collective-permute-start.8 = (bf16[144,128]{1,0:T(8,128)(2,1)S(1)}, bf16[144,128]{1,0:T(8,128)(2,1)S(1)}, u32[]{:S(2)}, u32[]{:S(2)}) collective-permute-start(bf16[144,128]{1,0:T(8,128)(2,1)S(1)} %get-tuple-element.29), channel_id=1, source_target_pairs={{0,96},{32,64},{64,32},{96,0},{128,224},{160,192},{192,160},{224,1... | collective-permute-start | bytes 110600 | tf_op jit(solution)/shard_map/ppermute | solution.py:492
  87.1 16.8 %all-to-all-start.2 = ((bf16[32,2,128]{2,1,0:T(2,128)(2,1)}), bf16[32,2,128]{2,1,0:T(2,128)(2,1)S(1)}, u32[]{:S(2)}, u32[]{:S(2)}) async-start(bf16[32,2,128]{2,1,0:T(2,128)(2,1)} %shard_map.82), calls=%async_computation.2 | async-start | bytes 32768 | tf_op jit(solution)/shard_map/all_to_all | solution.py:556

commit v6 on v5

--- a/solution.py
+++ b/solution.py
@@ -75,7 +75,7 @@
 
 
 def start_kernel(
-    own_h, dec, qkv, raw, sent, qm, ask, msg, far, own, wide, sem, part_sem, own_sem
+    own_h, dec, qkv, sent, q4, kvm_h, far, kvm, raw, own, wide, sem, part_sem, own_sem
 ):
     own_copy = pltpu.make_async_copy(own_h, own, own_sem)
     own_copy.start()
@@ -108,18 +108,18 @@
             got = wide[pl.ds(start, rows // 16, stride=16), :].astype(BF16)
             at = pl.ds(128 * c, 128)
             if part == 0:
-                qm[at, :] = got
-                if c == 0:
-                    ask[...] = got
-                    msg[pl.ds(512, 64), pl.ds(0, HD)] = got[:64]
-                    msg[pl.ds(512, 64), pl.ds(HD, HD)] = got[64:]
+                for copy in range(4):
+                    q4[copy, at, :] = got
             else:
                 lanes = pl.ds(HD * (part - 1), HD)
-                msg[at, lanes] = got
+                kvm[at, lanes] = got
                 if c == 0:
                     far[:, lanes] = got
+    keep = pltpu.make_async_copy(kvm, kvm_h, own_sem)
+    keep.start()
     for cp in copies:
         cp.wait()
+    keep.wait()
 
 
 def both(m, l):
@@ -159,26 +159,22 @@
 
 
 def near_kernel(
-    raw, qm, msg, cache_h, near_h, acc_h, ml_h, cache,
-    acc_s, ml_s, near_o, acc_o, ml_o, sem, out_sem,
+    raw, q4, kvm_h, col1, cache_h, near_o, acc_o, ml_o, cache, pass_on,
+    kvm, acc_s, ml_s, sem,
 ):
     rows = raw.shape[1]
     step = 256
-    fetch = pltpu.make_async_copy(cache_h, cache, sem.at[2])
+    load = pltpu.make_async_copy(kvm_h, kvm, sem.at[0])
+    load.start()
+    fetch = pltpu.make_async_copy(cache_h, cache, sem.at[1])
     fetch.start()
-    copies = []
+    pass_on[pl.ds(128, 128), :] = col1[...]
     inner = lax.div(lax.rem(head_id(), 16), 4)
 
     def order(dims, dim):
         a = lax.broadcasted_iota(jnp.int32, dims, dim)
         return 4 * (a & 127) + ((lax.shift_right_logical(a, 7) + inner) & 3)
 
-    mine = pl.ds(0, 512)
-    s = dot_t(qm[...], msg[mine, pl.ds(0, HD)])
-    s = jnp.where(order((1, 512), 1) <= order((512, 1), 0), s, NEG)
-    m, l, acc = softmax_once([(s, msg[mine, pl.ds(HD, HD)])], True)
-    acc_o[...] = acc
-    ml_o[...] = both(m, l)
     tri = lax.broadcasted_iota(jnp.int32, (step, step), 1) <= lax.broadcasted_iota(
         jnp.int32, (step, step), 0
     )
@@ -191,23 +187,21 @@
             parts.append((dot_t(q, raw[1, before, :]), raw[2, before, :]))
         m, l, acc = softmax_once(parts)
         near_o[at, :] = (acc / l).astype(BF16)
-        cp = pltpu.make_async_copy(near_o.at[at], near_h.at[at], out_sem.at[b])
-        cp.start()
-        copies.append(cp)
         acc_s[at, :] = acc
         ml_s[at, :] = both(m, l)
+    load.wait()
+    pass_on[pl.ds(0, 128), :] = kvm[pl.ds(0, 128), :]
+    s = dot_t(q4[0], kvm[:, pl.ds(0, HD)])
+    s = jnp.where(order((1, 512), 1) <= order((512, 1), 0), s, NEG)
+    m, l, acc = softmax_once([(s, kvm[:, pl.ds(HD, HD)])], True)
+    acc_o[...] = acc
+    ml_o[...] = both(m, l)
     for c in range(4):
         at = pl.ds(128 * c, 128)
         pick = pl.ds(class_residue(c), 128, stride=16)
         m, l, acc = combine([term(acc_s, ml_s, pick), term(acc_o, ml_o, at)])
         acc_o[at, :] = acc
         ml_o[at, :] = both(m, l)
-    for i, (src, dst) in enumerate(((acc_o, acc_h), (ml_o, ml_h))):
-        cp = pltpu.make_async_copy(src, dst, sem.at[i])
-        cp.start()
-        copies.append(cp)
-    for cp in copies:
-        cp.wait()
     fetch.wait()
 
 
@@ -232,18 +226,14 @@
 
 
 def share_kernel(
-    qm, msg, got1, got2, got3, col1, col2, col3, acc_h, ml_h,
-    acc_o, ml_o, back1, back2, back3,
-    acc_n, ml_n, acc_m, ml_m, acc_2, ml_2, acc_f, ml_f, qf, kf, sem,
+    qs, kvm_h, col1, col2, acc_o, ml_o, back1, back2, back3,
+    kvm, acc_1, ml_1, acc_2, ml_2, acc_3, ml_3, acc_f, ml_f, qf, kf, sem,
 ):
+    load = pltpu.make_async_copy(kvm_h, kvm, sem)
+    load.start()
     z = lax.axis_index("seq")
     local = lax.rem(z, 4)
     group = lax.div(z, 4)
-    load_acc = pltpu.make_async_copy(acc_h, acc_n, sem.at[0])
-    load_ml = pltpu.make_async_copy(ml_h, ml_n, sem.at[1])
-    load_acc.start()
-    load_ml.start()
-    one = pl.ds(0, 512)
     head = pl.ds(0, 128)
     tail = pl.ds(128, 384)
     keys, values = pl.ds(0, HD), pl.ds(HD, HD)
@@ -260,92 +250,58 @@
             acc_r[...] = jnp.zeros((512, HD), F32)
             ml_r[...] = both(jnp.full((512, 1), NEG, F32), jnp.zeros((512, 1), F32))
 
-    def other_pair():
-        q = got2[...]
-        return softmax_once(
-            [
-                (dot_t(q, msg[one, keys]), msg[one, values]),
-                (dot_t(q, got1[one, keys]), got1[one, values]),
-            ],
-            True,
+    def far_level():
+        for x in range(4):
+            qf[pl.ds(128 * x, 128), :] = qs[local ^ x, head, :]
+        kf[head, :] = col1[...]
+        kf[pl.ds(128, 256), :] = col2[...]
+        s = dot_t(qf[...], kf[:, keys])
+        block = lax.shift_right_logical(lax.broadcasted_iota(jnp.int32, (1, 384), 1), 7)
+        odd = (group & 1) == 1
+        ok = jnp.where(block == 1, odd.astype(jnp.int32), (group >= 2).astype(jnp.int32))
+        return softmax_once([(jnp.where(ok > 0, s, NEG), kf[:, values])])
+
+    parts = ((1, acc_1, ml_1, back1), (2, acc_2, ml_2, back2), (3, acc_3, ml_3, back3))
+    fill(group > 0, acc_f, ml_f, far_level)
+    load.wait()
+    for x, acc_r, ml_r, _ in parts:
+        fill(
+            (local ^ x) > local,
+            acc_r,
+            ml_r,
+            lambda x=x: softmax_once(
+                [(dot_t(qs[local ^ x], kvm[:, keys]), kvm[:, values])], True
+            ),
         )
-
-    def own_pair():
-        return softmax_once([(dot_t(qm[...], got1[one, keys]), got1[one, values])], True)
-
-    def far_level():
-        half = pl.ds(512, 64)
-        qf[pl.ds(0, 128), :] = qm[head, :]
-        qf[pl.ds(128, 128), :] = got2[head, :]
-        qf[pl.ds(256, 64), :] = got1[half, keys]
-        qf[pl.ds(320, 64), :] = got1[half, values]
-        qf[pl.ds(384, 128), :] = got3[...]
-        for i, col in enumerate((col1, col2, col3)):
-            kf[pl.ds(128 * i, 128), :] = col[...]
-        s = dot_t(qf[...], kf[:, keys])
-        at = lax.broadcasted_iota(jnp.int32, (1, 384), 1)
-        return softmax_once([(jnp.where(at < 128 * group, s, NEG), kf[:, values])])
-
-    fill(local < 2, acc_2, ml_2, other_pair)
-    fill((local & 1) == 1, acc_m, ml_m, own_pair)
-    fill(group > 0, acc_f, ml_f, far_level)
 
     def give(out, terms, rows):
         m, l, acc = combine(terms)
         out[rows, :] = (acc / jnp.where(l > 0.0, l, 1.0)).astype(BF16)
         return m, l
 
-    far2 = term(acc_f, ml_f, pl.ds(128, 128))
-    m_a, l_a = give(back2, [term(acc_2, ml_2, head), far2], head)
-    m_b, l_b = give(back2, [term(acc_2, ml_2, tail)], tail)
-    back2[pl.ds(512, 32), :] = pack(
-        jnp.concatenate([m_a, m_b], axis=0), jnp.concatenate([l_a, l_b], axis=0)
-    )
-    for out, first in ((back1, 256), (back3, 384)):
-        m, l = give(out, [term(acc_f, ml_f, pl.ds(first, 128))], head)
-        out[pl.ds(128, 16), :] = pack(m, l)
-    load_acc.wait()
-    load_ml.wait()
-    for at in (head, tail):
-        terms = [term(acc_n, ml_n, at), term(acc_m, ml_m, at)]
-        if at is head:
-            terms.append(term(acc_f, ml_f, head))
-        m, l, acc = combine(terms)
-        acc_n[at, :] = acc
-        ml_n[at, :] = both(m, l)
-    save_acc = pltpu.make_async_copy(acc_n, acc_o, sem.at[0])
-    save_ml = pltpu.make_async_copy(ml_n, ml_o, sem.at[1])
-    save_acc.start()
-    save_ml.start()
-    save_acc.wait()
-    save_ml.wait()
-
-
-def merge_kernel(near_h, acc_h, ml_h, back1, back2, back3, out, near, acc, ml, wide, sem):
-    copies = [
-        pltpu.make_async_copy(src, dst, sem.at[i])
-        for i, (src, dst) in enumerate(((near_h, near), (acc_h, acc), (ml_h, ml)))
-    ]
-    for cp in copies:
-        cp.start()
-    for cp in copies:
-        cp.wait()
+    for x, acc_r, ml_r, back in parts:
+        far = term(acc_f, ml_f, pl.ds(128 * x, 128))
+        m_a, l_a = give(back, [term(acc_r, ml_r, head), far], head)
+        m_b, l_b = give(back, [term(acc_r, ml_r, tail)], tail)
+        back[pl.ds(512, 32), :] = pack(
+            jnp.concatenate([m_a, m_b], axis=0), jnp.concatenate([l_a, l_b], axis=0)
+        )
+    acc_o[...] = acc_f[head, :]
+    ml_o[...] = ml_f[head, :]
+
+
+def merge_kernel(near, acc, ml, acc_f, ml_f, back1, back2, back3, out, wide):
     wide[...] = near[...].astype(F32)
     for c in range(4):
         at = pl.ds(128 * c, 128)
-        terms = [(ml[at, :][:, 0:1], ml[at, :][:, 1:2], acc[at, :])]
-        for part, rows, stat in ((back2, 128 * c, 512 + 8 * c), (back1, 0, 128), (back3, 0, 128)):
-            if c and part is not back2:
-                continue
-            pm, plen = unpack(part[pl.ds(stat // 16 * 16, 16), :][stat % 16 : stat % 16 + 8])
-            terms.append((pm, plen, part[pl.ds(rows, 128), :].astype(F32) * plen))
-        top = functools.reduce(jnp.maximum, [t[0] for t in terms])
-        total = 0.0
-        length = 0.0
-        for tm, tl, ta in terms:
-            w = jnp.exp2((tm - top) * EXP_SCALE)
-            length = length + tl * w
-            total = total + ta * w
+        terms = [term(acc, ml, at)]
+        if c == 0:
+            terms.append(term(acc_f, ml_f, at))
+        for part in (back1, back2, back3):
+            stat = part[pl.ds(512 + 16 * (c // 2), 16), :][8 * (c % 2) : 8 * (c % 2) + 8]
+            m, l = unpack(stat)
+            terms.append((m, l, part[at, :].astype(F32) * l))
+        _, length, total = combine(terms)
         wide[pl.ds(class_residue(c), 128, stride=16), :] = total / length
     out[...] = wide[...].astype(BF16)
 
@@ -465,19 +421,19 @@
 
 def staged(pre_qkv, cache_kv, dec_new, out_weight, owner_slot, prompt_lengths):
     qkv = jnp.swapaxes(pre_qkv, 0, 1)
-    raw, sent, qm, ask, msg, far = call(
+    sent, q4, kvm, far = call(
         start_kernel,
         (
-            shape((3, 2048, HD)),
             shape(dec_new.shape),
-            shape((512, HD)),
-            shape((128, HD)),
-            shape((576, 2 * HD)),
+            shape((4, 512, HD)),
+            pltpu.HBM((512, 2 * HD), BF16),
             shape((128, 2 * HD)),
         ),
         (far_memory(owner_slot), far_memory(dec_new), far_memory(qkv)),
         [hspec(), hspec(), hspec()],
         [
+            VMEM((512, 2 * HD), BF16),
+            VMEM((3, 2048, HD), BF16),
             SMEM((32,), jnp.int32),
             VMEM((2048, HD), F32),
             pltpu.SemaphoreType.DMA((16,)),
@@ -485,40 +441,39 @@
             pltpu.SemaphoreType.DMA,
         ],
         nbytes=4000000,
+        outs=[vspec(), vspec(), hspec(), vspec()],
     )
     arrived = lax.all_to_all(sent, "req", 0, 0, tiled=True)
+    rows4 = range(4)
+    col1 = lax.ppermute(far, "seq", [(i, i + 12) for i in rows4] + [(i + 4, i + 8) for i in rows4])
+    groups = [[4 * g + i for i in rows4] for g in rows4]
+    qs = lax.all_to_all(q4, "seq", 0, 0, axis_index_groups=groups, tiled=True)
 
     def swap(x, bits):
         return lax.ppermute(x, "seq", [(i, i ^ bits) for i in range(16)])
 
-    def relay(x, first, stop, hop):
-        return lax.ppermute(x, "seq", [(i, i + hop) for i in range(first, stop)])
-
-    col1 = relay(far, 0, 12, 4)
-    col3 = relay(far, 0, 4, 12)
-    got3 = swap(ask, 3)
-    got2 = swap(qm, 2)
-    got1 = swap(msg, 1)
-    col2 = relay(col1, 4, 12, 4)
-    state = [pltpu.HBM((512, HD), F32)] * 2
-    near_o, acc, ml, cache = call(
+    state = [shape((512, HD), F32)] * 2
+    near_o, acc, ml, cache, pass_on = call(
         near_kernel,
-        (pltpu.HBM((2048, HD), BF16), *state, shape(cache_kv.shape)),
-        (raw, qm, msg, far_memory(cache_kv)),
-        [vspec(), vspec(), vspec(), hspec()],
+        (shape((2048, HD)), *state, shape(cache_kv.shape), shape((256, 2 * HD))),
+        (qkv, q4, far_memory(kvm), col1, far_memory(cache_kv)),
+        [vspec(), vspec(), hspec(), vspec(), hspec()],
         [
+            VMEM((512, 2 * HD), BF16),
             VMEM((2048, HD), F32),
             VMEM((2048, HD), F32),
-            VMEM((2048, HD), BF16),
-            VMEM((512, HD), F32),
-            VMEM((512, HD), F32),
-            pltpu.SemaphoreType.DMA((8,)),
-            pltpu.SemaphoreType.DMA((8,)),
+            pltpu.SemaphoreType.DMA((2,)),
         ],
         flops=2 * 10**9,
         nbytes=3000000,
         trans=2 * 10**6,
-        outs=[hspec(), hspec(), hspec(), vspec()],
+    )
+    col2 = lax.ppermute(
+        pass_on,
+        "seq",
+        [(i + 8, i + 12) for i in rows4]
+        + [(i + 12, i + 8) for i in rows4]
+        + [(i, i + 4) for i in rows4],
     )
     partial = call(
         cache_kernel,
@@ -530,17 +485,17 @@
         nbytes=2000000,
     )
     parts = lax.all_to_all(partial, "seq", 0, 0, tiled=True)
-    acc, ml, back1, back2, back3 = call(
+    acc_f, ml_f, back1, back2, back3 = call(
         share_kernel,
-        (*state, shape((144, HD)), shape((544, HD)), shape((144, HD))),
-        (qm, msg, got1, got2, got3, col1, col2, col3, far_memory(acc), far_memory(ml)),
-        [vspec()] * 8 + [hspec()] * 2,
-        [VMEM((512, HD), F32)] * 8
-        + [VMEM((512, HD), BF16), VMEM((384, 2 * HD), BF16), pltpu.SemaphoreType.DMA((2,))],
+        (*[shape((128, HD), F32)] * 2, *[shape((544, HD))] * 3),
+        (qs, far_memory(kvm), col1, col2),
+        [vspec(), hspec(), vspec(), vspec()],
+        [VMEM((512, 2 * HD), BF16)]
+        + [VMEM((512, HD), F32)] * 8
+        + [VMEM((512, HD), BF16), VMEM((384, 2 * HD), BF16), pltpu.SemaphoreType.DMA],
         flops=10**9,
         nbytes=4000000,
         trans=10**6,
-        outs=[hspec()] * 2 + [vspec()] * 3,
     )
     back1 = swap(back1, 1)
     back3 = swap(back3, 3)
@@ -557,15 +512,9 @@
     prefill_out = call(
         merge_kernel,
         shape((2048, HD)),
-        (far_memory(near_o), far_memory(acc), far_memory(ml), back1, back2, back3),
-        [hspec()] * 3 + [vspec()] * 3,
-        [
-            VMEM((2048, HD), BF16),
-            VMEM((512, HD), F32),
-            VMEM((512, HD), F32),
-            VMEM((2048, HD), F32),
-            pltpu.SemaphoreType.DMA((3,)),
-        ],
+        (near_o, acc, ml, acc_f, ml_f, back1, back2, back3),
+        [vspec()] * 8,
+        [VMEM((2048, HD), F32)],
         flops=10**8,
         nbytes=4000000,
     )

time: 106 us -> 113 us (1.066)
  the two profiles are of different devices: /device:TPU:129 before, /device:TPU:1 now
where the time goes in v6:
time: 113 us
  starting transfers between devices  51.4 us (45%)
  blocking collectives  28.4 us (25%)
  Pallas kernels  23.3 us (21%)
  waiting for transfers between devices  9.08 us (8%)
    pallas_call x7, Pallas kernels, call(): pl.pallas_call(body, out_shape=out_shape, in_specs=specs, out_specs=vspec...  23.3 us
    ppermute x3, starting transfers between devices, swap(): return lax.ppermute(x, 'seq', [(i, i ^ bits) for i in range(16)])  16 us
    all_to_all x1, starting transfers between devices, staged(): parts = lax.all_to_all(partial, 'seq', 0, 0, tiled=True)  15.8 us
    all_to_all x1, blocking collectives, staged(): arrived = lax.all_to_all(sent, 'req', 0, 0, tiled=True)  15.1 us
    all_to_all x1, blocking collectives, staged(): results = lax.all_to_all(answers, ('head', 'req'), 0, 0, tiled=True)  13.3 us
    ppermute x1, starting transfers between devices, staged(): lax.ppermute(far, 'seq', [(i, i + 12) for i in rows4] + [(i + 4, i + 8) f...  8.81 us
    ppermute x1, waiting for transfers between devices, staged(): lax.ppermute(pass_on, 'seq', [(i + 8, i + 12) for i in rows4] + [(i + 12,...  7.76 us
    ppermute x1, starting transfers between devices, staged(): lax.ppermute(pass_on, 'seq', [(i + 8, i + 12) for i in rows4] + [(i + 12,...  7.31 us
  transfers between devices with their start and end apart: 7, of which 2 were waited for; matrix products, arithmetic and copies ran while one was open for 0% of the time, Pallas kernels for 15%

profile of v6, /device:TPU:1, one launch (start us, length us, event | category | flops | bytes accessed | tf_op | source)
XLA Modules:
  0.0 112.9 jit_solution(17594688242168277227)
XLA Ops:
  0.6 3.4 %shard_map.77 = (bf16[16,3,2,1024]{3,2,1,0:T(2,128)(2,1)S(1)}, bf16[4,512,128]{2,1,0:T(8,128)(2,1)}, bf16[512,256]{1,0:T(8,128)(2,1)}, bf16[128,256]{1,0:T(8,128)(2,1)S(1)}) custom-call(s32[32]{0:T(128)} %own.5, bf16[16,3,2,1024]{3,2,1,0:T(2,128)(2,1)} %dec.1, bf16[3,2048,128]{2,1,0:T(8,128)(2,1)} %bitcast.1), custom_call_target="tpu_custom_call" | custom-call | bytes 4000000 | tf_op jit(solution)/shard_map/pallas_call | solution.py:47
  4.1 15.1 %all_to_all.20.arr = bf16[16,3,2,1024]{3,2,1,0:T(2,128)(2,1)S(1)} all-to-all(bf16[16,3,2,1024]{3,2,1,0:T(2,128)(2,1)S(1)} %get-tuple-element.28), channel_id=1, replica_groups=mesh['seq'=16,'head'=4,'req'=8] {'req'}, dimensions={0} | all-to-all | bytes 393216 | tf_op jit(solution)/shard_map/all_to_all | solution.py:446
  19.2 3.5 %all-to-all-start = ((bf16[4,512,128]{2,1,0:T(8,128)(2,1)}), bf16[4,512,128]{2,1,0:T(8,128)(2,1)S(1)}, u32[]{:S(2)}, u32[]{:S(2)}) async-start(bf16[4,512,128]{2,1,0:T(8,128)(2,1)} %get-tuple-element.16.q4), calls=%async_computation | async-start | bytes 1048576 | tf_op jit(solution)/shard_map/all_to_all | solution.py:450
  22.7 8.8 %collective-permute-start = (bf16[128,256]{1,0:T(8,128)(2,1)S(1)}, bf16[128,256]{1,0:T(8,128)(2,1)S(1)}, u32[]{:S(2)}, u32[]{:S(2)}) collective-permute-start(bf16[128,256]{1,0:T(8,128)(2,1)S(1)} %get-tuple-element.18), channel_id=1, source_target_pairs={{0,384},{32,416},{64,448},{96,480},{128,256},{160,288},{192,320},{... | collective-permute-start | bytes 196616 | tf_op jit(solution)/shard_map/ppermute | solution.py:448
  31.5 1.3 %collective-permute-done.col1 = bf16[128,256]{1,0:T(8,128)(2,1)S(1)} collective-permute-done((bf16[128,256]{1,0:T(8,128)(2,1)S(1)}, bf16[128,256]{1,0:T(8,128)(2,1)S(1)}, u32[]{:S(2)}, u32[]{:S(2)}) %collective-permute-start) | collective-permute-done | bytes 65568 | tf_op jit(solution)/shard_map/ppermute | solution.py:448
  32.8 7.0 %shard_map.78 = (bf16[2048,128]{1,0:T(8,128)(2,1)S(1)}, f32[512,128]{1,0:T(8,128)S(1)}, f32[512,128]{1,0:T(8,128)S(1)}, bf16[4,2,64,1024]{3,2,1,0:T(8,128)(2,1)S(1)}, bf16[256,256]{1,0:T(8,128)(2,1)S(1)}) custom-call(bf16[3,2048,128]{2,1,0:T(8,128)(2,1)S(1)} %bitcast.2, bf16[4,512,128]{2,1,0:T(8,128)(2,1)} %get-tuple-element.16.q4, ...), custom_call_target="tpu_custom_call" | custom-call | flops 2000000000 | bytes 3000000 | tf_op jit(solution)/shard_map/pallas_call | solution.py:47
  39.8 2.5 %shard_map.81 = bf16[16,72,128]{2,1,0:T(8,128)(2,1)} custom-call(s32[32]{0:T(128)S(1)} %copy-done.2, s32[32]{0:T(128)S(1)} %copy-done.3, bf16[16,3,2,1024]{3,2,1,0:T(2,128)(2,1)S(1)} %all_to_all.20.arr, bf16[4,2,64,1024]{3,2,1,0:T(8,128)(2,1)S(1)} %get-tuple-element.29.cache), custom_call_target="tpu_custom_call" | custom-call | flops 100000000 | bytes 2000000 | tf_op jit(solution)/shard_map/pallas_call | solution.py:47
  42.4 0.0 all-to-all-done.qs
  42.4 15.8 %all-to-all-start.2 = ((bf16[16,72,128]{2,1,0:T(8,128)(2,1)}), bf16[16,72,128]{2,1,0:T(8,128)(2,1)S(1)}, u32[]{:S(2)}, u32[]{:S(2)}) async-start(bf16[16,72,128]{2,1,0:T(8,128)(2,1)} %shard_map.81), calls=%async_computation.2 | async-start | bytes 589824 | tf_op jit(solution)/shard_map/all_to_all | solution.py:487
  58.2 0.0 copy-start.1
  58.2 7.3 %collective-permute-start.1 = (bf16[256,256]{1,0:T(8,128)(2,1)S(1)}, bf16[256,256]{1,0:T(8,128)(2,1)S(1)}, u32[]{:S(2)}, u32[]{:S(2)}) collective-permute-start(bf16[256,256]{1,0:T(8,128)(2,1)S(1)} %get-tuple-element.22), channel_id=1, source_target_pairs={{256,384},{288,416},{320,448},{352,480},{384,256},{416,288},{448,3... | collective-permute-start | bytes 393224 | tf_op jit(solution)/shard_map/ppermute | solution.py:471
  65.5 7.8 %collective-permute-done.1.col2 = bf16[256,256]{1,0:T(8,128)(2,1)S(1)} collective-permute-done((bf16[256,256]{1,0:T(8,128)(2,1)S(1)}, bf16[256,256]{1,0:T(8,128)(2,1)S(1)}, u32[]{:S(2)}, u32[]{:S(2)}) %collective-permute-start.1) | collective-permute-done | bytes 131104 | tf_op jit(solution)/shard_map/ppermute | solution.py:471
  73.3 5.0 %shard_map.79 = (f32[128,128]{1,0:T(8,128)S(1)}, f32[128,128]{1,0:T(8,128)S(1)}, bf16[544,128]{1,0:T(8,128)(2,1)S(1)}, bf16[544,128]{1,0:T(8,128)(2,1)S(1)}, bf16[544,128]{1,0:T(8,128)(2,1)S(1)}) custom-call(bf16[4,512,128]{2,1,0:T(8,128)(2,1)S(1)} %all-to-all-done.qs, bf16[512,256]{1,0:T(8,128)(2,1)} %get-tuple-element.17.kvm_h, ...), custom_call_target="tpu_custom_call" | custom-call | flops 1000000000 | bytes 4000000 | tf_op jit(solution)/shard_map/pallas_call | solution.py:47
  78.3 5.0 %collective-permute-start.2 = (bf16[544,128]{1,0:T(8,128)(2,1)S(1)}, bf16[544,128]{1,0:T(8,128)(2,1)S(1)}, u32[]{:S(2)}, u32[]{:S(2)}) collective-permute-start(bf16[544,128]{1,0:T(8,128)(2,1)S(1)} %get-tuple-element.25), channel_id=1, source_target_pairs={{0,32},{32,0},{64,96},{96,64},{128,160},{160,128},{192,224},{224,1... | collective-permute-start | bytes 417800 | tf_op jit(solution)/shard_map/ppermute | solution.py:453
  83.2 8.9 %collective-permute-start.3 = (bf16[544,128]{1,0:T(8,128)(2,1)S(1)}, bf16[544,128]{1,0:T(8,128)(2,1)S(1)}, u32[]{:S(2)}, u32[]{:S(2)}) collective-permute-start(bf16[544,128]{1,0:T(8,128)(2,1)S(1)} %get-tuple-element.26), channel_id=1, source_target_pairs={{0,64},{32,96},{64,0},{96,32},{128,192},{160,224},{192,128},{224,1... | collective-permute-start | bytes 417800 | tf_op jit(solution)/shard_map/ppermute | solution.py:453
  92.1 2.1 %collective-permute-start.4 = (bf16[544,128]{1,0:T(8,128)(2,1)S(1)}, bf16[544,128]{1,0:T(8,128)(2,1)S(1)}, u32[]{:S(2)}, u32[]{:S(2)}) collective-permute-start(bf16[544,128]{1,0:T(8,128)(2,1)S(1)} %get-tuple-element.27), channel_id=1, source_target_pairs={{0,96},{32,64},{64,32},{96,0},{128,224},{160,192},{192,160},{224,1... | collective-permute-start | bytes 417800 | tf_op jit(solution)/shard_map/ppermute | solution.py:453
  94.3 0.0 all-to-all-done.2.got
  94.3 1.2 %shard_map.82 = bf16[32,2,128]{2,1,0:T(2,128)(2,1)S(1)} custom-call(s32[32]{0:T(128)S(1)} %copy-done.2, bf16[16,72,128]{2,1,0:T(8,128)(2,1)S(1)} %all-to-all-done.2.got, bf16[1024,256]{1,0:T(8,128)(2,1)S(1)} %copy-done.1), custom_call_target="tpu_custom_call" | custom-call | flops 10000000 | bytes 1000000 | tf_op jit(solution)/shard_map/pallas_call | solution.py:47
  95.4 13.3 %all_to_all.21.got = bf16[32,2,128]{2,1,0:T(2,128)(2,1)S(1)} all-to-all(bf16[32,2,128]{2,1,0:T(2,128)(2,1)S(1)} %shard_map.82), channel_id=1, replica_groups=mesh['seq'=16,'head'=4,'req'=8] {'head','req'}, dimensions={0} | all-to-all | bytes 32768 | tf_op jit(solution)/shard_map/all_to_all | solution.py:511
  108.8 1.6 %shard_map.83 = bf16[16,2,64]{2,1,0:T(2,128)(2,1)} custom-call(s32[32]{0:T(128)S(1)} %copy-done.2, bf16[32,2,128]{2,1,0:T(2,128)(2,1)S(1)} %all_to_all.21.got), custom_call_target="tpu_custom_call" | custom-call | bytes 100000 | tf_op jit(solution)/shard_map/pallas_call | solution.py:47
  110.3 0.0 collective-permute-done.2.back1
  110.3 0.0 collective-permute-done.3.back2
  110.3 0.0 collective-permute-done.4.back3
  110.3 2.6 %shard_map.80 = bf16[2048,128]{1,0:T(8,128)(2,1)} custom-call(bf16[2048,128]{1,0:T(8,128)(2,1)S(1)} %get-tuple-element.19.near, f32[512,128]{1,0:T(8,128)S(1)} %get-tuple-element.20.acc, f32[512,128]{1,0:T(8,128)S(1)} %get-tuple-element.21.ml, f32[128,128]{1,0:T(8,128)S(1)} %get-tuple-element.23.acc_f, f32[128,128]{1,0:T(8,128)S(1)} %get-tuple-element.24.ml_f, ...), custom_call_target="tpu_custom_call" | custom-call | flops 100000000 | bytes 4000000 | tf_op jit(solution)/shard_map/pallas_call | solution.py:47
  (7 shorter events, 0.0 us)
Async XLA Ops:
  0.6 32.2 %copy-start = (bf16[2048,3,128]{2,0,1:T(8,128)(2,1)S(1)}, bf16[2048,3,128]{2,0,1:T(8,128)(2,1)}, u32[]{:S(2)}) copy-start(bf16[2048,3,128]{2,0,1:T(8,128)(2,1)} %param.6) | copy-start | bytes 4718596
  19.2 23.2 %all-to-all-start = ((bf16[4,512,128]{2,1,0:T(8,128)(2,1)}), bf16[4,512,128]{2,1,0:T(8,128)(2,1)S(1)}, u32[]{:S(2)}, u32[]{:S(2)}) async-start(bf16[4,512,128]{2,1,0:T(8,128)(2,1)} %get-tuple-element.16.q4), calls=%async_computation | async-start | bytes 1048576 | tf_op jit(solution)/shard_map/all_to_all | solution.py:450
  22.7 10.1 %collective-permute-start = (bf16[128,256]{1,0:T(8,128)(2,1)S(1)}, bf16[128,256]{1,0:T(8,128)(2,1)S(1)}, u32[]{:S(2)}, u32[]{:S(2)}) collective-permute-start(bf16[128,256]{1,0:T(8,128)(2,1)S(1)} %get-tuple-element.18), channel_id=1, source_target_pairs={{0,384},{32,416},{64,448},{96,480},{128,256},{160,288},{192,320},{... | collective-permute-start | bytes 196616 | tf_op jit(solution)/shard_map/ppermute | solution.py:448
  32.8 7.0 %copy-start.2 = (s32[32]{0:T(128)S(1)}, s32[32]{0:T(128)}, u32[]{:S(2)}) copy-start(s32[32]{0:T(128)} %own.5) | copy-start | bytes 388
  32.8 7.0 %copy-start.3 = (s32[32]{0:T(128)S(1)}, s32[32]{0:T(128)}, u32[]{:S(2)}) copy-start(s32[32]{0:T(128)} %lens.1) | copy-start | bytes 388
  42.4 51.9 %all-to-all-start.2 = ((bf16[16,72,128]{2,1,0:T(8,128)(2,1)}), bf16[16,72,128]{2,1,0:T(8,128)(2,1)S(1)}, u32[]{:S(2)}, u32[]{:S(2)}) async-start(bf16[16,72,128]{2,1,0:T(8,128)(2,1)} %shard_map.81), calls=%async_computation.2 | async-start | bytes 589824 | tf_op jit(solution)/shard_map/all_to_all | solution.py:487
  58.2 36.1 %copy-start.1 = (bf16[1024,256]{1,0:T(8,128)(2,1)S(1)}, bf16[1024,256]{1,0:T(8,128)(2,1)}, u32[]{:S(2)}) copy-start(bf16[1024,256]{1,0:T(8,128)(2,1)} %weight.1) | copy-start | bytes 1572868
  58.2 15.1 %collective-permute-start.1 = (bf16[256,256]{1,0:T(8,128)(2,1)S(1)}, bf16[256,256]{1,0:T(8,128)(2,1)S(1)}, u32[]{:S(2)}, u32[]{:S(2)}) collective-permute-start(bf16[256,256]{1,0:T(8,128)(2,1)S(1)} %get-tuple-element.22), channel_id=1, source_target_pairs={{256,384},{288,416},{320,448},{352,480},{384,256},{416,288},{448,3... | collective-permute-start | bytes 393224 | tf_op jit(solution)/shard_map/ppermute | solution.py:471
  78.3 32.1 %collective-permute-start.2 = (bf16[544,128]{1,0:T(8,128)(2,1)S(1)}, bf16[544,128]{1,0:T(8,128)(2,1)S(1)}, u32[]{:S(2)}, u32[]{:S(2)}) collective-permute-start(bf16[544,128]{1,0:T(8,128)(2,1)S(1)} %get-tuple-element.25), channel_id=1, source_target_pairs={{0,32},{32,0},{64,96},{96,64},{128,160},{160,128},{192,224},{224,1... | collective-permute-start | bytes 417800 | tf_op jit(solution)/shard_map/ppermute | solution.py:453
  83.2 27.1 %collective-permute-start.3 = (bf16[544,128]{1,0:T(8,128)(2,1)S(1)}, bf16[544,128]{1,0:T(8,128)(2,1)S(1)}, u32[]{:S(2)}, u32[]{:S(2)}) collective-permute-start(bf16[544,128]{1,0:T(8,128)(2,1)S(1)} %get-tuple-element.26), channel_id=1, source_target_pairs={{0,64},{32,96},{64,0},{96,32},{128,192},{160,224},{192,128},{224,1... | collective-permute-start | bytes 417800 | tf_op jit(solution)/shard_map/ppermute | solution.py:453
  92.1 18.2 %collective-permute-start.4 = (bf16[544,128]{1,0:T(8,128)(2,1)S(1)}, bf16[544,128]{1,0:T(8,128)(2,1)S(1)}, u32[]{:S(2)}, u32[]{:S(2)}) collective-permute-start(bf16[544,128]{1,0:T(8,128)(2,1)S(1)} %get-tuple-element.27), channel_id=1, source_target_pairs={{0,96},{32,64},{64,32},{96,0},{128,224},{160,192},{192,160},{224,1... | collective-permute-start | bytes 417800 | tf_op jit(solution)/shard_map/ppermute | solution.py:453

commit v7 on v5

--- a/solution.py
+++ b/solution.py
@@ -159,13 +159,11 @@
 
 
 def near_kernel(
-    raw, qm, msg, cache_h, near_h, acc_h, ml_h, cache,
+    raw, qm, msg, near_h, acc_h, ml_h,
     acc_s, ml_s, near_o, acc_o, ml_o, sem, out_sem,
 ):
     rows = raw.shape[1]
     step = 256
-    fetch = pltpu.make_async_copy(cache_h, cache, sem.at[2])
-    fetch.start()
     copies = []
     inner = lax.div(lax.rem(head_id(), 16), 4)
 
@@ -208,7 +206,6 @@
         copies.append(cp)
     for cp in copies:
         cp.wait()
-    fetch.wait()
 
 
 def pack(rows_m, rows_l):
@@ -501,11 +498,11 @@
     got1 = swap(msg, 1)
     col2 = relay(col1, 4, 12, 4)
     state = [pltpu.HBM((512, HD), F32)] * 2
-    near_o, acc, ml, cache = call(
+    near_o, acc, ml = call(
         near_kernel,
-        (pltpu.HBM((2048, HD), BF16), *state, shape(cache_kv.shape)),
-        (raw, qm, msg, far_memory(cache_kv)),
-        [vspec(), vspec(), vspec(), hspec()],
+        (pltpu.HBM((2048, HD), BF16), *state),
+        (raw, qm, msg),
+        [vspec()] * 3,
         [
             VMEM((2048, HD), F32),
             VMEM((2048, HD), F32),
@@ -518,12 +515,12 @@
         flops=2 * 10**9,
         nbytes=3000000,
         trans=2 * 10**6,
-        outs=[hspec(), hspec(), hspec(), vspec()],
+        outs=[hspec()] * 3,
     )
     partial = call(
         cache_kernel,
         shape((16, 72, HD)),
-        (owner_slot, prompt_lengths, arrived, cache),
+        (owner_slot, prompt_lengths, arrived, cache_kv),
         [sspec(), sspec(), vspec(), vspec()],
         [VMEM((64, HD), F32), VMEM((64, HD), F32)],
         flops=10**8,

time: 106 us -> 103 us (0.972)
  blocking collectives: 0 us -> 10.7 us
  waiting for transfers between devices: 19.8 us -> 11.3 us
  starting transfers between devices: 62.1 us -> 58.1 us
    all_to_all x0 -> x1, blocking collectives: none -> 10.7 us  [staged(): arrived = lax.all_to_all(sent, 'req', 0, 0, tiled=True)]
    all_to_all x1 -> x0, starting transfers between devices: 5.02 us -> none  [staged(): arrived = lax.all_to_all(sent, 'req', 0, 0, tiled=True)]
    ppermute x6, waiting for transfers between devices: 4.54 us -> 0.02 us  [swap(): return lax.ppermute(x, 'seq', [(i, i ^ bits) for i in range(16)])]
    ppermute x3, waiting for transfers between devices: 11.5 us -> 7.55 us  [relay(): return lax.ppermute(x, 'seq', [(i, i + hop) for i in range(first, stop)])]
    ppermute x6, starting transfers between devices: 19.2 us -> 21.9 us  [swap(): return lax.ppermute(x, 'seq', [(i, i ^ bits) for i in range(16)])]
    all_to_all x1, starting transfers between devices: 9.79 us -> 8.07 us  [staged(): results = lax.all_to_all(answers, ('head', 'req'), 0, 0, tiled=True)]
  transfers between devices with their start and end apart: 12 -> 11, of which waited for: 3 -> 2; matrix products, arithmetic and copies ran while one was open for 0% -> 0% of each run, Pallas kernels for 15% -> 15%
where the time goes in v7:
time: 103 us
  starting transfers between devices  58.1 us (56%)
  Pallas kernels  22 us (21%)
  waiting for transfers between devices  11.3 us (11%)
  blocking collectives  10.7 us (10%)
    pallas_call x7, Pallas kernels, call(): pl.pallas_call(body, out_shape=out_shape, in_specs=specs, out_specs=vspec...  22 us
    ppermute x6, starting transfers between devices, swap(): return lax.ppermute(x, 'seq', [(i, i ^ bits) for i in range(16)])  21.9 us
    ppermute x3, starting transfers between devices, relay(): return lax.ppermute(x, 'seq', [(i, i + hop) for i in range(first, stop)])  14.8 us
    all_to_all x1, starting transfers between devices, staged(): parts = lax.all_to_all(partial, 'seq', 0, 0, tiled=True)  13.3 us
    all_to_all x1, blocking collectives, staged(): arrived = lax.all_to_all(sent, 'req', 0, 0, tiled=True)  10.7 us
    all_to_all x1, starting transfers between devices, staged(): results = lax.all_to_all(answers, ('head', 'req'), 0, 0, tiled=True)  8.07 us
    ppermute x3, waiting for transfers between devices, relay(): return lax.ppermute(x, 'seq', [(i, i + hop) for i in range(first, stop)])  7.55 us
    all_to_all x1, waiting for transfers between devices, staged(): results = lax.all_to_all(answers, ('head', 'req'), 0, 0, tiled=True)  3.74 us
  transfers between devices with their start and end apart: 11, of which 2 were waited for; matrix products, arithmetic and copies ran while one was open for 0% of the time, Pallas kernels for 15%

profile of v7, /device:TPU:129, one launch (start us, length us, event | category | flops | bytes accessed | tf_op | source)
XLA Modules:
  0.0 102.9 jit_solution(7485735712117852848)
XLA Ops:
  0.7 2.3 %shard_map.77 = (bf16[3,2048,128]{2,1,0:T(8,128)(2,1)S(1)}, bf16[16,3,2,1024]{3,2,1,0:T(2,128)(2,1)S(1)}, bf16[512,128]{1,0:T(8,128)(2,1)S(1)}, bf16[128,128]{1,...) custom-call(s32[32]{0:T(128)} %own.5, bf16[16,3,2,1024]{3,2,1,0:T(2,128)(2,1)} %dec.1, ...), custom_call_target="tpu_custom_call" | custom-call | bytes 4000000 | tf_op jit(solution)/shard_map/pallas_call | solution.py:47
  3.0 10.7 %all_to_all.15.arr = bf16[16,3,2,1024]{3,2,1,0:T(2,128)(2,1)S(1)} all-to-all(bf16[16,3,2,1024]{3,2,1,0:T(2,128)(2,1)S(1)} %get-tuple-element.29), channel_id=1, replica_groups=mesh['seq'=16,'head'=4,'req'=8] {'req'}, dimensions={0} | all-to-all | bytes 393216 | tf_op jit(solution)/shard_map/all_to_all | solution.py:486
  13.6 2.5 %shard_map.81 = bf16[16,72,128]{2,1,0:T(8,128)(2,1)} custom-call(s32[32]{0:T(128)S(1)} %copy-done.2, s32[32]{0:T(128)S(1)} %copy-done.3, bf16[16,3,2,1024]{3,2,1,0:T(2,128)(2,1)S(1)} %all_to_all.15.arr, bf16[4,2,64,1024]{3,2,1,0:T(8,128)(2,1)S(1)} %copy-done), custom_call_target="tpu_custom_call" | custom-call | flops 100000000 | bytes 2000000 | tf_op jit(solution)/shard_map/pallas_call | solution.py:47
  16.2 13.3 %all-to-all-start.1 = ((bf16[16,72,128]{2,1,0:T(8,128)(2,1)}), bf16[16,72,128]{2,1,0:T(8,128)(2,1)S(1)}, u32[]{:S(2)}, u32[]{:S(2)}) async-start(bf16[16,72,128]{2,1,0:T(8,128)(2,1)} %shard_map.81), calls=%async_computation.1 | async-start | bytes 589824 | tf_op jit(solution)/shard_map/all_to_all | solution.py:529
  29.5 3.1 %collective-permute-start = (bf16[576,256]{1,0:T(8,128)(2,1)S(1)}, bf16[576,256]{1,0:T(8,128)(2,1)S(1)}, u32[]{:S(2)}, u32[]{:S(2)}) collective-permute-start(bf16[576,256]{1,0:T(8,128)(2,1)S(1)} %get-tuple-element.18.msg), channel_id=1, source_target_pairs={{0,32},{32,0},{64,96},{96,64},{128,160},{160,128},{192,224},{224,1... | collective-permute-start | bytes 884744 | tf_op jit(solution)/shard_map/ppermute | solution.py:489
  32.6 6.1 %collective-permute-start.3 = (bf16[128,256]{1,0:T(8,128)(2,1)S(1)}, bf16[128,256]{1,0:T(8,128)(2,1)S(1)}, u32[]{:S(2)}, u32[]{:S(2)}) collective-permute-start(bf16[128,256]{1,0:T(8,128)(2,1)S(1)} %get-tuple-element.21), channel_id=1, source_target_pairs={{0,128},{32,160},{64,192},{96,224},{128,256},{160,288},{192,320},{... | collective-permute-start | bytes 196616 | tf_op jit(solution)/shard_map/ppermute | solution.py:492
  38.7 0.7 collective-permute-start.5
  39.3 3.1 %collective-permute-start.2 = (bf16[128,128]{1,0:T(8,128)(2,1)S(1)}, bf16[128,128]{1,0:T(8,128)(2,1)S(1)}, u32[]{:S(2)}, u32[]{:S(2)}) collective-permute-start(bf16[128,128]{1,0:T(8,128)(2,1)S(1)} %get-tuple-element.20), channel_id=1, source_target_pairs={{0,96},{32,64},{64,32},{96,0},{128,224},{160,192},{192,160},{224,1... | collective-permute-start | bytes 98312 | tf_op jit(solution)/shard_map/ppermute | solution.py:489
  42.4 3.1 %collective-permute-start.1 = (bf16[512,128]{1,0:T(8,128)(2,1)S(1)}, bf16[512,128]{1,0:T(8,128)(2,1)S(1)}, u32[]{:S(2)}, u32[]{:S(2)}) collective-permute-start(bf16[512,128]{1,0:T(8,128)(2,1)S(1)} %get-tuple-element.17.qm), channel_id=1, source_target_pairs={{0,64},{32,96},{64,0},{96,32},{128,192},{160,224},{192,128},{224,1... | collective-permute-start | bytes 393224 | tf_op jit(solution)/shard_map/ppermute | solution.py:489
  45.5 7.5 %collective-permute-done.3.col1 = bf16[128,256]{1,0:T(8,128)(2,1)S(1)} collective-permute-done((bf16[128,256]{1,0:T(8,128)(2,1)S(1)}, bf16[128,256]{1,0:T(8,128)(2,1)S(1)}, u32[]{:S(2)}, u32[]{:S(2)}) %collective-permute-start.3) | collective-permute-done | bytes 65568 | tf_op jit(solution)/shard_map/ppermute | solution.py:492
  53.1 8.0 %collective-permute-start.4 = (bf16[128,256]{1,0:T(8,128)(2,1)S(1)}, bf16[128,256]{1,0:T(8,128)(2,1)S(1)}, u32[]{:S(2)}, u32[]{:S(2)}) collective-permute-start(bf16[128,256]{1,0:T(8,128)(2,1)S(1)} %collective-permute-done.3.col1), channel_id=1, source_target_pairs={{128,256},{160,288},{192,320},{224,352},{256,384},{288,416},{320,4... | collective-permute-start | bytes 196616 | tf_op jit(solution)/shard_map/ppermute | solution.py:492
  61.1 6.4 %shard_map.78 = (bf16[2048,128]{1,0:T(8,128)(2,1)}, f32[512,128]{1,0:T(8,128)}, f32[512,128]{1,0:T(8,128)}) custom-call(bf16[3,2048,128]{2,1,0:T(8,128)(2,1)S(1)} %get-tuple-element.16.raw, bf16[512,128]{1,0:T(8,128)(2,1)S(1)} %get-tuple-element.17.qm, bf16[576,256]{1,0:T(8,128)(2,1)S(1)} %get-tuple-element.18.msg), custom_call_target="tpu_custom_call" | custom-call | flops 2000000000 | bytes 3000000 | tf_op jit(solution)/shard_map/pallas_call | solution.py:47
  67.6 0.0 collective-permute-done.4.col2
  67.6 0.0 collective-permute-done.1.got2
  67.6 0.0 copy-start.1
  67.6 4.2 %shard_map.79 = (f32[512,128]{1,0:T(8,128)}, f32[512,128]{1,0:T(8,128)}, bf16[144,128]{1,0:T(8,128)(2,1)S(1)}, bf16[544,128]{1,0:T(8,128)(2,1)S(1)}, bf16[144,128]{1,0:T(8,128)(2,1)S(1)}) custom-call(bf16[512,128]{1,0:T(8,128)(2,1)S(1)} %get-tuple-element.17.qm, bf16[576,256]{1,0:T(8,128)(2,1)S(1)} %get-tuple-element.18.msg, ...), custom_call_target="tpu_custom_call" | custom-call | flops 1000000000 | bytes 4000000 | tf_op jit(solution)/shard_map/pallas_call | solution.py:47
  71.8 7.7 %collective-permute-start.7 = (bf16[544,128]{1,0:T(8,128)(2,1)S(1)}, bf16[544,128]{1,0:T(8,128)(2,1)S(1)}, u32[]{:S(2)}, u32[]{:S(2)}) collective-permute-start(bf16[544,128]{1,0:T(8,128)(2,1)S(1)} %get-tuple-element.27), channel_id=1, source_target_pairs={{0,64},{32,96},{64,0},{96,32},{128,192},{160,224},{192,128},{224,1... | collective-permute-start | bytes 417800 | tf_op jit(solution)/shard_map/ppermute | solution.py:489
  79.5 1.9 %collective-permute-start.6 = (bf16[144,128]{1,0:T(8,128)(2,1)S(1)}, bf16[144,128]{1,0:T(8,128)(2,1)S(1)}, u32[]{:S(2)}, u32[]{:S(2)}) collective-permute-start(bf16[144,128]{1,0:T(8,128)(2,1)S(1)} %get-tuple-element.26), channel_id=1, source_target_pairs={{0,32},{32,0},{64,96},{96,64},{128,160},{160,128},{192,224},{224,1... | collective-permute-start | bytes 110600 | tf_op jit(solution)/shard_map/ppermute | solution.py:489
  81.4 3.1 %collective-permute-start.8 = (bf16[144,128]{1,0:T(8,128)(2,1)S(1)}, bf16[144,128]{1,0:T(8,128)(2,1)S(1)}, u32[]{:S(2)}, u32[]{:S(2)}) collective-permute-start(bf16[144,128]{1,0:T(8,128)(2,1)S(1)} %get-tuple-element.28), channel_id=1, source_target_pairs={{0,96},{32,64},{64,32},{96,0},{128,224},{160,192},{192,160},{224,1... | collective-permute-start | bytes 110600 | tf_op jit(solution)/shard_map/ppermute | solution.py:489
  84.6 1.8 %shard_map.82 = bf16[32,2,128]{2,1,0:T(2,128)(2,1)} custom-call(s32[32]{0:T(128)S(1)} %copy-done.2, bf16[16,72,128]{2,1,0:T(8,128)(2,1)S(1)} %all-to-all-done.1.got, bf16[1024,256]{1,0:T(8,128)(2,1)S(1)} %copy-done.1), custom_call_target="tpu_custom_call" | custom-call | flops 10000000 | bytes 1000000 | tf_op jit(solution)/shard_map/pallas_call | solution.py:47
  86.3 8.1 %all-to-all-start.2 = ((bf16[32,2,128]{2,1,0:T(2,128)(2,1)}), bf16[32,2,128]{2,1,0:T(2,128)(2,1)S(1)}, u32[]{:S(2)}, u32[]{:S(2)}) async-start(bf16[32,2,128]{2,1,0:T(2,128)(2,1)} %shard_map.82), calls=%async_computation.2 | async-start | bytes 32768 | tf_op jit(solution)/shard_map/all_to_all | solution.py:553
  94.4 3.2 %shard_map.80 = bf16[2048,128]{1,0:T(8,128)(2,1)} custom-call(bf16[2048,128]{1,0:T(8,128)(2,1)} %get-tuple-element.19.near_h, f32[512,128]{1,0:T(8,128)} %get-tuple-element.24.acc_h, f32[512,128]{1,0:T(8,128)} %get-tuple-element.25.ml_h, bf16[144,128]{1,0:T(8,128)(2,1)S(1)} %collective-permute-done.6.back1, ...), custom_call_target="tpu_custom_call" | custom-call | flops 100000000 | bytes 4000000 | tf_op jit(solution)/shard_map/pallas_call | solution.py:47
  97.6 3.7 %all-to-all-done.2.got = bf16[32,2,128]{2,1,0:T(2,128)(2,1)S(1)} async-done(((bf16[32,2,128]{2,1,0:T(2,128)(2,1)}), bf16[32,2,128]{2,1,0:T(2,128)(2,1)S(1)}, u32[]{:S(2)}, u32[]{:S(2)}) %all-to-all-start.2) | async-done | bytes 16416 | tf_op jit(solution)/shard_map/all_to_all | solution.py:553
  101.4 1.6 %shard_map.83 = bf16[16,2,64]{2,1,0:T(2,128)(2,1)} custom-call(s32[32]{0:T(128)S(1)} %copy-done.2, bf16[32,2,128]{2,1,0:T(2,128)(2,1)S(1)} %all-to-all-done.2.got), custom_call_target="tpu_custom_call" | custom-call | bytes 100000 | tf_op jit(solution)/shard_map/pallas_call | solution.py:47
  (14 shorter events, 0.0 us)
Async XLA Ops:
  0.6 13.0 %copy-start.2 = (s32[32]{0:T(128)S(1)}, s32[32]{0:T(128)}, u32[]{:S(2)}) copy-start(s32[32]{0:T(128)} %own.5) | copy-start | bytes 388
  0.6 13.0 %copy-start.3 = (s32[32]{0:T(128)S(1)}, s32[32]{0:T(128)}, u32[]{:S(2)}) copy-start(s32[32]{0:T(128)} %lens.1) | copy-start | bytes 388
  0.7 13.0 %copy-start = (bf16[4,2,64,1024]{3,2,1,0:T(8,128)(2,1)S(1)}, bf16[4,2,64,1024]{3,2,1,0:T(8,128)(2,1)}, u32[]{:S(2)}) copy-start(bf16[4,2,64,1024]{3,2,1,0:T(8,128)(2,1)} %cache.1) | copy-start | bytes 3145732
  16.2 68.4 %all-to-all-start.1 = ((bf16[16,72,128]{2,1,0:T(8,128)(2,1)}), bf16[16,72,128]{2,1,0:T(8,128)(2,1)S(1)}, u32[]{:S(2)}, u32[]{:S(2)}) async-start(bf16[16,72,128]{2,1,0:T(8,128)(2,1)} %shard_map.81), calls=%async_computation.1 | async-start | bytes 589824 | tf_op jit(solution)/shard_map/all_to_all | solution.py:529
  29.5 38.1 %collective-permute-start = (bf16[576,256]{1,0:T(8,128)(2,1)S(1)}, bf16[576,256]{1,0:T(8,128)(2,1)S(1)}, u32[]{:S(2)}, u32[]{:S(2)}) collective-permute-start(bf16[576,256]{1,0:T(8,128)(2,1)S(1)} %get-tuple-element.18.msg), channel_id=1, source_target_pairs={{0,32},{32,0},{64,96},{96,64},{128,160},{160,128},{192,224},{224,1... | collective-permute-start | bytes 884744 | tf_op jit(solution)/shard_map/ppermute | solution.py:489
  32.6 20.5 %collective-permute-start.3 = (bf16[128,256]{1,0:T(8,128)(2,1)S(1)}, bf16[128,256]{1,0:T(8,128)(2,1)S(1)}, u32[]{:S(2)}, u32[]{:S(2)}) collective-permute-start(bf16[128,256]{1,0:T(8,128)(2,1)S(1)} %get-tuple-element.21), channel_id=1, source_target_pairs={{0,128},{32,160},{64,192},{96,224},{128,256},{160,288},{192,320},{... | collective-permute-start | bytes 196616 | tf_op jit(solution)/shard_map/ppermute | solution.py:492
  38.7 28.9 %collective-permute-start.5 = (bf16[128,256]{1,0:T(8,128)(2,1)S(1)}, bf16[128,256]{1,0:T(8,128)(2,1)S(1)}, u32[]{:S(2)}, u32[]{:S(2)}) collective-permute-start(bf16[128,256]{1,0:T(8,128)(2,1)S(1)} %get-tuple-element.21), channel_id=1, source_target_pairs={{0,384},{32,416},{64,448},{96,480},{1,385},{33,417},{65,449},{97,4... | collective-permute-start | bytes 196616 | tf_op jit(solution)/shard_map/ppermute | solution.py:492
  39.3 28.2 %collective-permute-start.2 = (bf16[128,128]{1,0:T(8,128)(2,1)S(1)}, bf16[128,128]{1,0:T(8,128)(2,1)S(1)}, u32[]{:S(2)}, u32[]{:S(2)}) collective-permute-start(bf16[128,128]{1,0:T(8,128)(2,1)S(1)} %get-tuple-element.20), channel_id=1, source_target_pairs={{0,96},{32,64},{64,32},{96,0},{128,224},{160,192},{192,160},{224,1... | collective-permute-start | bytes 98312 | tf_op jit(solution)/shard_map/ppermute | solution.py:489
  42.4 25.2 %collective-permute-start.1 = (bf16[512,128]{1,0:T(8,128)(2,1)S(1)}, bf16[512,128]{1,0:T(8,128)(2,1)S(1)}, u32[]{:S(2)}, u32[]{:S(2)}) collective-permute-start(bf16[512,128]{1,0:T(8,128)(2,1)S(1)} %get-tuple-element.17.qm), channel_id=1, source_target_pairs={{0,64},{32,96},{64,0},{96,32},{128,192},{160,224},{192,128},{224,1... | collective-permute-start | bytes 393224 | tf_op jit(solution)/shard_map/ppermute | solution.py:489
  53.1 14.5 %collective-permute-start.4 = (bf16[128,256]{1,0:T(8,128)(2,1)S(1)}, bf16[128,256]{1,0:T(8,128)(2,1)S(1)}, u32[]{:S(2)}, u32[]{:S(2)}) collective-permute-start(bf16[128,256]{1,0:T(8,128)(2,1)S(1)} %collective-permute-done.3.col1), channel_id=1, source_target_pairs={{128,256},{160,288},{192,320},{224,352},{256,384},{288,416},{320,4... | collective-permute-start | bytes 196616 | tf_op jit(solution)/shard_map/ppermute | solution.py:492
  67.6 16.9 %copy-start.1 = (bf16[1024,256]{1,0:T(8,128)(2,1)S(1)}, bf16[1024,256]{1,0:T(8,128)(2,1)}, u32[]{:S(2)}) copy-start(bf16[1024,256]{1,0:T(8,128)(2,1)} %weight.1) | copy-start | bytes 1572868
  71.8 22.6 %collective-permute-start.7 = (bf16[544,128]{1,0:T(8,128)(2,1)S(1)}, bf16[544,128]{1,0:T(8,128)(2,1)S(1)}, u32[]{:S(2)}, u32[]{:S(2)}) collective-permute-start(bf16[544,128]{1,0:T(8,128)(2,1)S(1)} %get-tuple-element.27), channel_id=1, source_target_pairs={{0,64},{32,96},{64,0},{96,32},{128,192},{160,224},{192,128},{224,1... | collective-permute-start | bytes 417800 | tf_op jit(solution)/shard_map/ppermute | solution.py:489
  79.5 14.9 %collective-permute-start.6 = (bf16[144,128]{1,0:T(8,128)(2,1)S(1)}, bf16[144,128]{1,0:T(8,128)(2,1)S(1)}, u32[]{:S(2)}, u32[]{:S(2)}) collective-permute-start(bf16[144,128]{1,0:T(8,128)(2,1)S(1)} %get-tuple-element.26), channel_id=1, source_target_pairs={{0,32},{32,0},{64,96},{96,64},{128,160},{160,128},{192,224},{224,1... | collective-permute-start | bytes 110600 | tf_op jit(solution)/shard_map/ppermute | solution.py:489
  81.4 13.0 %collective-permute-start.8 = (bf16[144,128]{1,0:T(8,128)(2,1)S(1)}, bf16[144,128]{1,0:T(8,128)(2,1)S(1)}, u32[]{:S(2)}, u32[]{:S(2)}) collective-permute-start(bf16[144,128]{1,0:T(8,128)(2,1)S(1)} %get-tuple-element.28), channel_id=1, source_target_pairs={{0,96},{32,64},{64,32},{96,0},{128,224},{160,192},{192,160},{224,1... | collective-permute-start | bytes 110600 | tf_op jit(solution)/shard_map/ppermute | solution.py:489
  86.3 15.0 %all-to-all-start.2 = ((bf16[32,2,128]{2,1,0:T(2,128)(2,1)}), bf16[32,2,128]{2,1,0:T(2,128)(2,1)S(1)}, u32[]{:S(2)}, u32[]{:S(2)}) async-start(bf16[32,2,128]{2,1,0:T(2,128)(2,1)} %shard_map.82), calls=%async_computation.2 | async-start | bytes 32768 | tf_op jit(solution)/shard_map/all_to_all | solution.py:553

commit v8 on v7

--- a/solution.py
+++ b/solution.py
@@ -445,15 +445,17 @@
         total = total + got[pl.ds(8 * h, 8)].astype(F32)
     out[...] = jnp.zeros(out.shape, BF16)
     for b in range(8):
-        first = total[b]
-        for k in range(4):
-            slot = own[4 * b + k]
-            grp, rank = rank_in_block(own, 4 * b, k)
-
-            @pl.when(grp == me)
-            def _(first=first, slot=slot, rank=rank):
-                row = jnp.where(rank == 0, first[0:1], first[1:2])
-                out[slot & 15] = jnp.concatenate([row[:, :64], row[:, 64:]], axis=0).astype(BF16)
+        seats = [(own[4 * b + k], *rank_in_block(own, 4 * b, k)) for k in range(4)]
+        for r in range(2):
+            place = jnp.int32(-1)
+            for slot, grp, rank in seats:
+                place = jnp.where((grp == me) & (rank == r), slot & 15, place)
+            row = total[b, r : r + 1]
+            both_tokens = jnp.concatenate([row[:, :64], row[:, 64:]], axis=0).astype(BF16)
+
+            @pl.when(place >= 0)
+            def _(place=place, both_tokens=both_tokens):
+                out[place] = both_tokens
 
 
 def shape(dims, dtype=BF16):

time: 103 us -> 104 us (level)
  no operation moved by 1% of the time
where the time goes in v8:
time: 104 us
  starting transfers between devices  58.1 us (56%)
  Pallas kernels  22.7 us (22%)
  waiting for transfers between devices  11.3 us (11%)
  blocking collectives  10.7 us (10%)
    pallas_call x7, Pallas kernels, call(): pl.pallas_call(body, out_shape=out_shape, in_specs=specs, out_specs=vspec...  22.7 us
    ppermute x6, starting transfers between devices, swap(): return lax.ppermute(x, 'seq', [(i, i ^ bits) for i in range(16)])  21.9 us
    ppermute x3, starting transfers between devices, relay(): return lax.ppermute(x, 'seq', [(i, i + hop) for i in range(first, stop)])  14.8 us
    all_to_all x1, starting transfers between devices, staged(): parts = lax.all_to_all(partial, 'seq', 0, 0, tiled=True)  13.3 us
    all_to_all x1, blocking collectives, staged(): arrived = lax.all_to_all(sent, 'req', 0, 0, tiled=True)  10.7 us
    all_to_all x1, starting transfers between devices, staged(): results = lax.all_to_all(answers, ('head', 'req'), 0, 0, tiled=True)  8.07 us
    ppermute x3, waiting for transfers between devices, relay(): return lax.ppermute(x, 'seq', [(i, i + hop) for i in range(first, stop)])  7.55 us
    all_to_all x1, waiting for transfers between devices, staged(): results = lax.all_to_all(answers, ('head', 'req'), 0, 0, tiled=True)  3.74 us
  transfers between devices with their start and end apart: 11, of which 2 were waited for; matrix products, arithmetic and copies ran while one was open for 0% of the time, Pallas kernels for 15%

profile of v8, /device:TPU:129, one launch (start us, length us, event | category | flops | bytes accessed | tf_op | source)
XLA Modules:
  0.0 103.6 jit_solution(4326582624658009624)
XLA Ops:
  0.7 2.3 %shard_map.77 = (bf16[3,2048,128]{2,1,0:T(8,128)(2,1)S(1)}, bf16[16,3,2,1024]{3,2,1,0:T(2,128)(2,1)S(1)}, bf16[512,128]{1,0:T(8,128)(2,1)S(1)}, bf16[128,128]{1,...) custom-call(s32[32]{0:T(128)} %own.5, bf16[16,3,2,1024]{3,2,1,0:T(2,128)(2,1)} %dec.1, ...), custom_call_target="tpu_custom_call" | custom-call | bytes 4000000 | tf_op jit(solution)/shard_map/pallas_call | solution.py:47
  3.0 10.7 %all_to_all.15.arr = bf16[16,3,2,1024]{3,2,1,0:T(2,128)(2,1)S(1)} all-to-all(bf16[16,3,2,1024]{3,2,1,0:T(2,128)(2,1)S(1)} %get-tuple-element.29), channel_id=1, replica_groups=mesh['seq'=16,'head'=4,'req'=8] {'req'}, dimensions={0} | all-to-all | bytes 393216 | tf_op jit(solution)/shard_map/all_to_all | solution.py:488
  13.6 2.5 %shard_map.81 = bf16[16,72,128]{2,1,0:T(8,128)(2,1)} custom-call(s32[32]{0:T(128)S(1)} %copy-done.2, s32[32]{0:T(128)S(1)} %copy-done.3, bf16[16,3,2,1024]{3,2,1,0:T(2,128)(2,1)S(1)} %all_to_all.15.arr, bf16[4,2,64,1024]{3,2,1,0:T(8,128)(2,1)S(1)} %copy-done), custom_call_target="tpu_custom_call" | custom-call | flops 100000000 | bytes 2000000 | tf_op jit(solution)/shard_map/pallas_call | solution.py:47
  16.2 13.3 %all-to-all-start.1 = ((bf16[16,72,128]{2,1,0:T(8,128)(2,1)}), bf16[16,72,128]{2,1,0:T(8,128)(2,1)S(1)}, u32[]{:S(2)}, u32[]{:S(2)}) async-start(bf16[16,72,128]{2,1,0:T(8,128)(2,1)} %shard_map.81), calls=%async_computation.1 | async-start | bytes 589824 | tf_op jit(solution)/shard_map/all_to_all | solution.py:531
  29.5 3.1 %collective-permute-start = (bf16[576,256]{1,0:T(8,128)(2,1)S(1)}, bf16[576,256]{1,0:T(8,128)(2,1)S(1)}, u32[]{:S(2)}, u32[]{:S(2)}) collective-permute-start(bf16[576,256]{1,0:T(8,128)(2,1)S(1)} %get-tuple-element.18.msg), channel_id=1, source_target_pairs={{0,32},{32,0},{64,96},{96,64},{128,160},{160,128},{192,224},{224,1... | collective-permute-start | bytes 884744 | tf_op jit(solution)/shard_map/ppermute | solution.py:491
  32.6 6.1 %collective-permute-start.3 = (bf16[128,256]{1,0:T(8,128)(2,1)S(1)}, bf16[128,256]{1,0:T(8,128)(2,1)S(1)}, u32[]{:S(2)}, u32[]{:S(2)}) collective-permute-start(bf16[128,256]{1,0:T(8,128)(2,1)S(1)} %get-tuple-element.21), channel_id=1, source_target_pairs={{0,128},{32,160},{64,192},{96,224},{128,256},{160,288},{192,320},{... | collective-permute-start | bytes 196616 | tf_op jit(solution)/shard_map/ppermute | solution.py:494
  38.7 0.7 collective-permute-start.5
  39.3 3.1 %collective-permute-start.2 = (bf16[128,128]{1,0:T(8,128)(2,1)S(1)}, bf16[128,128]{1,0:T(8,128)(2,1)S(1)}, u32[]{:S(2)}, u32[]{:S(2)}) collective-permute-start(bf16[128,128]{1,0:T(8,128)(2,1)S(1)} %get-tuple-element.20), channel_id=1, source_target_pairs={{0,96},{32,64},{64,32},{96,0},{128,224},{160,192},{192,160},{224,1... | collective-permute-start | bytes 98312 | tf_op jit(solution)/shard_map/ppermute | solution.py:491
  42.4 3.1 %collective-permute-start.1 = (bf16[512,128]{1,0:T(8,128)(2,1)S(1)}, bf16[512,128]{1,0:T(8,128)(2,1)S(1)}, u32[]{:S(2)}, u32[]{:S(2)}) collective-permute-start(bf16[512,128]{1,0:T(8,128)(2,1)S(1)} %get-tuple-element.17.qm), channel_id=1, source_target_pairs={{0,64},{32,96},{64,0},{96,32},{128,192},{160,224},{192,128},{224,1... | collective-permute-start | bytes 393224 | tf_op jit(solution)/shard_map/ppermute | solution.py:491
  45.5 7.5 %collective-permute-done.3.col1 = bf16[128,256]{1,0:T(8,128)(2,1)S(1)} collective-permute-done((bf16[128,256]{1,0:T(8,128)(2,1)S(1)}, bf16[128,256]{1,0:T(8,128)(2,1)S(1)}, u32[]{:S(2)}, u32[]{:S(2)}) %collective-permute-start.3) | collective-permute-done | bytes 65568 | tf_op jit(solution)/shard_map/ppermute | solution.py:494
  53.1 8.0 %collective-permute-start.4 = (bf16[128,256]{1,0:T(8,128)(2,1)S(1)}, bf16[128,256]{1,0:T(8,128)(2,1)S(1)}, u32[]{:S(2)}, u32[]{:S(2)}) collective-permute-start(bf16[128,256]{1,0:T(8,128)(2,1)S(1)} %collective-permute-done.3.col1), channel_id=1, source_target_pairs={{128,256},{160,288},{192,320},{224,352},{256,384},{288,416},{320,4... | collective-permute-start | bytes 196616 | tf_op jit(solution)/shard_map/ppermute | solution.py:494
  61.1 6.4 %shard_map.78 = (bf16[2048,128]{1,0:T(8,128)(2,1)}, f32[512,128]{1,0:T(8,128)}, f32[512,128]{1,0:T(8,128)}) custom-call(bf16[3,2048,128]{2,1,0:T(8,128)(2,1)S(1)} %get-tuple-element.16.raw, bf16[512,128]{1,0:T(8,128)(2,1)S(1)} %get-tuple-element.17.qm, bf16[576,256]{1,0:T(8,128)(2,1)S(1)} %get-tuple-element.18.msg), custom_call_target="tpu_custom_call" | custom-call | flops 2000000000 | bytes 3000000 | tf_op jit(solution)/shard_map/pallas_call | solution.py:47
  67.6 0.0 collective-permute-done.4.col2
  67.6 0.0 collective-permute-done.1.got2
  67.6 0.0 copy-start.1
  67.6 4.2 %shard_map.79 = (f32[512,128]{1,0:T(8,128)}, f32[512,128]{1,0:T(8,128)}, bf16[144,128]{1,0:T(8,128)(2,1)S(1)}, bf16[544,128]{1,0:T(8,128)(2,1)S(1)}, bf16[144,128]{1,0:T(8,128)(2,1)S(1)}) custom-call(bf16[512,128]{1,0:T(8,128)(2,1)S(1)} %get-tuple-element.17.qm, bf16[576,256]{1,0:T(8,128)(2,1)S(1)} %get-tuple-element.18.msg, ...), custom_call_target="tpu_custom_call" | custom-call | flops 1000000000 | bytes 4000000 | tf_op jit(solution)/shard_map/pallas_call | solution.py:47
  71.8 7.7 %collective-permute-start.7 = (bf16[544,128]{1,0:T(8,128)(2,1)S(1)}, bf16[544,128]{1,0:T(8,128)(2,1)S(1)}, u32[]{:S(2)}, u32[]{:S(2)}) collective-permute-start(bf16[544,128]{1,0:T(8,128)(2,1)S(1)} %get-tuple-element.27), channel_id=1, source_target_pairs={{0,64},{32,96},{64,0},{96,32},{128,192},{160,224},{192,128},{224,1... | collective-permute-start | bytes 417800 | tf_op jit(solution)/shard_map/ppermute | solution.py:491
  79.5 1.9 %collective-permute-start.6 = (bf16[144,128]{1,0:T(8,128)(2,1)S(1)}, bf16[144,128]{1,0:T(8,128)(2,1)S(1)}, u32[]{:S(2)}, u32[]{:S(2)}) collective-permute-start(bf16[144,128]{1,0:T(8,128)(2,1)S(1)} %get-tuple-element.26), channel_id=1, source_target_pairs={{0,32},{32,0},{64,96},{96,64},{128,160},{160,128},{192,224},{224,1... | collective-permute-start | bytes 110600 | tf_op jit(solution)/shard_map/ppermute | solution.py:491
  81.4 3.1 %collective-permute-start.8 = (bf16[144,128]{1,0:T(8,128)(2,1)S(1)}, bf16[144,128]{1,0:T(8,128)(2,1)S(1)}, u32[]{:S(2)}, u32[]{:S(2)}) collective-permute-start(bf16[144,128]{1,0:T(8,128)(2,1)S(1)} %get-tuple-element.28), channel_id=1, source_target_pairs={{0,96},{32,64},{64,32},{96,0},{128,224},{160,192},{192,160},{224,1... | collective-permute-start | bytes 110600 | tf_op jit(solution)/shard_map/ppermute | solution.py:491
  84.6 1.8 %shard_map.82 = bf16[32,2,128]{2,1,0:T(2,128)(2,1)} custom-call(s32[32]{0:T(128)S(1)} %copy-done.2, bf16[16,72,128]{2,1,0:T(8,128)(2,1)S(1)} %all-to-all-done.1.got, bf16[1024,256]{1,0:T(8,128)(2,1)S(1)} %copy-done.1), custom_call_target="tpu_custom_call" | custom-call | flops 10000000 | bytes 1000000 | tf_op jit(solution)/shard_map/pallas_call | solution.py:47
  86.3 8.1 %all-to-all-start.2 = ((bf16[32,2,128]{2,1,0:T(2,128)(2,1)}), bf16[32,2,128]{2,1,0:T(2,128)(2,1)S(1)}, u32[]{:S(2)}, u32[]{:S(2)}) async-start(bf16[32,2,128]{2,1,0:T(2,128)(2,1)} %shard_map.82), calls=%async_computation.2 | async-start | bytes 32768 | tf_op jit(solution)/shard_map/all_to_all | solution.py:555
  94.4 3.2 %shard_map.80 = bf16[2048,128]{1,0:T(8,128)(2,1)} custom-call(bf16[2048,128]{1,0:T(8,128)(2,1)} %get-tuple-element.19.near_h, f32[512,128]{1,0:T(8,128)} %get-tuple-element.24.acc_h, f32[512,128]{1,0:T(8,128)} %get-tuple-element.25.ml_h, bf16[144,128]{1,0:T(8,128)(2,1)S(1)} %collective-permute-done.6.back1, ...), custom_call_target="tpu_custom_call" | custom-call | flops 100000000 | bytes 4000000 | tf_op jit(solution)/shard_map/pallas_call | solution.py:47
  97.6 3.7 %all-to-all-done.2.got = bf16[32,2,128]{2,1,0:T(2,128)(2,1)S(1)} async-done(((bf16[32,2,128]{2,1,0:T(2,128)(2,1)}), bf16[32,2,128]{2,1,0:T(2,128)(2,1)S(1)}, u32[]{:S(2)}, u32[]{:S(2)}) %all-to-all-start.2) | async-done | bytes 16416 | tf_op jit(solution)/shard_map/all_to_all | solution.py:555
  101.4 2.3 %shard_map.83 = bf16[16,2,64]{2,1,0:T(2,128)(2,1)} custom-call(s32[32]{0:T(128)S(1)} %copy-done.2, bf16[32,2,128]{2,1,0:T(2,128)(2,1)S(1)} %all-to-all-done.2.got), custom_call_target="tpu_custom_call" | custom-call | bytes 100000 | tf_op jit(solution)/shard_map/pallas_call | solution.py:47
  (14 shorter events, 0.0 us)
Async XLA Ops:
  0.6 13.0 %copy-start.2 = (s32[32]{0:T(128)S(1)}, s32[32]{0:T(128)}, u32[]{:S(2)}) copy-start(s32[32]{0:T(128)} %own.5) | copy-start | bytes 388
  0.6 13.0 %copy-start.3 = (s32[32]{0:T(128)S(1)}, s32[32]{0:T(128)}, u32[]{:S(2)}) copy-start(s32[32]{0:T(128)} %lens.1) | copy-start | bytes 388
  0.7 13.0 %copy-start = (bf16[4,2,64,1024]{3,2,1,0:T(8,128)(2,1)S(1)}, bf16[4,2,64,1024]{3,2,1,0:T(8,128)(2,1)}, u32[]{:S(2)}) copy-start(bf16[4,2,64,1024]{3,2,1,0:T(8,128)(2,1)} %cache.1) | copy-start | bytes 3145732
  16.2 68.4 %all-to-all-start.1 = ((bf16[16,72,128]{2,1,0:T(8,128)(2,1)}), bf16[16,72,128]{2,1,0:T(8,128)(2,1)S(1)}, u32[]{:S(2)}, u32[]{:S(2)}) async-start(bf16[16,72,128]{2,1,0:T(8,128)(2,1)} %shard_map.81), calls=%async_computation.1 | async-start | bytes 589824 | tf_op jit(solution)/shard_map/all_to_all | solution.py:531
  29.5 38.1 %collective-permute-start = (bf16[576,256]{1,0:T(8,128)(2,1)S(1)}, bf16[576,256]{1,0:T(8,128)(2,1)S(1)}, u32[]{:S(2)}, u32[]{:S(2)}) collective-permute-start(bf16[576,256]{1,0:T(8,128)(2,1)S(1)} %get-tuple-element.18.msg), channel_id=1, source_target_pairs={{0,32},{32,0},{64,96},{96,64},{128,160},{160,128},{192,224},{224,1... | collective-permute-start | bytes 884744 | tf_op jit(solution)/shard_map/ppermute | solution.py:491
  32.6 20.5 %collective-permute-start.3 = (bf16[128,256]{1,0:T(8,128)(2,1)S(1)}, bf16[128,256]{1,0:T(8,128)(2,1)S(1)}, u32[]{:S(2)}, u32[]{:S(2)}) collective-permute-start(bf16[128,256]{1,0:T(8,128)(2,1)S(1)} %get-tuple-element.21), channel_id=1, source_target_pairs={{0,128},{32,160},{64,192},{96,224},{128,256},{160,288},{192,320},{... | collective-permute-start | bytes 196616 | tf_op jit(solution)/shard_map/ppermute | solution.py:494
  38.7 28.9 %collective-permute-start.5 = (bf16[128,256]{1,0:T(8,128)(2,1)S(1)}, bf16[128,256]{1,0:T(8,128)(2,1)S(1)}, u32[]{:S(2)}, u32[]{:S(2)}) collective-permute-start(bf16[128,256]{1,0:T(8,128)(2,1)S(1)} %get-tuple-element.21), channel_id=1, source_target_pairs={{0,384},{32,416},{64,448},{96,480},{1,385},{33,417},{65,449},{97,4... | collective-permute-start | bytes 196616 | tf_op jit(solution)/shard_map/ppermute | solution.py:494
  39.3 28.2 %collective-permute-start.2 = (bf16[128,128]{1,0:T(8,128)(2,1)S(1)}, bf16[128,128]{1,0:T(8,128)(2,1)S(1)}, u32[]{:S(2)}, u32[]{:S(2)}) collective-permute-start(bf16[128,128]{1,0:T(8,128)(2,1)S(1)} %get-tuple-element.20), channel_id=1, source_target_pairs={{0,96},{32,64},{64,32},{96,0},{128,224},{160,192},{192,160},{224,1... | collective-permute-start | bytes 98312 | tf_op jit(solution)/shard_map/ppermute | solution.py:491
  42.4 25.2 %collective-permute-start.1 = (bf16[512,128]{1,0:T(8,128)(2,1)S(1)}, bf16[512,128]{1,0:T(8,128)(2,1)S(1)}, u32[]{:S(2)}, u32[]{:S(2)}) collective-permute-start(bf16[512,128]{1,0:T(8,128)(2,1)S(1)} %get-tuple-element.17.qm), channel_id=1, source_target_pairs={{0,64},{32,96},{64,0},{96,32},{128,192},{160,224},{192,128},{224,1... | collective-permute-start | bytes 393224 | tf_op jit(solution)/shard_map/ppermute | solution.py:491
  53.1 14.5 %collective-permute-start.4 = (bf16[128,256]{1,0:T(8,128)(2,1)S(1)}, bf16[128,256]{1,0:T(8,128)(2,1)S(1)}, u32[]{:S(2)}, u32[]{:S(2)}) collective-permute-start(bf16[128,256]{1,0:T(8,128)(2,1)S(1)} %collective-permute-done.3.col1), channel_id=1, source_target_pairs={{128,256},{160,288},{192,320},{224,352},{256,384},{288,416},{320,4... | collective-permute-start | bytes 196616 | tf_op jit(solution)/shard_map/ppermute | solution.py:494
  67.6 16.9 %copy-start.1 = (bf16[1024,256]{1,0:T(8,128)(2,1)S(1)}, bf16[1024,256]{1,0:T(8,128)(2,1)}, u32[]{:S(2)}) copy-start(bf16[1024,256]{1,0:T(8,128)(2,1)} %weight.1) | copy-start | bytes 1572868
  71.8 22.6 %collective-permute-start.7 = (bf16[544,128]{1,0:T(8,128)(2,1)S(1)}, bf16[544,128]{1,0:T(8,128)(2,1)S(1)}, u32[]{:S(2)}, u32[]{:S(2)}) collective-permute-start(bf16[544,128]{1,0:T(8,128)(2,1)S(1)} %get-tuple-element.27), channel_id=1, source_target_pairs={{0,64},{32,96},{64,0},{96,32},{128,192},{160,224},{192,128},{224,1... | collective-permute-start | bytes 417800 | tf_op jit(solution)/shard_map/ppermute | solution.py:491
  79.5 14.9 %collective-permute-start.6 = (bf16[144,128]{1,0:T(8,128)(2,1)S(1)}, bf16[144,128]{1,0:T(8,128)(2,1)S(1)}, u32[]{:S(2)}, u32[]{:S(2)}) collective-permute-start(bf16[144,128]{1,0:T(8,128)(2,1)S(1)} %get-tuple-element.26), channel_id=1, source_target_pairs={{0,32},{32,0},{64,96},{96,64},{128,160},{160,128},{192,224},{224,1... | collective-permute-start | bytes 110600 | tf_op jit(solution)/shard_map/ppermute | solution.py:491
  81.4 13.0 %collective-permute-start.8 = (bf16[144,128]{1,0:T(8,128)(2,1)S(1)}, bf16[144,128]{1,0:T(8,128)(2,1)S(1)}, u32[]{:S(2)}, u32[]{:S(2)}) collective-permute-start(bf16[144,128]{1,0:T(8,128)(2,1)S(1)} %get-tuple-element.28), channel_id=1, source_target_pairs={{0,96},{32,64},{64,32},{96,0},{128,224},{160,192},{192,160},{224,1... | collective-permute-start | bytes 110600 | tf_op jit(solution)/shard_map/ppermute | solution.py:491
  86.3 15.0 %all-to-all-start.2 = ((bf16[32,2,128]{2,1,0:T(2,128)(2,1)}), bf16[32,2,128]{2,1,0:T(2,128)(2,1)S(1)}, u32[]{:S(2)}, u32[]{:S(2)}) async-start(bf16[32,2,128]{2,1,0:T(2,128)(2,1)} %shard_map.82), calls=%async_computation.2 | async-start | bytes 32768 | tf_op jit(solution)/shard_map/all_to_all | solution.py:555
